TPU v7x, 128 devices: a whole 4x4x4 slice. The times are simulated.
128 devices in a mesh: samp: 16 (over z, y), col: 8 (over x, core).
Axes of the slice: x: 4, y: 4, z: 4, core: 2. Of those that a mesh axis runs over, the one named last changes fastest.
Arguments:
- spectra: float32 [32768, 8192], P('samp', 'col'), as said below
- w_start: float32 [32768, 512], P('samp'), may hold values from 0.05 to 1
- h_start: float32 [8192, 512], P('col'), may hold values from 0.05 to 1
Outputs:
- w_factor: float32 [32768, 512], P('samp')
- h_factor: float32 [8192, 512], P('col')
Inputs may be any that keep to these rules, and one draw needn't show every extreme that they name: `spectra`: every entry is positive.
All inputs are finite; a program needn't handle non-finite values.
Results may differ from a plain program's by a relative error of at most 0.0003.
Values sent between devices are 32-bit elements; how exact they have to be, the bound alone decides.
No kernel may reach another device: no remote copies, remote signals or barrier semaphores. Data moves between devices by JAX's collectives and lax.ppermute only.
A program may use at most 128 MiB of HBM per device.

v0:
```python
import functools
import jax
import jax.numpy as jnp
from jax import lax
from jax.experimental import pallas as pl
from jax.experimental.pallas import tpu as pltpu
from jax.sharding import PartitionSpec as P

BLOCK = 128
SWEEPS = 3
floor_value = 1e-06
REL = (0, 1, 3, 2)
f32, bf16 = jnp.float32, jnp.bfloat16
ANY = pl.BlockSpec(memory_space=pl.ANY)
HBM = pl.BlockSpec(memory_space=pltpu.HBM)
VM = pl.BlockSpec(memory_space=pltpu.VMEM)


def sds(*shape, dtype=f32):
    return jax.ShapeDtypeStruct(shape, dtype)


def cost(flops, nbytes):
    return pl.CostEstimate(flops=flops, bytes_accessed=nbytes, transcendentals=0)


def params(mib):
    return pltpu.CompilerParams(vmem_limit_bytes=mib << 20)


def split(a):
    hi = a.astype(bf16)
    return hi, (a - hi.astype(f32)).astype(bf16)


def dot3(ah, al, bh, bl):
    d = functools.partial(jnp.dot, preferred_element_type=f32)
    return d(ah, bh) + (d(ah, bl) + d(al, bh))


def place():
    s, q = lax.axis_index("samp"), lax.axis_index("col")
    return s // 4, s % 4, q // 2, q % 2


def prod_kernel(chunks, sibling, first, nadd, *refs):
    refs = list(refs)
    x_ref = refs.pop(0)
    if first:
        h_ref = refs.pop(0)
    else:
        hh_ref, hl_ref = refs.pop(0), refs.pop(0)
    adds = [refs.pop(0) for _ in range(nadd)]
    out_ref = refs.pop(0)
    if first:
        hh_ref, hl_ref = refs.pop(0), refs.pop(0)
    xs, sem = refs
    _, _, _, c = place()
    cc = 1 - c if sibling else c
    copies = []
    for i, k in enumerate(chunks):
        row = pl.multiple_of(512 * k + 256 * cc, 256)
        cp = pltpu.make_async_copy(x_ref.at[pl.ds(row, 256), :], xs.at[pl.ds(256 * i, 256), :], sem.at[i])
        cp.start()
        copies.append(cp)
    if first:
        hh, hl = split(h_ref[...])
        hh_ref[...] = hh
        hl_ref[...] = hl
    if nadd:
        n = adds[0].shape[0]
        out_ref[:n, :] = adds[0][...] + adds[1][:n, :]
    else:
        n = 0
    for at in range(0, 256 * len(chunks), 512):
        copies[at // 256].wait()
        copies[at // 256 + 1].wait()
        ah, al = split(xs[at : at + 512, :])
        out = dot3(ah, al, hh_ref[...], hl_ref[...])
        if nadd:
            out = out + adds[1][n + at : n + at + 512, :]
        out_ref[n + at : n + at + 512, :] = out


def prod(spectra, h, chunks, sibling, adds=()):
    first = not isinstance(h, tuple)
    n = 256 * len(chunks)
    ins = [spectra] + ([h] if first else list(h)) + list(adds)
    outs = [sds(n + (adds[0].shape[0] if adds else 0), 512)]
    if first:
        outs += [sds(1024, 512, dtype=bf16)] * 2
    out = pl.pallas_call(
        functools.partial(prod_kernel, chunks, sibling, first, len(adds)),
        out_shape=outs,
        in_specs=[HBM] + [VM] * (len(ins) - 1),
        out_specs=[VM] * len(outs),
        scratch_shapes=[pltpu.VMEM((n, 1024), f32), pltpu.SemaphoreType.DMA((len(chunks),))],
        compiler_params=params(50),
        cost_estimate=cost(6 * n * 1024 * 512, n * 6144 + (2 << 20)),
        name="prod",
    )(*ins)
    return out if first else out[0]


def flip_kernel(x_ref, th_ref, tl_ref):
    for k in range(0, 1024, 128):
        hi, lo = split(x_ref[:, k : k + 128].T)
        th_ref[0, k : k + 128, :] = hi
        tl_ref[0, k : k + 128, :] = lo


def flip(spectra):
    spec = pl.BlockSpec((1, 1024, 128), lambda i: (i, 0, 0))
    return pl.pallas_call(
        flip_kernel,
        grid=(16,),
        out_shape=[sds(16, 1024, 128, dtype=bf16)] * 2,
        in_specs=[pl.BlockSpec((128, 1024), lambda i: (i, 0))],
        out_specs=[spec, spec],
        compiler_params=params(6),
        cost_estimate=cost(1 << 24, 16 << 20),
        name="flip",
    )(spectra)


def back_kernel(chunks, later, *refs):
    refs = list(refs)
    th_ref, tl_ref = refs.pop(0), refs.pop(0)
    ws = [refs.pop(0) for _ in chunks]
    acc_ref = refs.pop(0) if later else None
    if later:
        refs.pop(0)
    out_ref, w_out, sem = refs
    z, y, x, c = place()
    at, copies = [], []
    for k, (r, sibling) in enumerate(chunks):
        first = 2 * (2 * ((x + r) % 4) + (1 - c if sibling else c))
        at += [first, first + 1]
        cp = pltpu.make_async_copy(ws[k], w_out.at[pl.ds(pl.multiple_of(128 * first, 256), 256), :], sem.at[k])
        cp.start()
        copies.append(cp)
    wh, wl = split(jnp.concatenate([w[...] for w in ws], axis=0))
    for k in range(0, 1024, 512):
        rows = slice(k, k + 512)
        ah = jnp.concatenate([th_ref[i, rows, :] for i in at], axis=1)
        al = jnp.concatenate([tl_ref[i, rows, :] for i in at], axis=1)
        out = dot3(ah, al, wh, wl)
        if later:
            out = out + acc_ref[rows, :]
        out_ref[rows, :] = out
    for cp in copies:
        cp.wait()


def back(flipped, ws, chunks, carry=()):
    ins = list(flipped) + list(ws) + list(carry)
    n = len(ins)
    return pl.pallas_call(
        functools.partial(back_kernel, tuple(chunks), bool(carry)),
        out_shape=[sds(1024, 512), sds(2048, 512)],
        in_specs=[VM] * (2 + len(ws)) + ([VM, HBM] if carry else []),
        out_specs=[VM, HBM],
        scratch_shapes=[pltpu.SemaphoreType.DMA((len(ws),))],
        input_output_aliases={n - 1: 1} if carry else {},
        compiler_params=params(12),
        cost_estimate=cost(6 * 1024 * 512 * 256 * len(chunks), 6 << 20),
        name="back",
    )(*ins)


def gram_h_kernel(h_ref, mine_ref, theirs_ref, tmp):
    z, y, _, c = place()
    h = h_ref[...]
    tmp[...] = h.T
    left = tmp[pl.ds(pl.multiple_of(32 * (4 * z + y), 32), 32), :]
    both = dot3(*split(left), *split(h))
    first = (c == 0).astype(f32)
    mine_ref[...] = both[:16] * first + both[16:] * (1.0 - first)
    theirs_ref[...] = both[16:] * first + both[:16] * (1.0 - first)


def gram_h(h):
    return pl.pallas_call(
        gram_h_kernel,
        out_shape=[sds(16, 512)] * 2,
        in_specs=[VM],
        out_specs=[VM] * 2,
        scratch_shapes=[pltpu.VMEM((512, 1024), f32)],
        compiler_params=params(12),
        cost_estimate=cost(6 * 512 * 32 * 1024, 4 << 20),
        name="gram_h",
    )(h)


def gram_w_kernel(w_ref, mine_ref, theirs_ref, tmp):
    z, y, _, c = place()
    w = w_ref[...]
    tmp[...] = dot3(*split(w.T), *split(w))
    for k in range(4):
        for m in range(4):
            s = 4 * ((z + REL[k]) % 4) + (y + REL[m]) % 4
            at = 64 * k + 16 * m
            mine_ref[at : at + 16, :] = tmp[pl.ds(pl.multiple_of(32 * s + 16 * c, 16), 16), :]
            theirs_ref[at : at + 16, :] = tmp[pl.ds(pl.multiple_of(32 * s + 16 * (1 - c), 16), 16), :]


def gram_w(w):
    return pl.pallas_call(
        gram_w_kernel,
        out_shape=[sds(256, 512)] * 2,
        in_specs=[VM],
        out_specs=[VM] * 2,
        scratch_shapes=[pltpu.VMEM((512, 512), f32)],
        compiler_params=params(10),
        cost_estimate=cost(6 * 512 * 512 * 256, 4 << 20),
        name="gram_w",
    )(w)


def sweep_kernel(axis, product, start, mine, theirs, *refs):
    outs, (g, gh, gl, fh, fl, ff, pp, sem) = refs[:-8], refs[-8:]
    z, y, x, c = place()
    n = ff.shape[0]
    first = n * (2 * x + c if axis == "col" else 4 * z + y)
    begin = pltpu.make_async_copy(start.at[pl.ds(pl.multiple_of(first, n), n), :], ff, sem)
    begin.start()
    for t, piece in enumerate((mine, theirs)):
        cc = c if t == 0 else 1 - c
        for j in range(4):
            for i in range(4):
                row = 32 * (4 * ((z + REL[i]) % 4) + (y + REL[j]) % 4) + 16 * cc
                g[pl.ds(pl.multiple_of(row, 16), 16), :] = piece[64 * j + 16 * i : 64 * j + 16 * i + 16, :]
    hi, lo = split(g[...])
    gh[...] = hi
    gl[...] = lo
    inv = []
    for b in range(0, 512, BLOCK):
        inv.append(1.0 / jnp.sum(g[b : b + BLOCK, b : b + BLOCK], axis=0, keepdims=True))
    total = product[:n, :]
    for k in range(n, product.shape[0], n):
        total = total + product[k : k + n, :]
    pp[...] = total
    begin.wait()
    hi, lo = split(ff[...])
    fh[...] = hi
    fl[...] = lo
    for _ in range(SWEEPS):
        for k, b in enumerate(range(0, 512, BLOCK)):
            cols = slice(b, b + BLOCK)
            fg = dot3(fh[...], fl[...], gh[:, cols], gl[:, cols])
            new = jnp.maximum(ff[:, cols] + (pp[:, cols] - fg) * inv[k], floor_value)
            ff[:, cols] = new
            hi, lo = split(new)
            fh[:, cols] = hi
            fl[:, cols] = lo
    n = n // len(outs)
    for k, out in enumerate(outs):
        out[...] = ff[n * k : n * (k + 1), :]


def sweep(product, start, axis, rows, pieces, nout):
    return pl.pallas_call(
        functools.partial(sweep_kernel, axis),
        out_shape=[sds(rows // nout, 512)] * nout,
        in_specs=[VM, HBM, VM, VM],
        out_specs=[VM] * nout,
        scratch_shapes=[
            pltpu.VMEM((512, 512), f32),
            pltpu.VMEM((512, 512), bf16),
            pltpu.VMEM((512, 512), bf16),
            pltpu.VMEM((rows, 512), bf16),
            pltpu.VMEM((rows, 512), bf16),
            pltpu.VMEM((rows, 512), f32),
            pltpu.VMEM((rows, 512), f32),
            pltpu.SemaphoreType.DMA,
        ],
        compiler_params=params(12),
        cost_estimate=cost(72 * rows * 512 * 512, 4 << 20),
        name="sweep",
    )(product, start, *pieces)


def lay_h_kernel(*refs):
    ins, out = refs[:8], refs[8]
    z, y, _, _ = place()
    for half in range(2):
        for j in range(4):
            for i in range(4):
                dz, dy = (REL[i], REL[j]) if half == 0 else (REL[j], REL[i])
                row = pl.multiple_of(64 * (4 * ((z + dz) % 4) + (y + dy) % 4) + 32 * half, 32)
                out[pl.ds(row, 32), :] = ins[4 * half + j][32 * i : 32 * (i + 1), :]


def lay_h(pieces):
    return pl.pallas_call(
        lay_h_kernel,
        out_shape=sds(1024, 512),
        in_specs=[VM] * 8,
        out_specs=VM,
        compiler_params=params(6),
        cost_estimate=cost(0, 4 << 20),
        name="lay_h",
    )(*pieces)


def moves(axis, dim):
    out = {}
    for r in range(4):
        pairs = []
        if axis == "col":
            for i in range(8):
                x, c = i // 2, i % 2
                pairs.append((i, 2 * x + 1 - c) if dim == "core" else (i, 2 * ((x + r) % 4) + c))
        else:
            for i in range(16):
                z, y = i // 4, i % 4
                pairs.append((i, 4 * ((z + r) % 4) + y) if dim == "z" else (i, 4 * z + (y + r) % 4))
        out[r] = pairs
    return out


XGROUPS = [[0, 2, 4, 6], [1, 3, 5, 7]]
CORE, X = moves("col", "core"), moves("col", "x")
Y, Z = moves("samp", "y"), moves("samp", "z")


def swap(a):
    return lax.ppermute(a, "col", CORE[0])


def send(a, axis, table, r):
    return lax.ppermute(a, axis, table[r])


def fetch(a, axis, table):
    return [lax.ppermute(a, axis, table[(4 - r) % 4]) for r in REL[1:]]


def after(a, *others):
    return lax.optimization_barrier((a,) + others)[0]


def join_kernel(nout, *refs):
    ins, outs = refs[:-nout], refs[-nout:]
    n = len(ins) // nout
    for k, out in enumerate(outs):
        rows = ins[n * k].shape[0]
        for i in range(n):
            out[rows * i : rows * (i + 1), :] = ins[n * k + i][...]


def join(parts, nout=1):
    rows = parts[0].shape[0] * len(parts) // nout
    out = pl.pallas_call(
        functools.partial(join_kernel, nout),
        out_shape=[sds(rows, 512)] * nout,
        in_specs=[VM] * len(parts),
        out_specs=[VM] * nout,
        compiler_params=params(4),
        cost_estimate=cost(0, rows * nout * 4096),
        name="join",
    )(*parts)
    return out if nout > 1 else out[0]


def add_kernel(n, *refs):
    total = refs[0][...]
    for r in refs[1:n]:
        total = total + r[...]
    outs = refs[n:]
    rows = total.shape[0] // len(outs)
    for k, out in enumerate(outs):
        out[...] = total[rows * k : rows * (k + 1)]


def add(parts, nout=1):
    rows = parts[0].shape[0]
    out = pl.pallas_call(
        functools.partial(add_kernel, len(parts)),
        out_shape=[sds(rows // nout, 512)] * nout,
        in_specs=[VM] * len(parts),
        out_specs=[VM] * nout,
        compiler_params=params(4),
        cost_estimate=cost(rows * 512 * len(parts), rows * 4096 * len(parts)),
        name="add",
    )(*parts)
    return out if nout > 1 else out[0]


def deal(pieces, axis, table):
    return [pieces[0]] + [send(pieces[k], axis, table, REL[k]) for k in (1, 2, 3)]


def over_all(strip):
    strip = add([strip] + fetch(strip, "col", X))
    strip = join([strip] + fetch(strip, "samp", Z))
    strip = join([strip] + fetch(strip, "samp", Y))
    return strip, swap(strip)


def shards(spectra, w_start, h_start):
    a, hh, hl = prod(spectra, h_start, (0, 1, 2, 3), True)
    recv = swap(a)
    g_mine, g_theirs = gram_h(after(h_start, a))
    g_theirs = swap(g_theirs)
    h = (after(hh, g_mine), hl)
    low = prod(spectra, h, (0, 1), False)
    both = prod(spectra, h, (2, 3), False, (low, recv))
    product = lax.psum_scatter(both, "col", scatter_dimension=0, axis_index_groups=XGROUPS, tiled=True)

    pieces_h = over_all(add([after(g_mine, both), g_theirs]))

    (w,) = sweep(product, w_start, "col", 256, pieces_h, 1)

    ws = swap(w)
    near_p, near_m, far = fetch(w, "col", X)

    g_mine, g_theirs = gram_w(w)
    flipped = flip(after(spectra, g_theirs))
    strips = add([g_mine, after(swap(g_theirs), *flipped)], 4)
    strips = deal(strips, "samp", Z)
    carry = back(flipped, (w, ws), ((0, False), (0, True)))
    strips = add([after(strips[0], carry[0])] + strips[1:], 4)
    strips = deal(strips, "samp", Y)
    sib_p, sib_m = swap(after(near_p, *strips)), swap(near_m)
    carry = back(flipped, (near_p, near_m), ((1, False), (3, False)), carry)
    strip = add([after(strips[0], carry[0])] + strips[1:])
    carry = back(flipped, (sib_p, sib_m), ((1, True), (3, True)), carry)
    sib_f = swap(far)
    back_sum, w_out = back(flipped, (far, sib_f), ((2, False), (2, True)), carry)

    product = lax.all_to_all(back_sum, "samp", 0, 0, tiled=True)
    pieces_w = over_all(after(strip, back_sum))
    ha, hb = sweep(product, h_start, "samp", 64, pieces_w, 2)

    row_a, row_b = join([ha] + fetch(ha, "samp", Z) + [hb] + fetch(hb, "samp", Y), 2)
    h_out = lay_h([row_a] + fetch(row_a, "samp", Y) + [row_b] + fetch(row_b, "samp", Z))
    return (w_out, h_out)


def solution(mesh):
    return jax.shard_map(
        shards,
        mesh=mesh,
        in_specs=(P("samp", "col"), P("samp", None), P("col", None)),
        out_specs=(P("samp", None), P("col", None)),
        check_vma=False,
    )
```

profile of v0, /device:TPU:24, one launch (start us, length us, event | category | flops | bytes accessed | tf_op | source)
XLA Modules:
  0.0 200.7 jit_solution(9778833663853205054)
XLA Ops:
  7.2 8.2 %prod.3 = (f32[1024,512]{1,0:T(8,128)}, bf16[1024,512]{1,0:T(8,128)(2,1)S(1)}, bf16[1024,512]{1,0:T(8,128)(2,1)S(1)}) custom-call(f32[2048,1024]{1,0:T(8,128)} %x_ref, f32[1024,512]{1,0:T(8,128)} %start.3), custom_call_target="tpu_custom_call" | custom-call | flops 3221225472 | bytes 8388608 | tf_op jit(solution)/shard_map/prod/pallas_call | solution.py:92
  16.8 3.4 %prod.4.refs_3_ = f32[512,512]{1,0:T(8,128)S(1)} custom-call(f32[2048,1024]{1,0:T(8,128)} %x_ref, bf16[1024,512]{1,0:T(8,128)(2,1)S(1)} %get-tuple-element.44.refs_1_, bf16[1024,512]{1,0:T(8,128)(2,1)S(1)} %get-tuple-element.45.refs_2_), custom_call_target="tpu_custom_call" | custom-call | flops 1610612736 | bytes 5242880 | tf_op jit(solution)/shard_map/prod/pallas_call | solution.py:92
  21.5 6.3 %prod.5 = f32[1024,512]{1,0:T(8,128)} custom-call(f32[2048,1024]{1,0:T(8,128)} %x_ref, bf16[1024,512]{1,0:T(8,128)(2,1)S(1)} %get-tuple-element.44.refs_1_, bf16[1024,512]{1,0:T(8,128)(2,1)S(1)} %get-tuple-element.45.refs_2_, f32[512,512]{1,0:T(8,128)S(1)} %prod.4.refs_3_, f32[1024,512]{1,0:T(8,128)} %copy-done.5), custom_call_target="tpu_custom_call" | custom-call | flops 1610612736 | bytes 5242880 | tf_op jit(solution)/shard_map/prod/pallas_call | solution.py:92
  29.3 2.8 %collective-permute-start.2 = (f32[16,512]{1,0:T(8,128)S(1)}, f32[16,512]{1,0:T(8,128)S(1)}, u32[]{:S(2)}, u32[]{:S(2)}) collective-permute-start(f32[16,512]{1,0:T(8,128)S(1)} %add.9.refs_0_), channel_id=1, source_target_pairs={{0,6},{1,7},{2,0},{3,1},{4,2},{5,3},{6,4},{7,5},{8,14},{9,15},{10,... | collective-permute-start | bytes 98312 | tf_op jit(solution)/shard_map/ppermute | solution.py:336
  34.3 3.2 %collective-permute-done.3.refs_2_ = f32[16,512]{1,0:T(8,128)S(1)} collective-permute-done((f32[16,512]{1,0:T(8,128)S(1)}, f32[16,512]{1,0:T(8,128)S(1)}, u32[]{:S(2)}, u32[]{:S(2)}) %collective-permute-start.3) | collective-permute-done | bytes 32800 | tf_op jit(solution)/shard_map/ppermute | solution.py:336
  37.5 4.1 %collective-permute-start.5 = (f32[16,512]{1,0:T(8,128)S(1)}, f32[16,512]{1,0:T(8,128)S(1)}, u32[]{:S(2)}, u32[]{:S(2)}) collective-permute-start(f32[16,512]{1,0:T(8,128)S(1)} %add.10.refs_0_), channel_id=1, source_target_pairs={{0,96},{8,104},{16,112},{24,120},{32,0},{40,8},{48,16},{56,24},{64... | collective-permute-start | bytes 98312 | tf_op jit(solution)/shard_map/ppermute | solution.py:336
  43.5 3.3 %collective-permute-done.6.refs_2_ = f32[16,512]{1,0:T(8,128)S(1)} collective-permute-done((f32[16,512]{1,0:T(8,128)S(1)}, f32[16,512]{1,0:T(8,128)S(1)}, u32[]{:S(2)}, u32[]{:S(2)}) %collective-permute-start.6) | collective-permute-done | bytes 32800 | tf_op jit(solution)/shard_map/ppermute | solution.py:336
  48.4 3.2 %collective-permute-start.9 = (f32[64,512]{1,0:T(8,128)S(1)}, f32[64,512]{1,0:T(8,128)S(1)}, u32[]{:S(2)}, u32[]{:S(2)}) collective-permute-start(f32[64,512]{1,0:T(8,128)S(1)} %join.5.refs_0_), channel_id=1, source_target_pairs={{0,8},{8,16},{16,24},{24,0},{32,40},{40,48},{48,56},{56,32},{64,72... | collective-permute-start | bytes 393224 | tf_op jit(solution)/shard_map/ppermute | solution.py:336
  63.1 4.0 %sweep.2.w_ref.refs_2_ = f32[256,512]{1,0:T(8,128)S(1)} custom-call(f32[256,512]{1,0:T(8,128)S(1)} %copy-done.4, f32[2048,512]{1,0:T(8,128)S(1)} %copy-done.3, f32[256,512]{1,0:T(8,128)S(1)} %join.6.mine, f32[256,512]{1,0:T(8,128)S(1)} %collective-permute-done.11.theirs), custom_call_target="tpu_custom_call" | custom-call | flops 4831838208 | bytes 4194304 | tf_op jit(solution)/shard_map/sweep/pallas_call | solution.py:262
  71.9 3.4 %copy-done = f32[2048,1024]{1,0:T(8,128)S(1)} copy-done((f32[2048,1024]{1,0:T(8,128)S(1)}, f32[2048,1024]{1,0:T(8,128)}, u32[]{:S(2)}) %copy-start) | copy-done | bytes 8388632
  75.3 3.3 %flip.1 = (bf16[16,1024,128]{2,1,0:T(8,128)(2,1)S(1)}, bf16[16,1024,128]{2,1,0:T(8,128)(2,1)S(1)}) custom-call(f32[2048,1024]{1,0:T(8,128)S(1)} %copy-done), custom_call_target="tpu_custom_call" | custom-call | flops 16777216 | bytes 16777216 | tf_op jit(solution)/shard_map/flip/pallas_call | solution.py:114
  82.0 2.9 %collective-permute-done.17.refs_1_ = f32[64,512]{1,0:T(8,128)S(1)} collective-permute-done((f32[64,512]{1,0:T(8,128)S(1)}, f32[64,512]{1,0:T(8,128)S(1)}, u32[]{:S(2)}, u32[]{:S(2)}) %collective-permute-start.17) | collective-permute-done | bytes 131104 | tf_op jit(solution)/shard_map/ppermute | solution.py:332
  95.6 2.6 %collective-permute-done.21.refs_2_ = f32[16,512]{1,0:T(8,128)S(1)} collective-permute-done((f32[16,512]{1,0:T(8,128)S(1)}, f32[16,512]{1,0:T(8,128)S(1)}, u32[]{:S(2)}, u32[]{:S(2)}) %collective-permute-start.21) | collective-permute-done | bytes 32800 | tf_op jit(solution)/shard_map/ppermute | solution.py:332
  108.0 7.0 %all-to-all-start = ((f32[16,64,512]{2,1,0:T(8,128)}), f32[16,64,512]{2,1,0:T(8,128)}, u32[]{:S(2)}, u32[]{:S(2)}) async-start(f32[16,64,512]{2,1,0:T(8,128)} %bitcast.2), calls=%async_computation.1 | async-start | bytes 4194304 | tf_op jit(solution)/shard_map/all_to_all | solution.py:432
  119.5 2.8 %collective-permute-done.27.refs_2_ = f32[16,512]{1,0:T(8,128)S(1)} collective-permute-done((f32[16,512]{1,0:T(8,128)S(1)}, f32[16,512]{1,0:T(8,128)S(1)}, u32[]{:S(2)}, u32[]{:S(2)}) %collective-permute-start.27) | collective-permute-done | bytes 32800 | tf_op jit(solution)/shard_map/ppermute | solution.py:336
  122.9 2.8 %collective-permute-start.29 = (f32[16,512]{1,0:T(8,128)S(1)}, f32[16,512]{1,0:T(8,128)S(1)}, u32[]{:S(2)}, u32[]{:S(2)}) collective-permute-start(f32[16,512]{1,0:T(8,128)S(1)} %add.14.refs_0_), channel_id=1, source_target_pairs={{0,96},{8,104},{16,112},{24,120},{32,0},{40,8},{48,16},{56,24},{64... | collective-permute-start | bytes 98312 | tf_op jit(solution)/shard_map/ppermute | solution.py:336
  129.4 12.8 %collective-permute-done.30.refs_2_ = f32[16,512]{1,0:T(8,128)S(1)} collective-permute-done((f32[16,512]{1,0:T(8,128)S(1)}, f32[16,512]{1,0:T(8,128)S(1)}, u32[]{:S(2)}, u32[]{:S(2)}) %collective-permute-start.30) | collective-permute-done | bytes 32800 | tf_op jit(solution)/shard_map/ppermute | solution.py:336
  143.5 2.6 %collective-permute-start.33 = (f32[64,512]{1,0:T(8,128)S(1)}, f32[64,512]{1,0:T(8,128)S(1)}, u32[]{:S(2)}, u32[]{:S(2)}) collective-permute-start(f32[64,512]{1,0:T(8,128)S(1)} %join.7.refs_0_), channel_id=1, source_target_pairs={{0,8},{8,16},{16,24},{24,0},{32,40},{40,48},{48,56},{56,32},{64,72... | collective-permute-start | bytes 393224 | tf_op jit(solution)/shard_map/ppermute | solution.py:336
  154.7 4.3 %sweep.3 = (f32[32,512]{1,0:T(8,128)S(1)}, f32[32,512]{1,0:T(8,128)S(1)}) custom-call(f32[1024,512]{1,0:T(8,128)} %bitcast.1.product, f32[1024,512]{1,0:T(8,128)S(1)} %copy-done.1, f32[256,512]{1,0:T(8,128)S(1)} %join.8.mine, f32[256,512]{1,0:T(8,128)S(1)} %collective-permute-done.35.theirs), custom_call_target="tpu_custom_call" | custom-call | flops 1207959552 | bytes 4194304 | tf_op jit(solution)/shard_map/sweep/pallas_call | solution.py:262
  162.3 3.2 %collective-permute-start.40 = (f32[32,512]{1,0:T(8,128)S(1)}, f32[32,512]{1,0:T(8,128)S(1)}, u32[]{:S(2)}, u32[]{:S(2)}) collective-permute-start(f32[32,512]{1,0:T(8,128)S(1)} %get-tuple-element.75.refs_4_), channel_id=1, source_target_pairs={{0,8},{8,16},{16,24},{24,0},{32,40},{40,48},{48,56},{56,32},{64,72... | collective-permute-start | bytes 196616 | tf_op jit(solution)/shard_map/ppermute | solution.py:336
  167.8 3.5 %collective-permute-done.41.refs_7_ = f32[32,512]{1,0:T(8,128)S(1)} collective-permute-done((f32[32,512]{1,0:T(8,128)S(1)}, f32[32,512]{1,0:T(8,128)S(1)}, u32[]{:S(2)}, u32[]{:S(2)}) %collective-permute-start.41) | collective-permute-done | bytes 65568 | tf_op jit(solution)/shard_map/ppermute | solution.py:336
  171.5 3.2 %collective-permute-start.43 = (f32[128,512]{1,0:T(8,128)S(1)}, f32[128,512]{1,0:T(8,128)S(1)}, u32[]{:S(2)}, u32[]{:S(2)}) collective-permute-start(f32[128,512]{1,0:T(8,128)S(1)} %get-tuple-element.76.refs_0_), channel_id=1, source_target_pairs={{0,8},{8,16},{16,24},{24,0},{32,40},{40,48},{48,56},{56,32},{64,72... | collective-permute-start | bytes 786440 | tf_op jit(solution)/shard_map/ppermute | solution.py:336
  176.9 7.5 %collective-permute-done.42.refs_1_ = f32[128,512]{1,0:T(8,128)S(1)} collective-permute-done((f32[128,512]{1,0:T(8,128)S(1)}, f32[128,512]{1,0:T(8,128)S(1)}, u32[]{:S(2)}, u32[]{:S(2)}) %collective-permute-start.42) | collective-permute-done | bytes 262176 | tf_op jit(solution)/shard_map/ppermute | solution.py:336
  186.7 5.7 %collective-permute-done.47.refs_7_ = f32[128,512]{1,0:T(8,128)S(1)} collective-permute-done((f32[128,512]{1,0:T(8,128)S(1)}, f32[128,512]{1,0:T(8,128)S(1)}, u32[]{:S(2)}, u32[]{:S(2)}) %collective-permute-start.47) | collective-permute-done | bytes 262176 | tf_op jit(solution)/shard_map/ppermute | solution.py:336
  (113 shorter events, 80.2 us)
Async XLA Ops:
  7.2 52.7 %reduce-scatter.2.cloned.1.call-start = ((), (), s32[]{:S(2)}) async-start(), calls=%async_computation.2 | async-start | bytes 2621440 | tf_op jit(solution)/shard_map/reduce_scatter | solution.py:409
  47.1 6.6 %collective-permute-start.10 = (f32[64,512]{1,0:T(8,128)S(1)}, f32[64,512]{1,0:T(8,128)S(1)}, u32[]{:S(2)}, u32[]{:S(2)}) collective-permute-start(f32[64,512]{1,0:T(8,128)S(1)} %join.5.refs_0_), channel_id=1, source_target_pairs={{0,16},{8,24},{16,0},{24,8},{32,48},{40,56},{48,32},{56,40},{64,80... | collective-permute-start | bytes 393224 | tf_op jit(solution)/shard_map/ppermute | solution.py:336
  48.4 6.6 %collective-permute-start.8 = (f32[64,512]{1,0:T(8,128)S(1)}, f32[64,512]{1,0:T(8,128)S(1)}, u32[]{:S(2)}, u32[]{:S(2)}) collective-permute-start(f32[64,512]{1,0:T(8,128)S(1)} %join.5.refs_0_), channel_id=1, source_target_pairs={{0,24},{8,0},{16,8},{24,16},{32,56},{40,32},{48,40},{56,48},{64,88... | collective-permute-start | bytes 393224 | tf_op jit(solution)/shard_map/ppermute | solution.py:336
  48.4 6.6 %collective-permute-start.9 = (f32[64,512]{1,0:T(8,128)S(1)}, f32[64,512]{1,0:T(8,128)S(1)}, u32[]{:S(2)}, u32[]{:S(2)}) collective-permute-start(f32[64,512]{1,0:T(8,128)S(1)} %join.5.refs_0_), channel_id=1, source_target_pairs={{0,8},{8,16},{16,24},{24,0},{32,40},{40,48},{48,56},{56,32},{64,72... | collective-permute-start | bytes 393224 | tf_op jit(solution)/shard_map/ppermute | solution.py:336
  67.8 10.8 %collective-permute-start.15 = (f32[256,512]{1,0:T(8,128)S(1)}, f32[256,512]{1,0:T(8,128)S(1)}, u32[]{:S(2)}, u32[]{:S(2)}) collective-permute-start(f32[256,512]{1,0:T(8,128)S(1)} %get-tuple-element.48), channel_id=1, source_target_pairs={{0,1},{1,0},{2,3},{3,2},{4,5},{5,4},{6,7},{7,6},{8,9},{9,8},{10,11... | collective-permute-start | bytes 1572872 | tf_op jit(solution)/shard_map/ppermute | solution.py:328
  67.9 12.4 %collective-permute-start.16 = (f32[256,512]{1,0:T(8,128)S(1)}, f32[256,512]{1,0:T(8,128)S(1)}, u32[]{:S(2)}, u32[]{:S(2)}) collective-permute-start(f32[256,512]{1,0:T(8,128)S(1)} %sweep.2.w_ref.refs_2_), channel_id=1, source_target_pairs={{0,1},{1,0},{2,3},{3,2},{4,5},{5,4},{6,7},{7,6},{8,9},{9,8},{10,11... | collective-permute-start | bytes 1572872 | tf_op jit(solution)/shard_map/ppermute | solution.py:328
  68.4 25.1 %collective-permute-start.14 = (f32[256,512]{1,0:T(8,128)S(1)}, f32[256,512]{1,0:T(8,128)S(1)}, u32[]{:S(2)}, u32[]{:S(2)}) collective-permute-start(f32[256,512]{1,0:T(8,128)S(1)} %sweep.2.w_ref.refs_2_), channel_id=1, source_target_pairs={{0,6},{1,7},{2,0},{3,1},{4,2},{5,3},{6,4},{7,5},{8,14},{9,15},{10,... | collective-permute-start | bytes 1572872 | tf_op jit(solution)/shard_map/ppermute | solution.py:336
  69.2 26.1 %collective-permute-start.24 = (f32[256,512]{1,0:T(8,128)S(1)}, f32[256,512]{1,0:T(8,128)S(1)}, u32[]{:S(2)}, u32[]{:S(2)}) collective-permute-start(f32[256,512]{1,0:T(8,128)S(1)} %sweep.2.w_ref.refs_2_), channel_id=1, source_target_pairs={{0,2},{1,3},{2,4},{3,5},{4,6},{5,7},{6,0},{7,1},{8,10},{9,11},{10,... | collective-permute-start | bytes 1572872 | tf_op jit(solution)/shard_map/ppermute | solution.py:336
  70.4 28.5 %collective-permute-start.12 = (f32[256,512]{1,0:T(8,128)S(1)}, f32[256,512]{1,0:T(8,128)S(1)}, u32[]{:S(2)}, u32[]{:S(2)}) collective-permute-start(f32[256,512]{1,0:T(8,128)S(1)} %sweep.2.w_ref.refs_2_), channel_id=1, source_target_pairs={{0,4},{1,5},{2,6},{3,7},{4,0},{5,1},{6,2},{7,3},{8,12},{9,13},{10,... | collective-permute-start | bytes 1572872 | tf_op jit(solution)/shard_map/ppermute | solution.py:336
  80.3 8.7 %collective-permute-start.18 = (f32[64,512]{1,0:T(8,128)S(1)}, f32[64,512]{1,0:T(8,128)S(1)}, u32[]{:S(2)}, u32[]{:S(2)}) collective-permute-start(f32[64,512]{1,0:T(8,128)S(1)} %get-tuple-element.58), channel_id=1, source_target_pairs={{0,96},{8,104},{16,112},{24,120},{32,0},{40,8},{48,16},{56,24},{64... | collective-permute-start | bytes 393224 | tf_op jit(solution)/shard_map/ppermute | solution.py:332
  84.9 6.5 %collective-permute-start.19 = (f32[64,512]{1,0:T(8,128)S(1)}, f32[64,512]{1,0:T(8,128)S(1)}, u32[]{:S(2)}, u32[]{:S(2)}) collective-permute-start(f32[64,512]{1,0:T(8,128)S(1)} %get-tuple-element.59), channel_id=1, source_target_pairs={{0,64},{8,72},{16,80},{24,88},{32,96},{40,104},{48,112},{56,120},{... | collective-permute-start | bytes 393224 | tf_op jit(solution)/shard_map/ppermute | solution.py:332
  95.3 6.5 %collective-permute-start.25 = (f32[256,512]{1,0:T(8,128)S(1)}, f32[256,512]{1,0:T(8,128)S(1)}, u32[]{:S(2)}, u32[]{:S(2)}) collective-permute-start(f32[256,512]{1,0:T(8,128)S(1)} %collective-permute-done.24.refs_3_), channel_id=1, source_target_pairs={{0,1},{1,0},{2,3},{3,2},{4,5},{5,4},{6,7},{7,6},{8,9},{9,8},{10,11... | collective-permute-start | bytes 1572872 | tf_op jit(solution)/shard_map/ppermute | solution.py:328
  108.0 46.7 %all-to-all-start = ((f32[16,64,512]{2,1,0:T(8,128)}), f32[16,64,512]{2,1,0:T(8,128)}, u32[]{:S(2)}, u32[]{:S(2)}) async-start(f32[16,64,512]{2,1,0:T(8,128)} %bitcast.2), calls=%async_computation.1 | async-start | bytes 4194304 | tf_op jit(solution)/shard_map/all_to_all | solution.py:432
  122.9 6.5 %collective-permute-start.29 = (f32[16,512]{1,0:T(8,128)S(1)}, f32[16,512]{1,0:T(8,128)S(1)}, u32[]{:S(2)}, u32[]{:S(2)}) collective-permute-start(f32[16,512]{1,0:T(8,128)S(1)} %add.14.refs_0_), channel_id=1, source_target_pairs={{0,96},{8,104},{16,112},{24,120},{32,0},{40,8},{48,16},{56,24},{64... | collective-permute-start | bytes 98312 | tf_op jit(solution)/shard_map/ppermute | solution.py:336
  125.7 16.5 %collective-permute-start.30 = (f32[16,512]{1,0:T(8,128)S(1)}, f32[16,512]{1,0:T(8,128)S(1)}, u32[]{:S(2)}, u32[]{:S(2)}) collective-permute-start(f32[16,512]{1,0:T(8,128)S(1)} %add.14.refs_0_), channel_id=1, source_target_pairs={{0,32},{8,40},{16,48},{24,56},{32,64},{40,72},{48,80},{56,88},{64,... | collective-permute-start | bytes 98312 | tf_op jit(solution)/shard_map/ppermute | solution.py:336
  125.7 17.1 %collective-permute-start.31 = (f32[16,512]{1,0:T(8,128)S(1)}, f32[16,512]{1,0:T(8,128)S(1)}, u32[]{:S(2)}, u32[]{:S(2)}) collective-permute-start(f32[16,512]{1,0:T(8,128)S(1)} %add.14.refs_0_), channel_id=1, source_target_pairs={{0,64},{8,72},{16,80},{24,88},{32,96},{40,104},{48,112},{56,120},{... | collective-permute-start | bytes 98312 | tf_op jit(solution)/shard_map/ppermute | solution.py:336
  143.5 7.6 %collective-permute-start.33 = (f32[64,512]{1,0:T(8,128)S(1)}, f32[64,512]{1,0:T(8,128)S(1)}, u32[]{:S(2)}, u32[]{:S(2)}) collective-permute-start(f32[64,512]{1,0:T(8,128)S(1)} %join.7.refs_0_), channel_id=1, source_target_pairs={{0,8},{8,16},{16,24},{24,0},{32,40},{40,48},{48,56},{56,32},{64,72... | collective-permute-start | bytes 393224 | tf_op jit(solution)/shard_map/ppermute | solution.py:336
  158.9 6.6 %collective-permute-start.36 = (f32[32,512]{1,0:T(8,128)S(1)}, f32[32,512]{1,0:T(8,128)S(1)}, u32[]{:S(2)}, u32[]{:S(2)}) collective-permute-start(f32[32,512]{1,0:T(8,128)S(1)} %get-tuple-element.74.refs_0_), channel_id=1, source_target_pairs={{0,96},{8,104},{16,112},{24,120},{32,0},{40,8},{48,16},{56,24},{64... | collective-permute-start | bytes 196616 | tf_op jit(solution)/shard_map/ppermute | solution.py:336
  171.4 13.0 %collective-permute-start.42 = (f32[128,512]{1,0:T(8,128)S(1)}, f32[128,512]{1,0:T(8,128)S(1)}, u32[]{:S(2)}, u32[]{:S(2)}) collective-permute-start(f32[128,512]{1,0:T(8,128)S(1)} %get-tuple-element.76.refs_0_), channel_id=1, source_target_pairs={{0,24},{8,0},{16,8},{24,16},{32,56},{40,32},{48,40},{56,48},{64,88... | collective-permute-start | bytes 786440 | tf_op jit(solution)/shard_map/ppermute | solution.py:336
  171.5 15.2 %collective-permute-start.43 = (f32[128,512]{1,0:T(8,128)S(1)}, f32[128,512]{1,0:T(8,128)S(1)}, u32[]{:S(2)}, u32[]{:S(2)}) collective-permute-start(f32[128,512]{1,0:T(8,128)S(1)} %get-tuple-element.76.refs_0_), channel_id=1, source_target_pairs={{0,8},{8,16},{16,24},{24,0},{32,40},{40,48},{48,56},{56,32},{64,72... | collective-permute-start | bytes 786440 | tf_op jit(solution)/shard_map/ppermute | solution.py:336
  174.7 11.9 %collective-permute-start.44 = (f32[128,512]{1,0:T(8,128)S(1)}, f32[128,512]{1,0:T(8,128)S(1)}, u32[]{:S(2)}, u32[]{:S(2)}) collective-permute-start(f32[128,512]{1,0:T(8,128)S(1)} %get-tuple-element.76.refs_0_), channel_id=1, source_target_pairs={{0,16},{8,24},{16,0},{24,8},{32,48},{40,56},{48,32},{56,40},{64,80... | collective-permute-start | bytes 786440 | tf_op jit(solution)/shard_map/ppermute | solution.py:336
  174.7 11.9 %collective-permute-start.45 = (f32[128,512]{1,0:T(8,128)S(1)}, f32[128,512]{1,0:T(8,128)S(1)}, u32[]{:S(2)}, u32[]{:S(2)}) collective-permute-start(f32[128,512]{1,0:T(8,128)S(1)} %get-tuple-element.77.refs_4_), channel_id=1, source_target_pairs={{0,96},{8,104},{16,112},{24,120},{32,0},{40,8},{48,16},{56,24},{64... | collective-permute-start | bytes 786440 | tf_op jit(solution)/shard_map/ppermute | solution.py:336
  176.1 10.6 %collective-permute-start.46 = (f32[128,512]{1,0:T(8,128)S(1)}, f32[128,512]{1,0:T(8,128)S(1)}, u32[]{:S(2)}, u32[]{:S(2)}) collective-permute-start(f32[128,512]{1,0:T(8,128)S(1)} %get-tuple-element.77.refs_4_), channel_id=1, source_target_pairs={{0,32},{8,40},{16,48},{24,56},{32,64},{40,72},{48,80},{56,88},{64,... | collective-permute-start | bytes 786440 | tf_op jit(solution)/shard_map/ppermute | solution.py:336
  184.4 7.9 %collective-permute-start.47 = (f32[128,512]{1,0:T(8,128)S(1)}, f32[128,512]{1,0:T(8,128)S(1)}, u32[]{:S(2)}, u32[]{:S(2)}) collective-permute-start(f32[128,512]{1,0:T(8,128)S(1)} %get-tuple-element.77.refs_4_), channel_id=1, source_target_pairs={{0,64},{8,72},{16,80},{24,88},{32,96},{40,104},{48,112},{56,120},{... | collective-permute-start | bytes 786440 | tf_op jit(solution)/shard_map/ppermute | solution.py:336
  (32 other events, 146.6 us)
Sparse Core Ops, SparseCore 0:
  28.0 31.8 reduce-scatter.1
where the time goes:
time: 202 us; the launch traced here: 201 us
  waiting for transfers between devices  69.9 us (35%)
  starting transfers between devices  64.8 us (32%)
  Pallas kernels  42.4 us (21%)
  between operations  14.3 us (7%)
  local copies, waits for them, and re-layouts  9.24 us (5%)
    ppermute x33, waiting for transfers between devices, fetch(): return [lax.ppermute(a, axis, table[(4 - r) % 4]) for r in REL[1:]]  53.6 us
    ppermute x33, starting transfers between devices, fetch(): return [lax.ppermute(a, axis, table[(4 - r) % 4]) for r in REL[1:]]  46.9 us
    pallas_call x3, Pallas kernels, prod(): pl.pallas_call(functools.partial(prod_kernel, chunks, sibling, first, len...  17.8 us
    unnamed x12, local copies, waits for them, and re-layouts  9.24 us
    pallas_call x4, Pallas kernels, back(): pl.pallas_call(functools.partial(back_kernel, tuple(chunks), bool(carry))...  9.22 us
    ppermute x6, waiting for transfers between devices, send(): return lax.ppermute(a, axis, table[r])  8.99 us
    ppermute x6, starting transfers between devices, send(): return lax.ppermute(a, axis, table[r])  8.75 us
    pallas_call x2, Pallas kernels, sweep(): pl.pallas_call(functools.partial(sweep_kernel, axis), out_shape=[sds(rows...  8.27 us
  transfers between devices with their start and end apart: 50, of which 28 were waited for; matrix products, arithmetic and copies ran while one was open for 0% of the time, Pallas kernels for 7%

commit v1 on v0

--- a/solution.py
+++ b/solution.py
@@ -43,60 +43,57 @@
     return s // 4, s % 4, q // 2, q % 2
 
 
-def prod_kernel(chunks, sibling, first, nadd, *refs):
+def prod_kernel(chunks, sibling, first, recv, last, *refs):
     refs = list(refs)
     x_ref = refs.pop(0)
     if first:
         h_ref = refs.pop(0)
     else:
         hh_ref, hl_ref = refs.pop(0), refs.pop(0)
-    adds = [refs.pop(0) for _ in range(nadd)]
+    recv_ref = refs.pop(0) if recv else None
+    low_ref = refs.pop(0) if last else None
     out_ref = refs.pop(0)
     if first:
         hh_ref, hl_ref = refs.pop(0), refs.pop(0)
-    xs, sem = refs
-    _, _, _, c = place()
-    cc = 1 - c if sibling else c
-    copies = []
-    for i, k in enumerate(chunks):
-        row = pl.multiple_of(512 * k + 256 * cc, 256)
-        cp = pltpu.make_async_copy(x_ref.at[pl.ds(row, 256), :], xs.at[pl.ds(256 * i, 256), :], sem.at[i])
-        cp.start()
-        copies.append(cp)
-    if first:
         hh, hl = split(h_ref[...])
         hh_ref[...] = hh
         hl_ref[...] = hl
-    if nadd:
-        n = adds[0].shape[0]
-        out_ref[:n, :] = adds[0][...] + adds[1][:n, :]
+    _, _, _, c = place()
+    cc = 1 - c if sibling else c
+    if last:
+        tmp, sem = refs
+        low = pltpu.make_async_copy(low_ref, out_ref.at[pl.ds(0, 512), :], sem.at[0])
+        low.start()
+    rows = [x_ref[pl.ds(pl.multiple_of(512 * k + 256 * cc, 256), 256), :] for k in chunks]
+    ah, al = split(jnp.concatenate(rows, axis=0))
+    out = dot3(ah, al, hh_ref[...], hl_ref[...])
+    if recv:
+        out = out + recv_ref[...]
+    if last:
+        tmp[...] = out
+        high = pltpu.make_async_copy(tmp, out_ref.at[pl.ds(512, 512), :], sem.at[1])
+        high.start()
+        low.wait()
+        high.wait()
     else:
-        n = 0
-    for at in range(0, 256 * len(chunks), 512):
-        copies[at // 256].wait()
-        copies[at // 256 + 1].wait()
-        ah, al = split(xs[at : at + 512, :])
-        out = dot3(ah, al, hh_ref[...], hl_ref[...])
-        if nadd:
-            out = out + adds[1][n + at : n + at + 512, :]
-        out_ref[n + at : n + at + 512, :] = out
-
-
-def prod(spectra, h, chunks, sibling, adds=()):
+        out_ref[...] = out
+
+
+def prod(spectra, h, chunks, sibling, recv=None, low=None):
     first = not isinstance(h, tuple)
-    n = 256 * len(chunks)
-    ins = [spectra] + ([h] if first else list(h)) + list(adds)
-    outs = [sds(n + (adds[0].shape[0] if adds else 0), 512)]
+    last = low is not None
+    ins = [spectra] + ([h] if first else list(h)) + ([] if recv is None else [recv]) + ([low] if last else [])
+    outs = [sds(1024 if last else 512, 512)]
     if first:
         outs += [sds(1024, 512, dtype=bf16)] * 2
     out = pl.pallas_call(
-        functools.partial(prod_kernel, chunks, sibling, first, len(adds)),
+        functools.partial(prod_kernel, chunks, sibling, first, recv is not None, last),
         out_shape=outs,
-        in_specs=[HBM] + [VM] * (len(ins) - 1),
-        out_specs=[VM] * len(outs),
-        scratch_shapes=[pltpu.VMEM((n, 1024), f32), pltpu.SemaphoreType.DMA((len(chunks),))],
-        compiler_params=params(50),
-        cost_estimate=cost(6 * n * 1024 * 512, n * 6144 + (2 << 20)),
+        in_specs=[VM] * len(ins),
+        out_specs=[HBM] if last else [VM] * len(outs),
+        scratch_shapes=[pltpu.VMEM((512, 512), f32), pltpu.SemaphoreType.DMA((2,))] if last else [],
+        compiler_params=params(14),
+        cost_estimate=cost(6 * 512 * 1024 * 512, 6 << 20),
         name="prod",
     )(*ins)
     return out if first else out[0]
@@ -117,7 +114,7 @@
         out_shape=[sds(16, 1024, 128, dtype=bf16)] * 2,
         in_specs=[pl.BlockSpec((128, 1024), lambda i: (i, 0))],
         out_specs=[spec, spec],
-        compiler_params=params(6),
+        compiler_params=params(44),
         cost_estimate=cost(1 << 24, 16 << 20),
         name="flip",
     )(spectra)
@@ -130,7 +127,7 @@
     acc_ref = refs.pop(0) if later else None
     if later:
         refs.pop(0)
-    out_ref, w_out, sem = refs
+    out_ref, w_out, sem = refs[:3]
     z, y, x, c = place()
     at, copies = [], []
     for k, (r, sibling) in enumerate(chunks):
@@ -147,20 +144,26 @@
         out = dot3(ah, al, wh, wl)
         if later:
             out = out + acc_ref[rows, :]
-        out_ref[rows, :] = out
+        if len(refs) > 3:
+            refs[3][rows, :] = out
+            cp = pltpu.make_async_copy(refs[3].at[rows, :], out_ref.at[rows, :], sem.at[2 + k // 512])
+            cp.start()
+            copies.append(cp)
+        else:
+            out_ref[rows, :] = out
     for cp in copies:
         cp.wait()
 
 
-def back(flipped, ws, chunks, carry=()):
+def back(flipped, ws, chunks, carry=(), last=False):
     ins = list(flipped) + list(ws) + list(carry)
     n = len(ins)
     return pl.pallas_call(
         functools.partial(back_kernel, tuple(chunks), bool(carry)),
         out_shape=[sds(1024, 512), sds(2048, 512)],
         in_specs=[VM] * (2 + len(ws)) + ([VM, HBM] if carry else []),
-        out_specs=[VM, HBM],
-        scratch_shapes=[pltpu.SemaphoreType.DMA((len(ws),))],
+        out_specs=[HBM if last else VM, HBM],
+        scratch_shapes=[pltpu.SemaphoreType.DMA((4,))] + ([pltpu.VMEM((1024, 512), f32)] if last else []),
         input_output_aliases={n - 1: 1} if carry else {},
         compiler_params=params(12),
         cost_estimate=cost(6 * 1024 * 512 * 256 * len(chunks), 6 << 20),
@@ -193,15 +196,14 @@
 
 
 def gram_w_kernel(w_ref, mine_ref, theirs_ref, tmp):
-    z, y, _, c = place()
+    _, _, x, c = place()
     w = w_ref[...]
     tmp[...] = dot3(*split(w.T), *split(w))
     for k in range(4):
-        for m in range(4):
-            s = 4 * ((z + REL[k]) % 4) + (y + REL[m]) % 4
-            at = 64 * k + 16 * m
-            mine_ref[at : at + 16, :] = tmp[pl.ds(pl.multiple_of(32 * s + 16 * c, 16), 16), :]
-            theirs_ref[at : at + 16, :] = tmp[pl.ds(pl.multiple_of(32 * s + 16 * (1 - c), 16), 16), :]
+        row = 128 * ((x + REL[k]) % 4)
+        rows = slice(64 * k, 64 * (k + 1))
+        mine_ref[rows, :] = tmp[pl.ds(pl.multiple_of(row + 64 * c, 64), 64), :]
+        theirs_ref[rows, :] = tmp[pl.ds(pl.multiple_of(row + 64 * (1 - c), 64), 64), :]
 
 
 def gram_w(w):
@@ -227,6 +229,10 @@
     for t, piece in enumerate((mine, theirs)):
         cc = c if t == 0 else 1 - c
         for j in range(4):
+            if axis == "samp":
+                row = 128 * ((x + REL[j]) % 4) + 64 * cc
+                g[pl.ds(pl.multiple_of(row, 64), 64), :] = piece[64 * j : 64 * j + 64, :]
+                continue
             for i in range(4):
                 row = 32 * (4 * ((z + REL[i]) % 4) + (y + REL[j]) % 4) + 16 * cc
                 g[pl.ds(pl.multiple_of(row, 16), 16), :] = piece[64 * j + 16 * i : 64 * j + 16 * i + 16, :]
@@ -274,7 +280,7 @@
             pltpu.VMEM((rows, 512), f32),
             pltpu.SemaphoreType.DMA,
         ],
-        compiler_params=params(12),
+        compiler_params=params(50),
         cost_estimate=cost(72 * rows * 512 * 512, 4 << 20),
         name="sweep",
     )(product, start, *pieces)
@@ -322,6 +328,8 @@
 XGROUPS = [[0, 2, 4, 6], [1, 3, 5, 7]]
 CORE, X = moves("col", "core"), moves("col", "x")
 Y, Z = moves("samp", "y"), moves("samp", "z")
+Y_PAIRS = [[(i, i ^ k) for i in range(16)] for k in (1, 3)]
+Z_PAIRS = [[(i, i ^ k) for i in range(16)] for k in (4, 12)]
 
 
 def swap(a):
@@ -391,6 +399,10 @@
     return [pieces[0]] + [send(pieces[k], axis, table, REL[k]) for k in (1, 2, 3)]
 
 
+def pair_sum(a, pairs):
+    return add([a, lax.ppermute(a, "samp", pairs)])
+
+
 def over_all(strip):
     strip = add([strip] + fetch(strip, "col", X))
     strip = join([strip] + fetch(strip, "samp", Z))
@@ -399,14 +411,16 @@
 
 
 def shards(spectra, w_start, h_start):
-    a, hh, hl = prod(spectra, h_start, (0, 1, 2, 3), True)
-    recv = swap(a)
-    g_mine, g_theirs = gram_h(after(h_start, a))
+    g_mine, g_theirs = gram_h(h_start)
+    a1, hh, hl = prod(spectra, after(h_start, g_mine), (0, 1), True)
+    r1 = swap(a1)
+    h = (hh, hl)
+    a2 = prod(spectra, h, (2, 3), True)
+    r2 = swap(a2)
     g_theirs = swap(g_theirs)
-    h = (after(hh, g_mine), hl)
-    low = prod(spectra, h, (0, 1), False)
-    both = prod(spectra, h, (2, 3), False, (low, recv))
-    product = lax.psum_scatter(both, "col", scatter_dimension=0, axis_index_groups=XGROUPS, tiled=True)
+    low = prod(spectra, h, (0, 1), False, after(r1, a2))
+    both = prod(spectra, h, (2, 3), False, r2, low)
+    product = lax.all_to_all(both, "col", 0, 0, axis_index_groups=XGROUPS, tiled=True)
 
     pieces_h = over_all(add([after(g_mine, both), g_theirs]))
 
@@ -417,21 +431,22 @@
 
     g_mine, g_theirs = gram_w(w)
     flipped = flip(after(spectra, g_theirs))
-    strips = add([g_mine, after(swap(g_theirs), *flipped)], 4)
-    strips = deal(strips, "samp", Z)
+    slices = deal(add([g_mine, after(swap(g_theirs), *flipped)], 4), "col", X)
     carry = back(flipped, (w, ws), ((0, False), (0, True)))
-    strips = add([after(strips[0], carry[0])] + strips[1:], 4)
-    strips = deal(strips, "samp", Y)
-    sib_p, sib_m = swap(after(near_p, *strips)), swap(near_m)
-    carry = back(flipped, (near_p, near_m), ((1, False), (3, False)), carry)
-    strip = add([after(strips[0], carry[0])] + strips[1:])
-    carry = back(flipped, (sib_p, sib_m), ((1, True), (3, True)), carry)
+    part = add([after(slices[0], carry[0])] + slices[1:])
+    part = pair_sum(part, Y_PAIRS[0])
+    sib_p, sib_m = swap(after(near_p, part)), swap(after(near_m, part))
+    part = pair_sum(part, Y_PAIRS[1])
+    carry = back(flipped, (near_p, near_m), ((1, False), (3, False)), (after(carry[0], part), carry[1]))
+    part = pair_sum(after(part, carry[0]), Z_PAIRS[0])
+    carry = back(flipped, (sib_p, sib_m), ((1, True), (3, True)), (after(carry[0], part), carry[1]))
+    part = pair_sum(after(part, carry[0]), Z_PAIRS[1])
     sib_f = swap(far)
-    back_sum, w_out = back(flipped, (far, sib_f), ((2, False), (2, True)), carry)
+    back_sum, w_out = back(flipped, (far, sib_f), ((2, False), (2, True)), carry, True)
 
     product = lax.all_to_all(back_sum, "samp", 0, 0, tiled=True)
-    pieces_w = over_all(after(strip, back_sum))
-    ha, hb = sweep(product, h_start, "samp", 64, pieces_w, 2)
+    part = join([after(part, back_sum)] + fetch(part, "col", X))
+    ha, hb = sweep(product, h_start, "samp", 64, (part, swap(part)), 2)
 
     row_a, row_b = join([ha] + fetch(ha, "samp", Z) + [hb] + fetch(hb, "samp", Y), 2)
     h_out = lay_h([row_a] + fetch(row_a, "samp", Y) + [row_b] + fetch(row_b, "samp", Z))

time: 202 us -> 223 us (1.10)
  waiting for transfers between devices: 69.9 us -> 120 us
  between operations: 14.3 us -> 0.94 us
  starting transfers between devices: 64.8 us -> 55.6 us
  Pallas kernels: 42.4 us -> 39.1 us
  local copies, waits for them, and re-layouts: 9.24 us -> 6.58 us
    ppermute x0 -> x4, waiting for transfers between devices: none -> 39.1 us  [pair_sum(): return add([a, lax.ppermute(a, 'samp', pairs)])]
    ppermute x33 -> x27, starting transfers between devices: 46.9 us -> 35.5 us  [fetch(): return [lax.ppermute(a, axis, table[(4 - r) % 4]) for r in REL[1:]]]
    pallas_call x3 -> x4, Pallas kernels: 17.8 us -> 8.14 us  [prod(): pl.pallas_call(functools.partial(prod_kernel, chunks, sibling, first, rec...]
    ppermute x6 -> x3, waiting for transfers between devices: 8.99 us -> 18.5 us  [send(): return lax.ppermute(a, axis, table[r])]
    pallas_call x1, Pallas kernels: 3.33 us -> 10.5 us  [flip(): pl.pallas_call(flip_kernel, grid=(16,), out_shape=[sds(16, 1024, 128, dty...]
    ppermute x6 -> x3, starting transfers between devices: 8.75 us -> 1.85 us  [send(): return lax.ppermute(a, axis, table[r])]
    ppermute x0 -> x4, starting transfers between devices: none -> 4.51 us  [pair_sum(): return add([a, lax.ppermute(a, 'samp', pairs)])]
    all_to_all x0 -> x1, starting transfers between devices: none -> 4.31 us  [shards(): lax.all_to_all(both, 'col', 0, 0, axis_index_groups=XGROUPS, tiled=True)]
  transfers between devices with their start and end apart: 50 -> 46, of which waited for: 28 -> 27; matrix products, arithmetic and copies ran while one was open for 0% -> 0% of each run, Pallas kernels for 7% -> 10%
where the time goes in v1:
time: 223 us; the launch traced here: 222 us
  waiting for transfers between devices  120 us (54%)
  starting transfers between devices  55.6 us (25%)
  Pallas kernels  39.1 us (18%)
  local copies, waits for them, and re-layouts  6.58 us (3%)
    ppermute x27, waiting for transfers between devices, fetch(): return [lax.ppermute(a, axis, table[(4 - r) % 4]) for r in REL[1:]]  56.8 us
    ppermute x4, waiting for transfers between devices, pair_sum(): return add([a, lax.ppermute(a, 'samp', pairs)])  39.1 us
    ppermute x27, starting transfers between devices, fetch(): return [lax.ppermute(a, axis, table[(4 - r) % 4]) for r in REL[1:]]  35.5 us
    ppermute x3, waiting for transfers between devices, send(): return lax.ppermute(a, axis, table[r])  18.5 us
    pallas_call x1, Pallas kernels, flip(): pl.pallas_call(flip_kernel, grid=(16,), out_shape=[sds(16, 1024, 128, dty...  10.5 us
    pallas_call x4, Pallas kernels, back(): pl.pallas_call(functools.partial(back_kernel, tuple(chunks), bool(carry))...  9.06 us
    pallas_call x4, Pallas kernels, prod(): pl.pallas_call(functools.partial(prod_kernel, chunks, sibling, first, rec...  8.14 us
    pallas_call x2, Pallas kernels, sweep(): pl.pallas_call(functools.partial(sweep_kernel, axis), out_shape=[sds(rows...  7.66 us
  transfers between devices with their start and end apart: 46, of which 27 were waited for; matrix products, arithmetic and copies ran while one was open for 0% of the time, Pallas kernels for 10%

profile of v1, /device:TPU:24, one launch (start us, length us, event | category | flops | bytes accessed | tf_op | source)
XLA Modules:
  0.0 222.0 jit_solution(9598606424833012682)
XLA Ops:
  3.8 3.4 %copy-done = f32[2048,1024]{1,0:T(8,128)S(1)} copy-done((f32[2048,1024]{1,0:T(8,128)S(1)}, f32[2048,1024]{1,0:T(8,128)}, u32[]{:S(2)}) %copy-start) | copy-done | bytes 8388632
  13.7 2.8 %prod.7 = f32[1024,512]{1,0:T(8,128)} custom-call(f32[2048,1024]{1,0:T(8,128)S(1)} %copy-done, bf16[1024,512]{1,0:T(8,128)(2,1)S(1)} %get-tuple-element.42.refs_1_, bf16[1024,512]{1,0:T(8,128)(2,1)S(1)} %get-tuple-element.43.refs_2_, f32[512,512]{1,0:T(8,128)S(1)} %collective-permute-done.refs_3_, f32[512,512]{1,0:T(8,128)S(1)} %prod.6.refs_4_), custom_call_target="tpu_custom_call" | custom-call | flops 1610612736 | bytes 6291456 | tf_op jit(solution)/shard_map/prod/pallas_call | solution.py:89
  16.5 4.3 %all-to-all-start = ((f32[4,256,512]{2,1,0:T(8,128)}), f32[4,256,512]{2,1,0:T(8,128)S(1)}, u32[]{:S(2)}, u32[]{:S(2)}) async-start(f32[4,256,512]{2,1,0:T(8,128)} %bitcast), calls=%async_computation | async-start | bytes 4194304 | tf_op jit(solution)/shard_map/all_to_all | solution.py:423
  22.1 3.2 %collective-permute-start.3 = (f32[16,512]{1,0:T(8,128)S(1)}, f32[16,512]{1,0:T(8,128)S(1)}, u32[]{:S(2)}, u32[]{:S(2)}) collective-permute-start(f32[16,512]{1,0:T(8,128)S(1)} %add.8.refs_0_), channel_id=1, source_target_pairs={{0,6},{1,7},{2,0},{3,1},{4,2},{5,3},{6,4},{7,5},{8,14},{9,15},{10,... | collective-permute-start | bytes 98312 | tf_op jit(solution)/shard_map/ppermute | solution.py:344
  27.6 19.6 %collective-permute-done.3.refs_1_ = f32[16,512]{1,0:T(8,128)S(1)} collective-permute-done((f32[16,512]{1,0:T(8,128)S(1)}, f32[16,512]{1,0:T(8,128)S(1)}, u32[]{:S(2)}, u32[]{:S(2)}) %collective-permute-start.3) | collective-permute-done | bytes 32800 | tf_op jit(solution)/shard_map/ppermute | solution.py:344
  49.2 4.1 %collective-permute-start.6 = (f32[16,512]{1,0:T(8,128)S(1)}, f32[16,512]{1,0:T(8,128)S(1)}, u32[]{:S(2)}, u32[]{:S(2)}) collective-permute-start(f32[16,512]{1,0:T(8,128)S(1)} %add.9.refs_0_), channel_id=1, source_target_pairs={{0,96},{8,104},{16,112},{24,120},{32,0},{40,8},{48,16},{56,24},{64... | collective-permute-start | bytes 98312 | tf_op jit(solution)/shard_map/ppermute | solution.py:344
  55.1 3.3 %collective-permute-done.7.refs_2_ = f32[16,512]{1,0:T(8,128)S(1)} collective-permute-done((f32[16,512]{1,0:T(8,128)S(1)}, f32[16,512]{1,0:T(8,128)S(1)}, u32[]{:S(2)}, u32[]{:S(2)}) %collective-permute-start.7) | collective-permute-done | bytes 32800 | tf_op jit(solution)/shard_map/ppermute | solution.py:344
  70.0 4.6 %sweep.2.w_ref.refs_2_ = f32[256,512]{1,0:T(8,128)S(1)} custom-call(f32[1024,512]{1,0:T(8,128)S(1)} %bitcast.5, f32[2048,512]{1,0:T(8,128)} %start.2, f32[256,512]{1,0:T(8,128)S(1)} %join.5.mine, f32[256,512]{1,0:T(8,128)S(1)} %collective-permute-done.12.theirs), custom_call_target="tpu_custom_call" | custom-call | flops 4831838208 | bytes 4194304 | tf_op jit(solution)/shard_map/sweep/pallas_call | solution.py:268
  76.5 2.7 %collective-permute-start.15 = (f32[256,512]{1,0:T(8,128)S(1)}, f32[256,512]{1,0:T(8,128)S(1)}, u32[]{:S(2)}, u32[]{:S(2)}) collective-permute-start(f32[256,512]{1,0:T(8,128)S(1)} %sweep.2.w_ref.refs_2_), channel_id=1, source_target_pairs={{0,6},{1,7},{2,0},{3,1},{4,2},{5,3},{6,4},{7,5},{8,14},{9,15},{10,... | collective-permute-start | bytes 1572872 | tf_op jit(solution)/shard_map/ppermute | solution.py:344
  79.2 10.5 %flip.1 = (bf16[16,1024,128]{2,1,0:T(8,128)(2,1)S(1)}, bf16[16,1024,128]{2,1,0:T(8,128)(2,1)S(1)}) custom-call(f32[2048,1024]{1,0:T(8,128)} %x_ref), custom_call_target="tpu_custom_call" | custom-call | flops 16777216 | bytes 16777216 | tf_op jit(solution)/shard_map/flip/pallas_call | solution.py:111
  93.1 14.2 %collective-permute-done.18.refs_1_ = f32[64,512]{1,0:T(8,128)S(1)} collective-permute-done((f32[64,512]{1,0:T(8,128)S(1)}, f32[64,512]{1,0:T(8,128)S(1)}, u32[]{:S(2)}, u32[]{:S(2)}) %collective-permute-start.18) | collective-permute-done | bytes 131104 | tf_op jit(solution)/shard_map/ppermute | solution.py:340
  109.4 4.3 %collective-permute-done.20.refs_3_ = f32[64,512]{1,0:T(8,128)S(1)} collective-permute-done((f32[64,512]{1,0:T(8,128)S(1)}, f32[64,512]{1,0:T(8,128)S(1)}, u32[]{:S(2)}, u32[]{:S(2)}) %collective-permute-start.20) | collective-permute-done | bytes 131104 | tf_op jit(solution)/shard_map/ppermute | solution.py:340
  114.1 4.7 %collective-permute-done.21.refs_1_ = f32[64,512]{1,0:T(8,128)S(1)} collective-permute-done((f32[64,512]{1,0:T(8,128)S(1)}, f32[64,512]{1,0:T(8,128)S(1)}, u32[]{:S(2)}, u32[]{:S(2)}) %collective-permute-start.21) | collective-permute-done | bytes 131104 | tf_op jit(solution)/shard_map/ppermute | solution.py:403
  120.1 6.0 %collective-permute-done.25.refs_1_ = f32[64,512]{1,0:T(8,128)S(1)} collective-permute-done((f32[64,512]{1,0:T(8,128)S(1)}, f32[64,512]{1,0:T(8,128)S(1)}, u32[]{:S(2)}, u32[]{:S(2)}) %collective-permute-start.25) | collective-permute-done | bytes 131104 | tf_op jit(solution)/shard_map/ppermute | solution.py:403
  129.4 4.5 %collective-permute-done.26.refs_1_ = f32[64,512]{1,0:T(8,128)S(1)} collective-permute-done((f32[64,512]{1,0:T(8,128)S(1)}, f32[64,512]{1,0:T(8,128)S(1)}, u32[]{:S(2)}, u32[]{:S(2)}) %collective-permute-start.26) | collective-permute-done | bytes 131104 | tf_op jit(solution)/shard_map/ppermute | solution.py:403
  139.8 7.2 %all-to-all-start.1 = ((f32[16,64,512]{2,1,0:T(8,128)}), f32[16,64,512]{2,1,0:T(8,128)S(1)}, u32[]{:S(2)}, u32[]{:S(2)}) async-start(f32[16,64,512]{2,1,0:T(8,128)} %bitcast.6), calls=%async_computation.1 | async-start | bytes 4194304 | tf_op jit(solution)/shard_map/all_to_all | solution.py:447
  149.6 23.9 %collective-permute-done.27.refs_1_ = f32[64,512]{1,0:T(8,128)S(1)} collective-permute-done((f32[64,512]{1,0:T(8,128)S(1)}, f32[64,512]{1,0:T(8,128)S(1)}, u32[]{:S(2)}, u32[]{:S(2)}) %collective-permute-start.27) | collective-permute-done | bytes 131104 | tf_op jit(solution)/shard_map/ppermute | solution.py:403
  175.6 3.9 %collective-permute-done.28.refs_1_ = f32[64,512]{1,0:T(8,128)S(1)} collective-permute-done((f32[64,512]{1,0:T(8,128)S(1)}, f32[64,512]{1,0:T(8,128)S(1)}, u32[]{:S(2)}, u32[]{:S(2)}) %collective-permute-start.28) | collective-permute-done | bytes 131104 | tf_op jit(solution)/shard_map/ppermute | solution.py:344
  179.5 2.8 %collective-permute-done.29.refs_2_ = f32[64,512]{1,0:T(8,128)S(1)} collective-permute-done((f32[64,512]{1,0:T(8,128)S(1)}, f32[64,512]{1,0:T(8,128)S(1)}, u32[]{:S(2)}, u32[]{:S(2)}) %collective-permute-start.29) | collective-permute-done | bytes 131104 | tf_op jit(solution)/shard_map/ppermute | solution.py:344
  184.4 3.0 %sweep.3 = (f32[32,512]{1,0:T(8,128)S(1)}, f32[32,512]{1,0:T(8,128)S(1)}) custom-call(f32[1024,512]{1,0:T(8,128)S(1)} %bitcast.4, f32[1024,512]{1,0:T(8,128)} %start.3, f32[256,512]{1,0:T(8,128)S(1)} %join.6.mine, f32[256,512]{1,0:T(8,128)S(1)} %collective-permute-done.31.theirs), custom_call_target="tpu_custom_call" | custom-call | flops 1207959552 | bytes 4194304 | tf_op jit(solution)/shard_map/sweep/pallas_call | solution.py:268
  196.3 3.3 %collective-permute-done.37.refs_7_ = f32[32,512]{1,0:T(8,128)S(1)} collective-permute-done((f32[32,512]{1,0:T(8,128)S(1)}, f32[32,512]{1,0:T(8,128)S(1)}, u32[]{:S(2)}, u32[]{:S(2)}) %collective-permute-start.37) | collective-permute-done | bytes 65568 | tf_op jit(solution)/shard_map/ppermute | solution.py:344
  199.7 3.2 %collective-permute-start.39 = (f32[128,512]{1,0:T(8,128)S(1)}, f32[128,512]{1,0:T(8,128)S(1)}, u32[]{:S(2)}, u32[]{:S(2)}) collective-permute-start(f32[128,512]{1,0:T(8,128)S(1)} %get-tuple-element.76.refs_0_), channel_id=1, source_target_pairs={{0,8},{8,16},{16,24},{24,0},{32,40},{40,48},{48,56},{56,32},{64,72... | collective-permute-start | bytes 786440 | tf_op jit(solution)/shard_map/ppermute | solution.py:344
  204.9 7.7 %collective-permute-done.38.refs_1_ = f32[128,512]{1,0:T(8,128)S(1)} collective-permute-done((f32[128,512]{1,0:T(8,128)S(1)}, f32[128,512]{1,0:T(8,128)S(1)}, u32[]{:S(2)}, u32[]{:S(2)}) %collective-permute-start.38) | collective-permute-done | bytes 262176 | tf_op jit(solution)/shard_map/ppermute | solution.py:344
  215.1 5.3 %collective-permute-done.43.refs_7_ = f32[128,512]{1,0:T(8,128)S(1)} collective-permute-done((f32[128,512]{1,0:T(8,128)S(1)}, f32[128,512]{1,0:T(8,128)S(1)}, u32[]{:S(2)}, u32[]{:S(2)}) %collective-permute-start.43) | collective-permute-done | bytes 262176 | tf_op jit(solution)/shard_map/ppermute | solution.py:344
  (102 shorter events, 68.6 us)
Async XLA Ops:
  16.5 53.5 %all-to-all-start = ((f32[4,256,512]{2,1,0:T(8,128)}), f32[4,256,512]{2,1,0:T(8,128)S(1)}, u32[]{:S(2)}, u32[]{:S(2)}) async-start(f32[4,256,512]{2,1,0:T(8,128)} %bitcast), calls=%async_computation | async-start | bytes 4194304 | tf_op jit(solution)/shard_map/all_to_all | solution.py:423
  22.1 25.2 %collective-permute-start.3 = (f32[16,512]{1,0:T(8,128)S(1)}, f32[16,512]{1,0:T(8,128)S(1)}, u32[]{:S(2)}, u32[]{:S(2)}) collective-permute-start(f32[16,512]{1,0:T(8,128)S(1)} %add.8.refs_0_), channel_id=1, source_target_pairs={{0,6},{1,7},{2,0},{3,1},{4,2},{5,3},{6,4},{7,5},{8,14},{9,15},{10,... | collective-permute-start | bytes 98312 | tf_op jit(solution)/shard_map/ppermute | solution.py:344
  25.3 22.4 %collective-permute-start.4 = (f32[16,512]{1,0:T(8,128)S(1)}, f32[16,512]{1,0:T(8,128)S(1)}, u32[]{:S(2)}, u32[]{:S(2)}) collective-permute-start(f32[16,512]{1,0:T(8,128)S(1)} %add.8.refs_0_), channel_id=1, source_target_pairs={{0,2},{1,3},{2,4},{3,5},{4,6},{5,7},{6,0},{7,1},{8,10},{9,11},{10,... | collective-permute-start | bytes 98312 | tf_op jit(solution)/shard_map/ppermute | solution.py:344
  25.3 23.9 %collective-permute-start.5 = (f32[16,512]{1,0:T(8,128)S(1)}, f32[16,512]{1,0:T(8,128)S(1)}, u32[]{:S(2)}, u32[]{:S(2)}) collective-permute-start(f32[16,512]{1,0:T(8,128)S(1)} %add.8.refs_0_), channel_id=1, source_target_pairs={{0,4},{1,5},{2,6},{3,7},{4,0},{5,1},{6,2},{7,3},{8,12},{9,13},{10,... | collective-permute-start | bytes 98312 | tf_op jit(solution)/shard_map/ppermute | solution.py:344
  75.4 14.3 %collective-permute-start.16 = (f32[256,512]{1,0:T(8,128)S(1)}, f32[256,512]{1,0:T(8,128)S(1)}, u32[]{:S(2)}, u32[]{:S(2)}) collective-permute-start(f32[256,512]{1,0:T(8,128)S(1)} %get-tuple-element.48), channel_id=1, source_target_pairs={{0,1},{1,0},{2,3},{3,2},{4,5},{5,4},{6,7},{7,6},{8,9},{9,8},{10,11... | collective-permute-start | bytes 1572872 | tf_op jit(solution)/shard_map/ppermute | solution.py:336
  75.6 15.7 %collective-permute-start.17 = (f32[256,512]{1,0:T(8,128)S(1)}, f32[256,512]{1,0:T(8,128)S(1)}, u32[]{:S(2)}, u32[]{:S(2)}) collective-permute-start(f32[256,512]{1,0:T(8,128)S(1)} %sweep.2.w_ref.refs_2_), channel_id=1, source_target_pairs={{0,1},{1,0},{2,3},{3,2},{4,5},{5,4},{6,7},{7,6},{8,9},{9,8},{10,11... | collective-permute-start | bytes 1572872 | tf_op jit(solution)/shard_map/ppermute | solution.py:336
  76.0 42.9 %collective-permute-start.23 = (f32[256,512]{1,0:T(8,128)S(1)}, f32[256,512]{1,0:T(8,128)S(1)}, u32[]{:S(2)}, u32[]{:S(2)}) collective-permute-start(f32[256,512]{1,0:T(8,128)S(1)} %sweep.2.w_ref.refs_2_), channel_id=1, source_target_pairs={{0,2},{1,3},{2,4},{3,5},{4,6},{5,7},{6,0},{7,1},{8,10},{9,11},{10,... | collective-permute-start | bytes 1572872 | tf_op jit(solution)/shard_map/ppermute | solution.py:344
  76.5 42.4 %collective-permute-start.15 = (f32[256,512]{1,0:T(8,128)S(1)}, f32[256,512]{1,0:T(8,128)S(1)}, u32[]{:S(2)}, u32[]{:S(2)}) collective-permute-start(f32[256,512]{1,0:T(8,128)S(1)} %sweep.2.w_ref.refs_2_), channel_id=1, source_target_pairs={{0,6},{1,7},{2,0},{3,1},{4,2},{5,3},{6,4},{7,5},{8,14},{9,15},{10,... | collective-permute-start | bytes 1572872 | tf_op jit(solution)/shard_map/ppermute | solution.py:344
  89.8 17.5 %collective-permute-start.18 = (f32[64,512]{1,0:T(8,128)S(1)}, f32[64,512]{1,0:T(8,128)S(1)}, u32[]{:S(2)}, u32[]{:S(2)}) collective-permute-start(f32[64,512]{1,0:T(8,128)S(1)} %get-tuple-element.57), channel_id=1, source_target_pairs={{0,2},{1,3},{2,4},{3,5},{4,6},{5,7},{6,0},{7,1},{8,10},{9,11},{10,... | collective-permute-start | bytes 393224 | tf_op jit(solution)/shard_map/ppermute | solution.py:340
  89.9 30.3 %collective-permute-start.13 = (f32[256,512]{1,0:T(8,128)S(1)}, f32[256,512]{1,0:T(8,128)S(1)}, u32[]{:S(2)}, u32[]{:S(2)}) collective-permute-start(f32[256,512]{1,0:T(8,128)S(1)} %sweep.2.w_ref.refs_2_), channel_id=1, source_target_pairs={{0,4},{1,5},{2,6},{3,7},{4,0},{5,1},{6,2},{7,3},{8,12},{9,13},{10,... | collective-permute-start | bytes 1572872 | tf_op jit(solution)/shard_map/ppermute | solution.py:344
  91.3 18.1 %collective-permute-start.19 = (f32[64,512]{1,0:T(8,128)S(1)}, f32[64,512]{1,0:T(8,128)S(1)}, u32[]{:S(2)}, u32[]{:S(2)}) collective-permute-start(f32[64,512]{1,0:T(8,128)S(1)} %get-tuple-element.58), channel_id=1, source_target_pairs={{0,6},{1,7},{2,0},{3,1},{4,2},{5,3},{6,4},{7,5},{8,14},{9,15},{10,... | collective-permute-start | bytes 393224 | tf_op jit(solution)/shard_map/ppermute | solution.py:340
  118.8 15.0 %collective-permute-start.24 = (f32[256,512]{1,0:T(8,128)S(1)}, f32[256,512]{1,0:T(8,128)S(1)}, u32[]{:S(2)}, u32[]{:S(2)}) collective-permute-start(f32[256,512]{1,0:T(8,128)S(1)} %collective-permute-done.23.refs_3_), channel_id=1, source_target_pairs={{0,1},{1,0},{2,3},{3,2},{4,5},{5,4},{6,7},{7,6},{8,9},{9,8},{10,11... | collective-permute-start | bytes 1572872 | tf_op jit(solution)/shard_map/ppermute | solution.py:336
  118.9 14.9 %collective-permute-start.22 = (f32[256,512]{1,0:T(8,128)S(1)}, f32[256,512]{1,0:T(8,128)S(1)}, u32[]{:S(2)}, u32[]{:S(2)}) collective-permute-start(f32[256,512]{1,0:T(8,128)S(1)} %collective-permute-done.15.refs_2_), channel_id=1, source_target_pairs={{0,1},{1,0},{2,3},{3,2},{4,5},{5,4},{6,7},{7,6},{8,9},{9,8},{10,11... | collective-permute-start | bytes 1572872 | tf_op jit(solution)/shard_map/ppermute | solution.py:336
  119.4 6.7 %collective-permute-start.25 = (f32[64,512]{1,0:T(8,128)S(1)}, f32[64,512]{1,0:T(8,128)S(1)}, u32[]{:S(2)}, u32[]{:S(2)}) collective-permute-start(f32[64,512]{1,0:T(8,128)S(1)} %add.12.refs_0_), channel_id=1, source_target_pairs={{0,24},{8,16},{16,8},{24,0},{32,56},{40,48},{48,40},{56,32},{64,88... | collective-permute-start | bytes 393224 | tf_op jit(solution)/shard_map/ppermute | solution.py:403
  120.1 16.2 %collective-permute-start.14 = (f32[256,512]{1,0:T(8,128)S(1)}, f32[256,512]{1,0:T(8,128)S(1)}, u32[]{:S(2)}, u32[]{:S(2)}) collective-permute-start(f32[256,512]{1,0:T(8,128)S(1)} %collective-permute-done.13.refs_2_), channel_id=1, source_target_pairs={{0,1},{1,0},{2,3},{3,2},{4,5},{5,4},{6,7},{7,6},{8,9},{9,8},{10,11... | collective-permute-start | bytes 1572872 | tf_op jit(solution)/shard_map/ppermute | solution.py:336
  139.8 44.6 %all-to-all-start.1 = ((f32[16,64,512]{2,1,0:T(8,128)}), f32[16,64,512]{2,1,0:T(8,128)S(1)}, u32[]{:S(2)}, u32[]{:S(2)}) async-start(f32[16,64,512]{2,1,0:T(8,128)} %bitcast.6), calls=%async_computation.1 | async-start | bytes 4194304 | tf_op jit(solution)/shard_map/all_to_all | solution.py:447
  146.9 26.6 %collective-permute-start.27 = (f32[64,512]{1,0:T(8,128)S(1)}, f32[64,512]{1,0:T(8,128)S(1)}, u32[]{:S(2)}, u32[]{:S(2)}) collective-permute-start(f32[64,512]{1,0:T(8,128)S(1)} %add.14.refs_0_), channel_id=1, source_target_pairs={{0,96},{8,104},{16,112},{24,120},{32,64},{40,72},{48,80},{56,88},{... | collective-permute-start | bytes 393224 | tf_op jit(solution)/shard_map/ppermute | solution.py:403
  173.6 8.7 %collective-permute-start.29 = (f32[64,512]{1,0:T(8,128)S(1)}, f32[64,512]{1,0:T(8,128)S(1)}, u32[]{:S(2)}, u32[]{:S(2)}) collective-permute-start(f32[64,512]{1,0:T(8,128)S(1)} %add.15.refs_0_), channel_id=1, source_target_pairs={{0,2},{1,3},{2,4},{3,5},{4,6},{5,7},{6,0},{7,1},{8,10},{9,11},{10,... | collective-permute-start | bytes 393224 | tf_op jit(solution)/shard_map/ppermute | solution.py:344
  199.5 13.1 %collective-permute-start.38 = (f32[128,512]{1,0:T(8,128)S(1)}, f32[128,512]{1,0:T(8,128)S(1)}, u32[]{:S(2)}, u32[]{:S(2)}) collective-permute-start(f32[128,512]{1,0:T(8,128)S(1)} %get-tuple-element.76.refs_0_), channel_id=1, source_target_pairs={{0,24},{8,0},{16,8},{24,16},{32,56},{40,32},{48,40},{56,48},{64,88... | collective-permute-start | bytes 786440 | tf_op jit(solution)/shard_map/ppermute | solution.py:344
  199.7 15.5 %collective-permute-start.39 = (f32[128,512]{1,0:T(8,128)S(1)}, f32[128,512]{1,0:T(8,128)S(1)}, u32[]{:S(2)}, u32[]{:S(2)}) collective-permute-start(f32[128,512]{1,0:T(8,128)S(1)} %get-tuple-element.76.refs_0_), channel_id=1, source_target_pairs={{0,8},{8,16},{16,24},{24,0},{32,40},{40,48},{48,56},{56,32},{64,72... | collective-permute-start | bytes 786440 | tf_op jit(solution)/shard_map/ppermute | solution.py:344
  202.9 12.3 %collective-permute-start.40 = (f32[128,512]{1,0:T(8,128)S(1)}, f32[128,512]{1,0:T(8,128)S(1)}, u32[]{:S(2)}, u32[]{:S(2)}) collective-permute-start(f32[128,512]{1,0:T(8,128)S(1)} %get-tuple-element.76.refs_0_), channel_id=1, source_target_pairs={{0,16},{8,24},{16,0},{24,8},{32,48},{40,56},{48,32},{56,40},{64,80... | collective-permute-start | bytes 786440 | tf_op jit(solution)/shard_map/ppermute | solution.py:344
  202.9 12.3 %collective-permute-start.41 = (f32[128,512]{1,0:T(8,128)S(1)}, f32[128,512]{1,0:T(8,128)S(1)}, u32[]{:S(2)}, u32[]{:S(2)}) collective-permute-start(f32[128,512]{1,0:T(8,128)S(1)} %get-tuple-element.77.refs_4_), channel_id=1, source_target_pairs={{0,96},{8,104},{16,112},{24,120},{32,0},{40,8},{48,16},{56,24},{64... | collective-permute-start | bytes 786440 | tf_op jit(solution)/shard_map/ppermute | solution.py:344
  204.5 10.6 %collective-permute-start.42 = (f32[128,512]{1,0:T(8,128)S(1)}, f32[128,512]{1,0:T(8,128)S(1)}, u32[]{:S(2)}, u32[]{:S(2)}) collective-permute-start(f32[128,512]{1,0:T(8,128)S(1)} %get-tuple-element.77.refs_4_), channel_id=1, source_target_pairs={{0,32},{8,40},{16,48},{24,56},{32,64},{40,72},{48,80},{56,88},{64,... | collective-permute-start | bytes 786440 | tf_op jit(solution)/shard_map/ppermute | solution.py:344
  212.6 7.9 %collective-permute-start.43 = (f32[128,512]{1,0:T(8,128)S(1)}, f32[128,512]{1,0:T(8,128)S(1)}, u32[]{:S(2)}, u32[]{:S(2)}) collective-permute-start(f32[128,512]{1,0:T(8,128)S(1)} %get-tuple-element.77.refs_4_), channel_id=1, source_target_pairs={{0,64},{8,72},{16,80},{24,88},{32,96},{40,104},{48,112},{56,120},{... | collective-permute-start | bytes 786440 | tf_op jit(solution)/shard_map/ppermute | solution.py:344
  (26 other events, 116.6 us)

commit v2 on v1

--- a/solution.py
+++ b/solution.py
@@ -114,7 +114,7 @@
         out_shape=[sds(16, 1024, 128, dtype=bf16)] * 2,
         in_specs=[pl.BlockSpec((128, 1024), lambda i: (i, 0))],
         out_specs=[spec, spec],
-        compiler_params=params(44),
+        compiler_params=params(6),
         cost_estimate=cost(1 << 24, 16 << 20),
         name="flip",
     )(spectra)
@@ -196,14 +196,15 @@
 
 
 def gram_w_kernel(w_ref, mine_ref, theirs_ref, tmp):
-    _, _, x, c = place()
+    z, y, _, c = place()
     w = w_ref[...]
     tmp[...] = dot3(*split(w.T), *split(w))
     for k in range(4):
-        row = 128 * ((x + REL[k]) % 4)
-        rows = slice(64 * k, 64 * (k + 1))
-        mine_ref[rows, :] = tmp[pl.ds(pl.multiple_of(row + 64 * c, 64), 64), :]
-        theirs_ref[rows, :] = tmp[pl.ds(pl.multiple_of(row + 64 * (1 - c), 64), 64), :]
+        for m in range(4):
+            s = 4 * ((z + REL[k]) % 4) + (y + REL[m]) % 4
+            at = 64 * k + 16 * m
+            mine_ref[at : at + 16, :] = tmp[pl.ds(pl.multiple_of(32 * s + 16 * c, 16), 16), :]
+            theirs_ref[at : at + 16, :] = tmp[pl.ds(pl.multiple_of(32 * s + 16 * (1 - c), 16), 16), :]
 
 
 def gram_w(w):
@@ -223,16 +224,15 @@
     outs, (g, gh, gl, fh, fl, ff, pp, sem) = refs[:-8], refs[-8:]
     z, y, x, c = place()
     n = ff.shape[0]
-    first = n * (2 * x + c if axis == "col" else 4 * z + y)
-    begin = pltpu.make_async_copy(start.at[pl.ds(pl.multiple_of(first, n), n), :], ff, sem)
+    if axis == "col":
+        rows = start
+    else:
+        rows = start.at[pl.ds(pl.multiple_of(n * (4 * z + y), n), n), :]
+    begin = pltpu.make_async_copy(rows, ff, sem)
     begin.start()
     for t, piece in enumerate((mine, theirs)):
         cc = c if t == 0 else 1 - c
         for j in range(4):
-            if axis == "samp":
-                row = 128 * ((x + REL[j]) % 4) + 64 * cc
-                g[pl.ds(pl.multiple_of(row, 64), 64), :] = piece[64 * j : 64 * j + 64, :]
-                continue
             for i in range(4):
                 row = 32 * (4 * ((z + REL[i]) % 4) + (y + REL[j]) % 4) + 16 * cc
                 g[pl.ds(pl.multiple_of(row, 16), 16), :] = piece[64 * j + 16 * i : 64 * j + 16 * i + 16, :]
@@ -268,7 +268,7 @@
     return pl.pallas_call(
         functools.partial(sweep_kernel, axis),
         out_shape=[sds(rows // nout, 512)] * nout,
-        in_specs=[VM, HBM, VM, VM],
+        in_specs=[VM, VM if axis == "col" else HBM, VM, VM],
         out_specs=[VM] * nout,
         scratch_shapes=[
             pltpu.VMEM((512, 512), f32),
@@ -280,10 +280,31 @@
             pltpu.VMEM((rows, 512), f32),
             pltpu.SemaphoreType.DMA,
         ],
-        compiler_params=params(50),
+        compiler_params=params(12 if axis == "col" else 50),
         cost_estimate=cost(72 * rows * 512 * 512, 4 << 20),
         name="sweep",
     )(product, start, *pieces)
+
+
+def take_kernel(w_ref, out_ref, sem):
+    _, _, x, c = place()
+    rows = w_ref.at[pl.ds(pl.multiple_of(256 * (2 * x + c), 256), 256), :]
+    cp = pltpu.make_async_copy(rows, out_ref, sem)
+    cp.start()
+    cp.wait()
+
+
+def take(w_start):
+    return pl.pallas_call(
+        take_kernel,
+        out_shape=sds(256, 512),
+        in_specs=[HBM],
+        out_specs=VM,
+        scratch_shapes=[pltpu.SemaphoreType.DMA],
+        compiler_params=params(57),
+        cost_estimate=cost(0, 1 << 20),
+        name="take",
+    )(w_start)
 
 
 def lay_h_kernel(*refs):
@@ -328,8 +349,6 @@
 XGROUPS = [[0, 2, 4, 6], [1, 3, 5, 7]]
 CORE, X = moves("col", "core"), moves("col", "x")
 Y, Z = moves("samp", "y"), moves("samp", "z")
-Y_PAIRS = [[(i, i ^ k) for i in range(16)] for k in (1, 3)]
-Z_PAIRS = [[(i, i ^ k) for i in range(16)] for k in (4, 12)]
 
 
 def swap(a):
@@ -399,53 +418,52 @@
     return [pieces[0]] + [send(pieces[k], axis, table, REL[k]) for k in (1, 2, 3)]
 
 
-def pair_sum(a, pairs):
-    return add([a, lax.ppermute(a, "samp", pairs)])
-
-
-def over_all(strip):
-    strip = add([strip] + fetch(strip, "col", X))
+def spread(strip):
     strip = join([strip] + fetch(strip, "samp", Z))
-    strip = join([strip] + fetch(strip, "samp", Y))
-    return strip, swap(strip)
+    return join([strip] + fetch(strip, "samp", Y))
 
 
 def shards(spectra, w_start, h_start):
     g_mine, g_theirs = gram_h(h_start)
-    a1, hh, hl = prod(spectra, after(h_start, g_mine), (0, 1), True)
+    strip = add([g_mine, swap(g_theirs)])
+
+    a1, hh, hl = prod(spectra, after(h_start, strip), (0, 1), True)
     r1 = swap(a1)
     h = (hh, hl)
     a2 = prod(spectra, h, (2, 3), True)
     r2 = swap(a2)
-    g_theirs = swap(g_theirs)
     low = prod(spectra, h, (0, 1), False, after(r1, a2))
-    both = prod(spectra, h, (2, 3), False, r2, low)
+    strip = add([strip] + fetch(strip, "col", X))
+    both = prod(spectra, h, (2, 3), False, r2, after(low, strip))
     product = lax.all_to_all(both, "col", 0, 0, axis_index_groups=XGROUPS, tiled=True)
 
-    pieces_h = over_all(add([after(g_mine, both), g_theirs]))
-
-    (w,) = sweep(product, w_start, "col", 256, pieces_h, 1)
+    part = spread(after(strip, both))
+    w0 = take(after(w_start, part))
+    (w,) = sweep(product, w0, "col", 256, (part, swap(part)), 1)
 
     ws = swap(w)
     near_p, near_m, far = fetch(w, "col", X)
 
     g_mine, g_theirs = gram_w(w)
     flipped = flip(after(spectra, g_theirs))
-    slices = deal(add([g_mine, after(swap(g_theirs), *flipped)], 4), "col", X)
+    strips = add([g_mine, after(swap(g_theirs), *flipped)], 4)
+    strips = deal(strips, "samp", Z)
     carry = back(flipped, (w, ws), ((0, False), (0, True)))
-    part = add([after(slices[0], carry[0])] + slices[1:])
-    part = pair_sum(part, Y_PAIRS[0])
-    sib_p, sib_m = swap(after(near_p, part)), swap(after(near_m, part))
-    part = pair_sum(part, Y_PAIRS[1])
-    carry = back(flipped, (near_p, near_m), ((1, False), (3, False)), (after(carry[0], part), carry[1]))
-    part = pair_sum(after(part, carry[0]), Z_PAIRS[0])
+    strips = add([after(strips[0], carry[0])] + strips[1:], 4)
+    strips = deal(strips, "samp", Y)
+    sib_p, sib_m = swap(after(near_p, *strips)), swap(after(near_m, *strips))
+    strip = add(strips)
+    carry = back(flipped, (near_p, near_m), ((1, False), (3, False)), (after(carry[0], strip), carry[1]))
+    part = join([after(strip, carry[0])] + fetch(strip, "samp", Z))
     carry = back(flipped, (sib_p, sib_m), ((1, True), (3, True)), (after(carry[0], part), carry[1]))
-    part = pair_sum(after(part, carry[0]), Z_PAIRS[1])
-    sib_f = swap(far)
+    sib_f = swap(after(far, part))
+    part = join([after(part, carry[0])] + fetch(part, "samp", Y))
+    carry = (after(carry[0], part), carry[1])
     back_sum, w_out = back(flipped, (far, sib_f), ((2, False), (2, True)), carry, True)
 
     product = lax.all_to_all(back_sum, "samp", 0, 0, tiled=True)
-    part = join([after(part, back_sum)] + fetch(part, "col", X))
+    part = after(part, back_sum)
+    part = add([part] + fetch(part, "col", X))
     ha, hb = sweep(product, h_start, "samp", 64, (part, swap(part)), 2)
 
     row_a, row_b = join([ha] + fetch(ha, "samp", Z) + [hb] + fetch(hb, "samp", Y), 2)

time: 223 us -> 187 us (0.84)
  waiting for transfers between devices: 120 us -> 79.1 us
  starting transfers between devices: 55.6 us -> 65.9 us
  Pallas kernels: 39.1 us -> 33.3 us
    ppermute x4 -> x0, waiting for transfers between devices: 39.1 us -> none  [pair_sum(): return add([a, lax.ppermute(a, 'samp', pairs)])]
    ppermute x3 -> x6, starting transfers between devices: 1.85 us -> 9.24 us  [send(): return lax.ppermute(a, axis, table[r])]
    ppermute x27 -> x33, starting transfers between devices: 35.5 us -> 42.9 us  [fetch(): return [lax.ppermute(a, axis, table[(4 - r) % 4]) for r in REL[1:]]]
    pallas_call x1, Pallas kernels: 10.5 us -> 3.33 us  [flip(): pl.pallas_call(flip_kernel, grid=(16,), out_shape=[sds(16, 1024, 128, dty...]
    ppermute x3 -> x6, waiting for transfers between devices: 18.5 us -> 11.8 us  [send(): return lax.ppermute(a, axis, table[r])]
    ppermute x4 -> x0, starting transfers between devices: 4.51 us -> none  [pair_sum(): return add([a, lax.ppermute(a, 'samp', pairs)])]
    all_to_all x1, waiting for transfers between devices: 0.01 us -> 4.15 us  [shards(): lax.all_to_all(both, 'col', 0, 0, axis_index_groups=XGROUPS, tiled=True)]
    ppermute x27 -> x33, waiting for transfers between devices: 56.8 us -> 59.9 us  [fetch(): return [lax.ppermute(a, axis, table[(4 - r) % 4]) for r in REL[1:]]]
  transfers between devices with their start and end apart: 46 -> 51, of which waited for: 27 -> 28; matrix products, arithmetic and copies ran while one was open for 0% -> 0% of each run, Pallas kernels for 10% -> 9%
where the time goes in v2:
time: 187 us
  waiting for transfers between devices  79.1 us (42%)
  starting transfers between devices  65.9 us (35%)
  Pallas kernels  33.3 us (18%)
  local copies, waits for them, and re-layouts  7.48 us (4%)
    ppermute x33, waiting for transfers between devices, fetch(): return [lax.ppermute(a, axis, table[(4 - r) % 4]) for r in REL[1:]]  59.9 us
    ppermute x33, starting transfers between devices, fetch(): return [lax.ppermute(a, axis, table[(4 - r) % 4]) for r in REL[1:]]  42.9 us
    ppermute x6, waiting for transfers between devices, send(): return lax.ppermute(a, axis, table[r])  11.8 us
    ppermute x6, starting transfers between devices, send(): return lax.ppermute(a, axis, table[r])  9.24 us
    pallas_call x4, Pallas kernels, back(): pl.pallas_call(functools.partial(back_kernel, tuple(chunks), bool(carry))...  9.05 us
    pallas_call x4, Pallas kernels, prod(): pl.pallas_call(functools.partial(prod_kernel, chunks, sibling, first, rec...  8.15 us
    unnamed x14, local copies, waits for them, and re-layouts  7.48 us
    all_to_all x1, starting transfers between devices, shards(): product = lax.all_to_all(back_sum, 'samp', 0, 0, tiled=True)  7.19 us
  transfers between devices with their start and end apart: 51, of which 28 were waited for; matrix products, arithmetic and copies ran while one was open for 0% of the time, Pallas kernels for 9%

profile of v2, /device:TPU:24, one launch (start us, length us, event | category | flops | bytes accessed | tf_op | source)
XLA Modules:
  0.0 186.7 jit_solution(6589005414249225065)
XLA Ops:
  4.8 3.4 %copy-done = f32[2048,1024]{1,0:T(8,128)S(1)} copy-done((f32[2048,1024]{1,0:T(8,128)S(1)}, f32[2048,1024]{1,0:T(8,128)}, u32[]{:S(2)}) %copy-start) | copy-done | bytes 8388632
  12.5 2.8 %collective-permute-start.3 = (f32[16,512]{1,0:T(8,128)S(1)}, f32[16,512]{1,0:T(8,128)S(1)}, u32[]{:S(2)}, u32[]{:S(2)}) collective-permute-start(f32[16,512]{1,0:T(8,128)S(1)} %add.6.refs_0_), channel_id=1, source_target_pairs={{0,6},{1,7},{2,0},{3,1},{4,2},{5,3},{6,4},{7,5},{8,14},{9,15},{10,... | collective-permute-start | bytes 98312 | tf_op jit(solution)/shard_map/ppermute | solution.py:363
  17.5 2.8 %collective-permute-done.4.refs_2_ = f32[16,512]{1,0:T(8,128)S(1)} collective-permute-done((f32[16,512]{1,0:T(8,128)S(1)}, f32[16,512]{1,0:T(8,128)S(1)}, u32[]{:S(2)}, u32[]{:S(2)}) %collective-permute-start.4) | collective-permute-done | bytes 32800 | tf_op jit(solution)/shard_map/ppermute | solution.py:363
  22.5 2.8 %prod.7 = f32[1024,512]{1,0:T(8,128)} custom-call(f32[2048,1024]{1,0:T(8,128)S(1)} %copy-done, bf16[1024,512]{1,0:T(8,128)(2,1)S(1)} %get-tuple-element.51.refs_1_, bf16[1024,512]{1,0:T(8,128)(2,1)S(1)} %get-tuple-element.52.refs_2_, f32[512,512]{1,0:T(8,128)S(1)} %collective-permute-done.1.refs_3_, f32[512,512]{1,0:T(8,128)S(1)} %prod.6.refs_4_), custom_call_target="tpu_custom_call" | custom-call | flops 1610612736 | bytes 6291456 | tf_op jit(solution)/shard_map/prod/pallas_call | solution.py:89
  25.3 4.5 %all-to-all-start = ((f32[4,256,512]{2,1,0:T(8,128)}), f32[4,256,512]{2,1,0:T(8,128)S(1)}, u32[]{:S(2)}, u32[]{:S(2)}) async-start(f32[4,256,512]{2,1,0:T(8,128)} %bitcast), calls=%async_computation | async-start | bytes 4194304 | tf_op jit(solution)/shard_map/all_to_all | solution.py:438
  29.8 4.0 %collective-permute-start.6 = (f32[16,512]{1,0:T(8,128)S(1)}, f32[16,512]{1,0:T(8,128)S(1)}, u32[]{:S(2)}, u32[]{:S(2)}) collective-permute-start(f32[16,512]{1,0:T(8,128)S(1)} %add.7.refs_0_), channel_id=1, source_target_pairs={{0,96},{8,104},{16,112},{24,120},{32,0},{40,8},{48,16},{56,24},{64... | collective-permute-start | bytes 98312 | tf_op jit(solution)/shard_map/ppermute | solution.py:363
  35.7 3.3 %collective-permute-done.7.refs_2_ = f32[16,512]{1,0:T(8,128)S(1)} collective-permute-done((f32[16,512]{1,0:T(8,128)S(1)}, f32[16,512]{1,0:T(8,128)S(1)}, u32[]{:S(2)}, u32[]{:S(2)}) %collective-permute-start.7) | collective-permute-done | bytes 32800 | tf_op jit(solution)/shard_map/ppermute | solution.py:363
  39.6 2.6 %collective-permute-start.11 = (f32[64,512]{1,0:T(8,128)S(1)}, f32[64,512]{1,0:T(8,128)S(1)}, u32[]{:S(2)}, u32[]{:S(2)}) collective-permute-start(f32[64,512]{1,0:T(8,128)S(1)} %join.5.refs_0_), channel_id=1, source_target_pairs={{0,16},{8,24},{16,0},{24,8},{32,48},{40,56},{48,32},{56,40},{64,80... | collective-permute-start | bytes 393224 | tf_op jit(solution)/shard_map/ppermute | solution.py:363
  50.6 4.1 %all-to-all-done = f32[4,256,512]{2,1,0:T(8,128)S(1)} async-done(((f32[4,256,512]{2,1,0:T(8,128)}), f32[4,256,512]{2,1,0:T(8,128)S(1)}, u32[]{:S(2)}, u32[]{:S(2)}) %all-to-all-start) | async-done | bytes 2097184 | tf_op jit(solution)/shard_map/all_to_all | solution.py:438
  55.9 4.1 %sweep.2.w_ref.refs_2_ = f32[256,512]{1,0:T(8,128)S(1)} custom-call(f32[1024,512]{1,0:T(8,128)S(1)} %bitcast.7, f32[256,512]{1,0:T(8,128)S(1)} %copy-done.4, f32[256,512]{1,0:T(8,128)S(1)} %join.6.mine, f32[256,512]{1,0:T(8,128)S(1)} %collective-permute-done.12.theirs), custom_call_target="tpu_custom_call" | custom-call | flops 4831838208 | bytes 4194304 | tf_op jit(solution)/shard_map/sweep/pallas_call | solution.py:268
  61.8 2.7 %collective-permute-start.22 = (f32[256,512]{1,0:T(8,128)S(1)}, f32[256,512]{1,0:T(8,128)S(1)}, u32[]{:S(2)}, u32[]{:S(2)}) collective-permute-start(f32[256,512]{1,0:T(8,128)S(1)} %sweep.2.w_ref.refs_2_), channel_id=1, source_target_pairs={{0,6},{1,7},{2,0},{3,1},{4,2},{5,3},{6,4},{7,5},{8,14},{9,15},{10,... | collective-permute-start | bytes 1572872 | tf_op jit(solution)/shard_map/ppermute | solution.py:363
  64.5 3.3 %flip.1 = (bf16[16,1024,128]{2,1,0:T(8,128)(2,1)S(1)}, bf16[16,1024,128]{2,1,0:T(8,128)(2,1)S(1)}) custom-call(f32[2048,1024]{1,0:T(8,128)S(1)} %bitcast.5), custom_call_target="tpu_custom_call" | custom-call | flops 16777216 | bytes 16777216 | tf_op jit(solution)/shard_map/flip/pallas_call | solution.py:111
  72.2 3.0 %collective-permute-done.16.refs_1_ = f32[64,512]{1,0:T(8,128)S(1)} collective-permute-done((f32[64,512]{1,0:T(8,128)S(1)}, f32[64,512]{1,0:T(8,128)S(1)}, u32[]{:S(2)}, u32[]{:S(2)}) %collective-permute-start.16) | collective-permute-done | bytes 131104 | tf_op jit(solution)/shard_map/ppermute | solution.py:359
  79.0 2.7 %collective-permute-done.18.refs_3_ = f32[64,512]{1,0:T(8,128)S(1)} collective-permute-done((f32[64,512]{1,0:T(8,128)S(1)}, f32[64,512]{1,0:T(8,128)S(1)}, u32[]{:S(2)}, u32[]{:S(2)}) %collective-permute-start.18) | collective-permute-done | bytes 131104 | tf_op jit(solution)/shard_map/ppermute | solution.py:359
  87.5 3.6 %collective-permute-done.21.refs_3_ = f32[16,512]{1,0:T(8,128)S(1)} collective-permute-done((f32[16,512]{1,0:T(8,128)S(1)}, f32[16,512]{1,0:T(8,128)S(1)}, u32[]{:S(2)}, u32[]{:S(2)}) %collective-permute-start.21) | collective-permute-done | bytes 32800 | tf_op jit(solution)/shard_map/ppermute | solution.py:359
  112.4 7.2 %all-to-all-start.1 = ((f32[16,64,512]{2,1,0:T(8,128)}), f32[16,64,512]{2,1,0:T(8,128)S(1)}, u32[]{:S(2)}, u32[]{:S(2)}) async-start(f32[16,64,512]{2,1,0:T(8,128)} %bitcast.8), calls=%async_computation.1 | async-start | bytes 4194304 | tf_op jit(solution)/shard_map/all_to_all | solution.py:464
  123.0 11.5 %collective-permute-done.33.refs_1_ = f32[256,512]{1,0:T(8,128)S(1)} collective-permute-done((f32[256,512]{1,0:T(8,128)S(1)}, f32[256,512]{1,0:T(8,128)S(1)}, u32[]{:S(2)}, u32[]{:S(2)}) %collective-permute-start.33) | collective-permute-done | bytes 524320 | tf_op jit(solution)/shard_map/ppermute | solution.py:363
  134.5 10.5 %collective-permute-done.34.refs_2_ = f32[256,512]{1,0:T(8,128)S(1)} collective-permute-done((f32[256,512]{1,0:T(8,128)S(1)}, f32[256,512]{1,0:T(8,128)S(1)}, u32[]{:S(2)}, u32[]{:S(2)}) %collective-permute-start.34) | collective-permute-done | bytes 524320 | tf_op jit(solution)/shard_map/ppermute | solution.py:363
  147.1 3.0 %sweep.3 = (f32[32,512]{1,0:T(8,128)S(1)}, f32[32,512]{1,0:T(8,128)S(1)}) custom-call(f32[1024,512]{1,0:T(8,128)S(1)} %bitcast.6, f32[1024,512]{1,0:T(8,128)} %start.1, f32[256,512]{1,0:T(8,128)S(1)} %add.11.mine, f32[256,512]{1,0:T(8,128)S(1)} %collective-permute-done.36.theirs), custom_call_target="tpu_custom_call" | custom-call | flops 1207959552 | bytes 4194304 | tf_op jit(solution)/shard_map/sweep/pallas_call | solution.py:268
  150.1 2.7 %collective-permute-start.37 = (f32[32,512]{1,0:T(8,128)S(1)}, f32[32,512]{1,0:T(8,128)S(1)}, u32[]{:S(2)}, u32[]{:S(2)}) collective-permute-start(f32[32,512]{1,0:T(8,128)S(1)} %get-tuple-element.90.refs_0_), channel_id=1, source_target_pairs={{0,96},{8,104},{16,112},{24,120},{32,0},{40,8},{48,16},{56,24},{64... | collective-permute-start | bytes 196616 | tf_op jit(solution)/shard_map/ppermute | solution.py:363
  160.6 3.5 %collective-permute-done.42.refs_7_ = f32[32,512]{1,0:T(8,128)S(1)} collective-permute-done((f32[32,512]{1,0:T(8,128)S(1)}, f32[32,512]{1,0:T(8,128)S(1)}, u32[]{:S(2)}, u32[]{:S(2)}) %collective-permute-start.42) | collective-permute-done | bytes 65568 | tf_op jit(solution)/shard_map/ppermute | solution.py:363
  164.3 3.2 %collective-permute-start.44 = (f32[128,512]{1,0:T(8,128)S(1)}, f32[128,512]{1,0:T(8,128)S(1)}, u32[]{:S(2)}, u32[]{:S(2)}) collective-permute-start(f32[128,512]{1,0:T(8,128)S(1)} %get-tuple-element.92.refs_0_), channel_id=1, source_target_pairs={{0,8},{8,16},{16,24},{24,0},{32,40},{40,48},{48,56},{56,32},{64,72... | collective-permute-start | bytes 786440 | tf_op jit(solution)/shard_map/ppermute | solution.py:363
  169.5 7.7 %collective-permute-done.43.refs_1_ = f32[128,512]{1,0:T(8,128)S(1)} collective-permute-done((f32[128,512]{1,0:T(8,128)S(1)}, f32[128,512]{1,0:T(8,128)S(1)}, u32[]{:S(2)}, u32[]{:S(2)}) %collective-permute-start.43) | collective-permute-done | bytes 262176 | tf_op jit(solution)/shard_map/ppermute | solution.py:363
  178.7 6.4 %collective-permute-done.48.refs_7_ = f32[128,512]{1,0:T(8,128)S(1)} collective-permute-done((f32[128,512]{1,0:T(8,128)S(1)}, f32[128,512]{1,0:T(8,128)S(1)}, u32[]{:S(2)}, u32[]{:S(2)}) %collective-permute-start.48) | collective-permute-done | bytes 262176 | tf_op jit(solution)/shard_map/ppermute | solution.py:363
  (119 shorter events, 80.2 us)
Async XLA Ops:
  10.0 10.7 %collective-permute-start.2 = (f32[512,512]{1,0:T(8,128)S(1)}, f32[512,512]{1,0:T(8,128)S(1)}, u32[]{:S(2)}, u32[]{:S(2)}) collective-permute-start(f32[512,512]{1,0:T(8,128)S(1)} %get-tuple-element.53), channel_id=1, source_target_pairs={{0,1},{1,0},{2,3},{3,2},{4,5},{5,4},{6,7},{7,6},{8,9},{9,8},{10,11... | collective-permute-start | bytes 3145736 | tf_op jit(solution)/shard_map/ppermute | solution.py:355
  12.0 10.5 %collective-permute-start.1 = (f32[512,512]{1,0:T(8,128)S(1)}, f32[512,512]{1,0:T(8,128)S(1)}, u32[]{:S(2)}, u32[]{:S(2)}) collective-permute-start(f32[512,512]{1,0:T(8,128)S(1)} %prod.5), channel_id=1, source_target_pairs={{0,1},{1,0},{2,3},{3,2},{4,5},{5,4},{6,7},{7,6},{8,9},{9,8},{10,11... | collective-permute-start | bytes 3145736 | tf_op jit(solution)/shard_map/ppermute | solution.py:355
  25.3 29.4 %all-to-all-start = ((f32[4,256,512]{2,1,0:T(8,128)}), f32[4,256,512]{2,1,0:T(8,128)S(1)}, u32[]{:S(2)}, u32[]{:S(2)}) async-start(f32[4,256,512]{2,1,0:T(8,128)} %bitcast), calls=%async_computation | async-start | bytes 4194304 | tf_op jit(solution)/shard_map/all_to_all | solution.py:438
  60.7 7.2 %collective-permute-start.14 = (f32[256,512]{1,0:T(8,128)S(1)}, f32[256,512]{1,0:T(8,128)S(1)}, u32[]{:S(2)}, u32[]{:S(2)}) collective-permute-start(f32[256,512]{1,0:T(8,128)S(1)} %get-tuple-element.58), channel_id=1, source_target_pairs={{0,1},{1,0},{2,3},{3,2},{4,5},{5,4},{6,7},{7,6},{8,9},{9,8},{10,11... | collective-permute-start | bytes 1572872 | tf_op jit(solution)/shard_map/ppermute | solution.py:355
  60.8 9.2 %collective-permute-start.15 = (f32[256,512]{1,0:T(8,128)S(1)}, f32[256,512]{1,0:T(8,128)S(1)}, u32[]{:S(2)}, u32[]{:S(2)}) collective-permute-start(f32[256,512]{1,0:T(8,128)S(1)} %sweep.2.w_ref.refs_2_), channel_id=1, source_target_pairs={{0,1},{1,0},{2,3},{3,2},{4,5},{5,4},{6,7},{7,6},{8,9},{9,8},{10,11... | collective-permute-start | bytes 1572872 | tf_op jit(solution)/shard_map/ppermute | solution.py:355
  61.3 32.0 %collective-permute-start.23 = (f32[256,512]{1,0:T(8,128)S(1)}, f32[256,512]{1,0:T(8,128)S(1)}, u32[]{:S(2)}, u32[]{:S(2)}) collective-permute-start(f32[256,512]{1,0:T(8,128)S(1)} %sweep.2.w_ref.refs_2_), channel_id=1, source_target_pairs={{0,2},{1,3},{2,4},{3,5},{4,6},{5,7},{6,0},{7,1},{8,10},{9,11},{10,... | collective-permute-start | bytes 1572872 | tf_op jit(solution)/shard_map/ppermute | solution.py:363
  61.8 33.2 %collective-permute-start.22 = (f32[256,512]{1,0:T(8,128)S(1)}, f32[256,512]{1,0:T(8,128)S(1)}, u32[]{:S(2)}, u32[]{:S(2)}) collective-permute-start(f32[256,512]{1,0:T(8,128)S(1)} %sweep.2.w_ref.refs_2_), channel_id=1, source_target_pairs={{0,6},{1,7},{2,0},{3,1},{4,2},{5,3},{6,4},{7,5},{8,14},{9,15},{10,... | collective-permute-start | bytes 1572872 | tf_op jit(solution)/shard_map/ppermute | solution.py:363
  67.9 7.3 %collective-permute-start.16 = (f32[64,512]{1,0:T(8,128)S(1)}, f32[64,512]{1,0:T(8,128)S(1)}, u32[]{:S(2)}, u32[]{:S(2)}) collective-permute-start(f32[64,512]{1,0:T(8,128)S(1)} %get-tuple-element.67), channel_id=1, source_target_pairs={{0,32},{8,40},{16,48},{24,56},{32,64},{40,72},{48,80},{56,88},{64,... | collective-permute-start | bytes 393224 | tf_op jit(solution)/shard_map/ppermute | solution.py:359
  69.9 28.8 %collective-permute-start.13 = (f32[256,512]{1,0:T(8,128)S(1)}, f32[256,512]{1,0:T(8,128)S(1)}, u32[]{:S(2)}, u32[]{:S(2)}) collective-permute-start(f32[256,512]{1,0:T(8,128)S(1)} %sweep.2.w_ref.refs_2_), channel_id=1, source_target_pairs={{0,4},{1,5},{2,6},{3,7},{4,0},{5,1},{6,2},{7,3},{8,12},{9,13},{10,... | collective-permute-start | bytes 1572872 | tf_op jit(solution)/shard_map/ppermute | solution.py:363
  69.9 9.0 %collective-permute-start.17 = (f32[64,512]{1,0:T(8,128)S(1)}, f32[64,512]{1,0:T(8,128)S(1)}, u32[]{:S(2)}, u32[]{:S(2)}) collective-permute-start(f32[64,512]{1,0:T(8,128)S(1)} %get-tuple-element.68), channel_id=1, source_target_pairs={{0,96},{8,104},{16,112},{24,120},{32,0},{40,8},{48,16},{56,24},{64... | collective-permute-start | bytes 393224 | tf_op jit(solution)/shard_map/ppermute | solution.py:359
  95.0 7.1 %collective-permute-start.29 = (f32[256,512]{1,0:T(8,128)S(1)}, f32[256,512]{1,0:T(8,128)S(1)}, u32[]{:S(2)}, u32[]{:S(2)}) collective-permute-start(f32[256,512]{1,0:T(8,128)S(1)} %collective-permute-done.23.refs_3_), channel_id=1, source_target_pairs={{0,1},{1,0},{2,3},{3,2},{4,5},{5,4},{6,7},{7,6},{8,9},{9,8},{10,11... | collective-permute-start | bytes 1572872 | tf_op jit(solution)/shard_map/ppermute | solution.py:355
  98.7 10.2 %collective-permute-start.27 = (f32[256,512]{1,0:T(8,128)S(1)}, f32[256,512]{1,0:T(8,128)S(1)}, u32[]{:S(2)}, u32[]{:S(2)}) collective-permute-start(f32[256,512]{1,0:T(8,128)S(1)} %collective-permute-done.13.refs_2_), channel_id=1, source_target_pairs={{0,1},{1,0},{2,3},{3,2},{4,5},{5,4},{6,7},{7,6},{8,9},{9,8},{10,11... | collective-permute-start | bytes 1572872 | tf_op jit(solution)/shard_map/ppermute | solution.py:355
  99.6 8.4 %collective-permute-start.31 = (f32[64,512]{1,0:T(8,128)S(1)}, f32[64,512]{1,0:T(8,128)S(1)}, u32[]{:S(2)}, u32[]{:S(2)}) collective-permute-start(f32[64,512]{1,0:T(8,128)S(1)} %join.7.refs_0_), channel_id=1, source_target_pairs={{0,8},{8,16},{16,24},{24,0},{32,40},{40,48},{48,56},{56,32},{64,72... | collective-permute-start | bytes 393224 | tf_op jit(solution)/shard_map/ppermute | solution.py:363
  112.4 34.6 %all-to-all-start.1 = ((f32[16,64,512]{2,1,0:T(8,128)}), f32[16,64,512]{2,1,0:T(8,128)S(1)}, u32[]{:S(2)}, u32[]{:S(2)}) async-start(f32[16,64,512]{2,1,0:T(8,128)} %bitcast.8), calls=%async_computation.1 | async-start | bytes 4194304 | tf_op jit(solution)/shard_map/all_to_all | solution.py:464
  119.6 14.9 %collective-permute-start.33 = (f32[256,512]{1,0:T(8,128)S(1)}, f32[256,512]{1,0:T(8,128)S(1)}, u32[]{:S(2)}, u32[]{:S(2)}) collective-permute-start(f32[256,512]{1,0:T(8,128)S(1)} %join.8.refs_0_), channel_id=1, source_target_pairs={{0,6},{1,7},{2,0},{3,1},{4,2},{5,3},{6,4},{7,5},{8,14},{9,15},{10,... | collective-permute-start | bytes 1572872 | tf_op jit(solution)/shard_map/ppermute | solution.py:363
  119.9 25.0 %collective-permute-start.34 = (f32[256,512]{1,0:T(8,128)S(1)}, f32[256,512]{1,0:T(8,128)S(1)}, u32[]{:S(2)}, u32[]{:S(2)}) collective-permute-start(f32[256,512]{1,0:T(8,128)S(1)} %join.8.refs_0_), channel_id=1, source_target_pairs={{0,2},{1,3},{2,4},{3,5},{4,6},{5,7},{6,0},{7,1},{8,10},{9,11},{10,... | collective-permute-start | bytes 1572872 | tf_op jit(solution)/shard_map/ppermute | solution.py:363
  121.7 23.3 %collective-permute-start.35 = (f32[256,512]{1,0:T(8,128)S(1)}, f32[256,512]{1,0:T(8,128)S(1)}, u32[]{:S(2)}, u32[]{:S(2)}) collective-permute-start(f32[256,512]{1,0:T(8,128)S(1)} %join.8.refs_0_), channel_id=1, source_target_pairs={{0,4},{1,5},{2,6},{3,7},{4,0},{5,1},{6,2},{7,3},{8,12},{9,13},{10,... | collective-permute-start | bytes 1572872 | tf_op jit(solution)/shard_map/ppermute | solution.py:363
  150.1 8.3 %collective-permute-start.37 = (f32[32,512]{1,0:T(8,128)S(1)}, f32[32,512]{1,0:T(8,128)S(1)}, u32[]{:S(2)}, u32[]{:S(2)}) collective-permute-start(f32[32,512]{1,0:T(8,128)S(1)} %get-tuple-element.90.refs_0_), channel_id=1, source_target_pairs={{0,96},{8,104},{16,112},{24,120},{32,0},{40,8},{48,16},{56,24},{64... | collective-permute-start | bytes 196616 | tf_op jit(solution)/shard_map/ppermute | solution.py:363
  164.2 13.1 %collective-permute-start.43 = (f32[128,512]{1,0:T(8,128)S(1)}, f32[128,512]{1,0:T(8,128)S(1)}, u32[]{:S(2)}, u32[]{:S(2)}) collective-permute-start(f32[128,512]{1,0:T(8,128)S(1)} %get-tuple-element.92.refs_0_), channel_id=1, source_target_pairs={{0,24},{8,0},{16,8},{24,16},{32,56},{40,32},{48,40},{56,48},{64,88... | collective-permute-start | bytes 786440 | tf_op jit(solution)/shard_map/ppermute | solution.py:363
  164.3 14.4 %collective-permute-start.44 = (f32[128,512]{1,0:T(8,128)S(1)}, f32[128,512]{1,0:T(8,128)S(1)}, u32[]{:S(2)}, u32[]{:S(2)}) collective-permute-start(f32[128,512]{1,0:T(8,128)S(1)} %get-tuple-element.92.refs_0_), channel_id=1, source_target_pairs={{0,8},{8,16},{16,24},{24,0},{32,40},{40,48},{48,56},{56,32},{64,72... | collective-permute-start | bytes 786440 | tf_op jit(solution)/shard_map/ppermute | solution.py:363
  167.5 11.2 %collective-permute-start.45 = (f32[128,512]{1,0:T(8,128)S(1)}, f32[128,512]{1,0:T(8,128)S(1)}, u32[]{:S(2)}, u32[]{:S(2)}) collective-permute-start(f32[128,512]{1,0:T(8,128)S(1)} %get-tuple-element.92.refs_0_), channel_id=1, source_target_pairs={{0,16},{8,24},{16,0},{24,8},{32,48},{40,56},{48,32},{56,40},{64,80... | collective-permute-start | bytes 786440 | tf_op jit(solution)/shard_map/ppermute | solution.py:363
  167.5 11.2 %collective-permute-start.46 = (f32[128,512]{1,0:T(8,128)S(1)}, f32[128,512]{1,0:T(8,128)S(1)}, u32[]{:S(2)}, u32[]{:S(2)}) collective-permute-start(f32[128,512]{1,0:T(8,128)S(1)} %get-tuple-element.93.refs_4_), channel_id=1, source_target_pairs={{0,96},{8,104},{16,112},{24,120},{32,0},{40,8},{48,16},{56,24},{64... | collective-permute-start | bytes 786440 | tf_op jit(solution)/shard_map/ppermute | solution.py:363
  168.7 10.0 %collective-permute-start.47 = (f32[128,512]{1,0:T(8,128)S(1)}, f32[128,512]{1,0:T(8,128)S(1)}, u32[]{:S(2)}, u32[]{:S(2)}) collective-permute-start(f32[128,512]{1,0:T(8,128)S(1)} %get-tuple-element.93.refs_4_), channel_id=1, source_target_pairs={{0,32},{8,40},{16,48},{24,56},{32,64},{40,72},{48,80},{56,88},{64,... | collective-permute-start | bytes 786440 | tf_op jit(solution)/shard_map/ppermute | solution.py:363
  177.3 7.9 %collective-permute-start.48 = (f32[128,512]{1,0:T(8,128)S(1)}, f32[128,512]{1,0:T(8,128)S(1)}, u32[]{:S(2)}, u32[]{:S(2)}) collective-permute-start(f32[128,512]{1,0:T(8,128)S(1)} %get-tuple-element.93.refs_4_), channel_id=1, source_target_pairs={{0,64},{8,72},{16,80},{24,88},{32,96},{40,104},{48,112},{56,120},{... | collective-permute-start | bytes 786440 | tf_op jit(solution)/shard_map/ppermute | solution.py:363
  (34 other events, 169.4 us)

commit v3 on v2

--- a/solution.py
+++ b/solution.py
@@ -429,12 +429,12 @@
 
     a1, hh, hl = prod(spectra, after(h_start, strip), (0, 1), True)
     r1 = swap(a1)
-    h = (hh, hl)
+    strip = add([after(strip, a1)] + fetch(strip, "col", X))
+    h = (after(hh, strip), hl)
     a2 = prod(spectra, h, (2, 3), True)
     r2 = swap(a2)
     low = prod(spectra, h, (0, 1), False, after(r1, a2))
-    strip = add([strip] + fetch(strip, "col", X))
-    both = prod(spectra, h, (2, 3), False, r2, after(low, strip))
+    both = prod(spectra, h, (2, 3), False, r2, low)
     product = lax.all_to_all(both, "col", 0, 0, axis_index_groups=XGROUPS, tiled=True)
 
     part = spread(after(strip, both))
@@ -442,7 +442,7 @@
     (w,) = sweep(product, w0, "col", 256, (part, swap(part)), 1)
 
     ws = swap(w)
-    near_p, near_m, far = fetch(w, "col", X)
+    near_p, near_m = send(w, "col", X, 3), send(w, "col", X, 1)
 
     g_mine, g_theirs = gram_w(w)
     flipped = flip(after(spectra, g_theirs))
@@ -450,20 +450,22 @@
     strips = deal(strips, "samp", Z)
     carry = back(flipped, (w, ws), ((0, False), (0, True)))
     strips = add([after(strips[0], carry[0])] + strips[1:], 4)
+    near_p, near_m = after(near_p, *strips), after(near_m, *strips)
+    far = send(after(w, near_p, near_m), "col", X, 2)
+    sib_p, sib_m = swap(near_p), swap(near_m)
     strips = deal(strips, "samp", Y)
-    sib_p, sib_m = swap(after(near_p, *strips)), swap(after(near_m, *strips))
-    strip = add(strips)
-    carry = back(flipped, (near_p, near_m), ((1, False), (3, False)), (after(carry[0], strip), carry[1]))
+    carry = back(flipped, (near_p, near_m), ((1, False), (3, False)), (after(carry[0], *strips), carry[1]))
+    strip = add([after(strips[0], carry[0])] + strips[1:])
+    carry = back(flipped, (sib_p, sib_m), ((1, True), (3, True)), (after(carry[0], strip), carry[1]))
     part = join([after(strip, carry[0])] + fetch(strip, "samp", Z))
-    carry = back(flipped, (sib_p, sib_m), ((1, True), (3, True)), (after(carry[0], part), carry[1]))
     sib_f = swap(after(far, part))
-    part = join([after(part, carry[0])] + fetch(part, "samp", Y))
     carry = (after(carry[0], part), carry[1])
     back_sum, w_out = back(flipped, (far, sib_f), ((2, False), (2, True)), carry, True)
 
     product = lax.all_to_all(back_sum, "samp", 0, 0, tiled=True)
     part = after(part, back_sum)
     part = add([part] + fetch(part, "col", X))
+    part = join([part] + fetch(part, "samp", Y))
     ha, hb = sweep(product, h_start, "samp", 64, (part, swap(part)), 2)
 
     row_a, row_b = join([ha] + fetch(ha, "samp", Z) + [hb] + fetch(hb, "samp", Y), 2)

time: 187 us -> 186 us (level)
  waiting for transfers between devices: 79.1 us -> 74 us
  starting transfers between devices: 65.9 us -> 69 us
    ppermute x33 -> x30, waiting for transfers between devices: 59.9 us -> 53.1 us  [fetch(): return [lax.ppermute(a, axis, table[(4 - r) % 4]) for r in REL[1:]]]
    ppermute x6 -> x9, starting transfers between devices: 9.24 us -> 12.5 us  [send(): return lax.ppermute(a, axis, table[r])]
    ppermute x6 -> x9, waiting for transfers between devices: 11.8 us -> 9.29 us  [send(): return lax.ppermute(a, axis, table[r])]
    ppermute x10, waiting for transfers between devices: 3.14 us -> 5.52 us  [swap(): return lax.ppermute(a, 'col', CORE[0])]
    all_to_all x1, waiting for transfers between devices: 4.15 us -> 6.02 us  [shards(): lax.all_to_all(both, 'col', 0, 0, axis_index_groups=XGROUPS, tiled=True)]
    ppermute x33 -> x30, starting transfers between devices: 42.9 us -> 43.7 us  [fetch(): return [lax.ppermute(a, axis, table[(4 - r) % 4]) for r in REL[1:]]]
  transfers between devices with their start and end apart: 51 -> 51, of which waited for: 28 -> 25; matrix products, arithmetic and copies ran while one was open for 0% -> 0% of each run, Pallas kernels for 9% -> 10%
where the time goes in v3:
time: 186 us; the launch traced here: 185 us
  waiting for transfers between devices  74 us (40%)
  starting transfers between devices  69 us (37%)
  Pallas kernels  33.2 us (18%)
  local copies, waits for them, and re-layouts  7.48 us (4%)
    ppermute x30, waiting for transfers between devices, fetch(): return [lax.ppermute(a, axis, table[(4 - r) % 4]) for r in REL[1:]]  53.1 us
    ppermute x30, starting transfers between devices, fetch(): return [lax.ppermute(a, axis, table[(4 - r) % 4]) for r in REL[1:]]  43.7 us
    ppermute x9, starting transfers between devices, send(): return lax.ppermute(a, axis, table[r])  12.5 us
    ppermute x9, waiting for transfers between devices, send(): return lax.ppermute(a, axis, table[r])  9.29 us
    pallas_call x4, Pallas kernels, back(): pl.pallas_call(functools.partial(back_kernel, tuple(chunks), bool(carry))...  9.05 us
    pallas_call x4, Pallas kernels, prod(): pl.pallas_call(functools.partial(prod_kernel, chunks, sibling, first, rec...  8.14 us
    unnamed x14, local copies, waits for them, and re-layouts  7.48 us
    pallas_call x2, Pallas kernels, sweep(): pl.pallas_call(functools.partial(sweep_kernel, axis), out_shape=[sds(rows...  7.1 us
  transfers between devices with their start and end apart: 51, of which 25 were waited for; matrix products, arithmetic and copies ran while one was open for 0% of the time, Pallas kernels for 10%

profile of v3, /device:TPU:24, one launch (start us, length us, event | category | flops | bytes accessed | tf_op | source)
XLA Modules:
  0.0 184.7 jit_solution(14693163654748925184)
XLA Ops:
  4.8 3.0 %collective-permute-start.3 = (f32[16,512]{1,0:T(8,128)S(1)}, f32[16,512]{1,0:T(8,128)S(1)}, u32[]{:S(2)}, u32[]{:S(2)}) collective-permute-start(f32[16,512]{1,0:T(8,128)S(1)} %add.6.refs_0_), channel_id=1, source_target_pairs={{0,4},{1,5},{2,6},{3,7},{4,0},{5,1},{6,2},{7,3},{8,12},{9,13},{10,... | collective-permute-start | bytes 98312 | tf_op jit(solution)/shard_map/ppermute | solution.py:363
  8.4 2.6 %collective-permute-start.1 = (f32[16,512]{1,0:T(8,128)S(1)}, f32[16,512]{1,0:T(8,128)S(1)}, u32[]{:S(2)}, u32[]{:S(2)}) collective-permute-start(f32[16,512]{1,0:T(8,128)S(1)} %add.6.refs_0_), channel_id=1, source_target_pairs={{0,6},{1,7},{2,0},{3,1},{4,2},{5,3},{6,4},{7,5},{8,14},{9,15},{10,... | collective-permute-start | bytes 98312 | tf_op jit(solution)/shard_map/ppermute | solution.py:363
  11.1 3.4 %copy-done = f32[2048,1024]{1,0:T(8,128)S(1)} copy-done((f32[2048,1024]{1,0:T(8,128)S(1)}, f32[2048,1024]{1,0:T(8,128)}, u32[]{:S(2)}) %copy-start) | copy-done | bytes 8388632
  21.0 2.8 %prod.7 = f32[1024,512]{1,0:T(8,128)} custom-call(f32[2048,1024]{1,0:T(8,128)S(1)} %copy-done, bf16[1024,512]{1,0:T(8,128)(2,1)S(1)} %get-tuple-element.56.refs_1_, bf16[1024,512]{1,0:T(8,128)(2,1)S(1)} %get-tuple-element.57.refs_2_, f32[512,512]{1,0:T(8,128)S(1)} %collective-permute-done.4.refs_3_, f32[512,512]{1,0:T(8,128)S(1)} %prod.6.refs_4_), custom_call_target="tpu_custom_call" | custom-call | flops 1610612736 | bytes 6291456 | tf_op jit(solution)/shard_map/prod/pallas_call | solution.py:89
  23.8 3.6 %all-to-all-start = ((f32[4,256,512]{2,1,0:T(8,128)}), f32[4,256,512]{2,1,0:T(8,128)S(1)}, u32[]{:S(2)}, u32[]{:S(2)}) async-start(f32[4,256,512]{2,1,0:T(8,128)} %bitcast), calls=%async_computation | async-start | bytes 4194304 | tf_op jit(solution)/shard_map/all_to_all | solution.py:438
  27.4 4.0 %collective-permute-start.8 = (f32[16,512]{1,0:T(8,128)S(1)}, f32[16,512]{1,0:T(8,128)S(1)}, u32[]{:S(2)}, u32[]{:S(2)}) collective-permute-start(f32[16,512]{1,0:T(8,128)S(1)} %add.7.refs_0_), channel_id=1, source_target_pairs={{0,64},{8,72},{16,80},{24,88},{32,96},{40,104},{48,112},{56,120},{... | collective-permute-start | bytes 98312 | tf_op jit(solution)/shard_map/ppermute | solution.py:363
  40.1 4.3 %collective-permute-done.11.refs_3_ = f32[64,512]{1,0:T(8,128)S(1)} collective-permute-done((f32[64,512]{1,0:T(8,128)S(1)}, f32[64,512]{1,0:T(8,128)S(1)}, u32[]{:S(2)}, u32[]{:S(2)}) %collective-permute-start.11) | collective-permute-done | bytes 131104 | tf_op jit(solution)/shard_map/ppermute | solution.py:363
  48.5 6.0 %all-to-all-done = f32[4,256,512]{2,1,0:T(8,128)S(1)} async-done(((f32[4,256,512]{2,1,0:T(8,128)}), f32[4,256,512]{2,1,0:T(8,128)S(1)}, u32[]{:S(2)}, u32[]{:S(2)}) %all-to-all-start) | async-done | bytes 2097184 | tf_op jit(solution)/shard_map/all_to_all | solution.py:438
  55.8 4.1 %sweep.2.w_ref.refs_2_ = f32[256,512]{1,0:T(8,128)S(1)} custom-call(f32[1024,512]{1,0:T(8,128)S(1)} %bitcast.8, f32[256,512]{1,0:T(8,128)S(1)} %copy-done.4, f32[256,512]{1,0:T(8,128)S(1)} %join.6.mine, f32[256,512]{1,0:T(8,128)S(1)} %collective-permute-done.12.theirs), custom_call_target="tpu_custom_call" | custom-call | flops 4831838208 | bytes 4194304 | tf_op jit(solution)/shard_map/sweep/pallas_call | solution.py:268
  61.7 2.7 %collective-permute-start.13 = (f32[256,512]{1,0:T(8,128)S(1)}, f32[256,512]{1,0:T(8,128)S(1)}, u32[]{:S(2)}, u32[]{:S(2)}) collective-permute-start(f32[256,512]{1,0:T(8,128)S(1)} %sweep.2.w_ref.refs_2_), channel_id=1, source_target_pairs={{0,6},{1,7},{2,0},{3,1},{4,2},{5,3},{6,4},{7,5},{8,14},{9,15},{10,... | collective-permute-start | bytes 1572872 | tf_op jit(solution)/shard_map/ppermute | solution.py:359
  64.4 3.3 %flip.1 = (bf16[16,1024,128]{2,1,0:T(8,128)(2,1)S(1)}, bf16[16,1024,128]{2,1,0:T(8,128)(2,1)S(1)}) custom-call(f32[2048,1024]{1,0:T(8,128)S(1)} %bitcast.5), custom_call_target="tpu_custom_call" | custom-call | flops 16777216 | bytes 16777216 | tf_op jit(solution)/shard_map/flip/pallas_call | solution.py:111
  85.1 4.0 %collective-permute-done.23.refs_3_ = f32[16,512]{1,0:T(8,128)S(1)} collective-permute-done((f32[16,512]{1,0:T(8,128)S(1)}, f32[16,512]{1,0:T(8,128)S(1)}, u32[]{:S(2)}, u32[]{:S(2)}) %collective-permute-start.23) | collective-permute-done | bytes 32800 | tf_op jit(solution)/shard_map/ppermute | solution.py:359
  89.1 2.4 %back.5 = (f32[1024,512]{1,0:T(8,128)S(1)}, f32[2048,512]{1,0:T(8,128)}) custom-call(bf16[16,1024,128]{2,1,0:T(8,128)(2,1)S(1)} %get-tuple-element.63.refs_0_, bf16[16,1024,128]{2,1,0:T(8,128)(2,1)S(1)} %get-tuple-element.64.refs_1_, f32[256,512]{1,0:T(8,128)S(1)} %collective-permute-done.13.refs_2_, ...), custom_call_target="tpu_custom_call", output_to_operand_aliasing={{1}: (5, {})} | custom-call | flops 1610612736 | bytes 6291456 | tf_op jit(solution)/shard_map/back/pallas_call | solution.py:161
  91.5 2.4 %collective-permute-start.28 = (f32[16,512]{1,0:T(8,128)S(1)}, f32[16,512]{1,0:T(8,128)S(1)}, u32[]{:S(2)}, u32[]{:S(2)}) collective-permute-start(f32[16,512]{1,0:T(8,128)S(1)} %add.10.refs_0_), channel_id=1, source_target_pairs={{0,64},{8,72},{16,80},{24,88},{32,96},{40,104},{48,112},{56,120},{... | collective-permute-start | bytes 98312 | tf_op jit(solution)/shard_map/ppermute | solution.py:363
  97.2 2.4 %back.6 = (f32[1024,512]{1,0:T(8,128)S(1)}, f32[2048,512]{1,0:T(8,128)}) custom-call(bf16[16,1024,128]{2,1,0:T(8,128)(2,1)S(1)} %get-tuple-element.63.refs_0_, bf16[16,1024,128]{2,1,0:T(8,128)(2,1)S(1)} %get-tuple-element.64.refs_1_, f32[256,512]{1,0:T(8,128)S(1)} %collective-permute-done.24.refs_2_, ...), custom_call_target="tpu_custom_call", output_to_operand_aliasing={{1}: (5, {})} | custom-call | flops 1610612736 | bytes 6291456 | tf_op jit(solution)/shard_map/back/pallas_call | solution.py:161
  105.1 6.8 %all-to-all-start.1 = ((f32[16,64,512]{2,1,0:T(8,128)}), f32[16,64,512]{2,1,0:T(8,128)S(1)}, u32[]{:S(2)}, u32[]{:S(2)}) async-start(f32[16,64,512]{2,1,0:T(8,128)} %bitcast.7), calls=%async_computation.1 | async-start | bytes 4194304 | tf_op jit(solution)/shard_map/all_to_all | solution.py:465
  114.4 3.1 %collective-permute-start.30 = (f32[64,512]{1,0:T(8,128)S(1)}, f32[64,512]{1,0:T(8,128)S(1)}, u32[]{:S(2)}, u32[]{:S(2)}) collective-permute-start(f32[64,512]{1,0:T(8,128)S(1)} %join.7.refs_0_), channel_id=1, source_target_pairs={{0,6},{1,7},{2,0},{3,1},{4,2},{5,3},{6,4},{7,5},{8,14},{9,15},{10,... | collective-permute-start | bytes 393224 | tf_op jit(solution)/shard_map/ppermute | solution.py:363
  118.5 2.7 %collective-permute-done.31.refs_2_ = f32[64,512]{1,0:T(8,128)S(1)} collective-permute-done((f32[64,512]{1,0:T(8,128)S(1)}, f32[64,512]{1,0:T(8,128)S(1)}, u32[]{:S(2)}, u32[]{:S(2)}) %collective-permute-start.31) | collective-permute-done | bytes 131104 | tf_op jit(solution)/shard_map/ppermute | solution.py:363
  124.9 20.8 %collective-permute-done.35.refs_3_ = f32[64,512]{1,0:T(8,128)S(1)} collective-permute-done((f32[64,512]{1,0:T(8,128)S(1)}, f32[64,512]{1,0:T(8,128)S(1)}, u32[]{:S(2)}, u32[]{:S(2)}) %collective-permute-start.35) | collective-permute-done | bytes 131104 | tf_op jit(solution)/shard_map/ppermute | solution.py:363
  148.8 3.0 %sweep.3 = (f32[32,512]{1,0:T(8,128)S(1)}, f32[32,512]{1,0:T(8,128)S(1)}) custom-call(f32[1024,512]{1,0:T(8,128)S(1)} %bitcast.6, f32[1024,512]{1,0:T(8,128)} %start.1, f32[256,512]{1,0:T(8,128)S(1)} %join.8.mine, f32[256,512]{1,0:T(8,128)S(1)} %collective-permute-done.36.theirs), custom_call_target="tpu_custom_call" | custom-call | flops 1207959552 | bytes 4194304 | tf_op jit(solution)/shard_map/sweep/pallas_call | solution.py:268
  151.9 2.8 %collective-permute-start.39 = (f32[32,512]{1,0:T(8,128)S(1)}, f32[32,512]{1,0:T(8,128)S(1)}, u32[]{:S(2)}, u32[]{:S(2)}) collective-permute-start(f32[32,512]{1,0:T(8,128)S(1)} %get-tuple-element.94.refs_0_), channel_id=1, source_target_pairs={{0,64},{8,72},{16,80},{24,88},{32,96},{40,104},{48,112},{56,120},{... | collective-permute-start | bytes 196616 | tf_op jit(solution)/shard_map/ppermute | solution.py:363
  154.7 3.2 %collective-permute-start.37 = (f32[32,512]{1,0:T(8,128)S(1)}, f32[32,512]{1,0:T(8,128)S(1)}, u32[]{:S(2)}, u32[]{:S(2)}) collective-permute-start(f32[32,512]{1,0:T(8,128)S(1)} %get-tuple-element.94.refs_0_), channel_id=1, source_target_pairs={{0,96},{8,104},{16,112},{24,120},{32,0},{40,8},{48,16},{56,24},{64... | collective-permute-start | bytes 196616 | tf_op jit(solution)/shard_map/ppermute | solution.py:363
  160.4 3.8 %collective-permute-done.42.refs_7_ = f32[32,512]{1,0:T(8,128)S(1)} collective-permute-done((f32[32,512]{1,0:T(8,128)S(1)}, f32[32,512]{1,0:T(8,128)S(1)}, u32[]{:S(2)}, u32[]{:S(2)}) %collective-permute-start.42) | collective-permute-done | bytes 65568 | tf_op jit(solution)/shard_map/ppermute | solution.py:363
  169.3 7.5 %collective-permute-done.45.refs_3_ = f32[128,512]{1,0:T(8,128)S(1)} collective-permute-done((f32[128,512]{1,0:T(8,128)S(1)}, f32[128,512]{1,0:T(8,128)S(1)}, u32[]{:S(2)}, u32[]{:S(2)}) %collective-permute-start.45) | collective-permute-done | bytes 262176 | tf_op jit(solution)/shard_map/ppermute | solution.py:363
  (119 shorter events, 78.9 us)
Async XLA Ops:
  4.8 11.5 %collective-permute-start.3 = (f32[16,512]{1,0:T(8,128)S(1)}, f32[16,512]{1,0:T(8,128)S(1)}, u32[]{:S(2)}, u32[]{:S(2)}) collective-permute-start(f32[16,512]{1,0:T(8,128)S(1)} %add.6.refs_0_), channel_id=1, source_target_pairs={{0,4},{1,5},{2,6},{3,7},{4,0},{5,1},{6,2},{7,3},{8,12},{9,13},{10,... | collective-permute-start | bytes 98312 | tf_op jit(solution)/shard_map/ppermute | solution.py:363
  7.8 8.5 %collective-permute-start.2 = (f32[16,512]{1,0:T(8,128)S(1)}, f32[16,512]{1,0:T(8,128)S(1)}, u32[]{:S(2)}, u32[]{:S(2)}) collective-permute-start(f32[16,512]{1,0:T(8,128)S(1)} %add.6.refs_0_), channel_id=1, source_target_pairs={{0,2},{1,3},{2,4},{3,5},{4,6},{5,7},{6,0},{7,1},{8,10},{9,11},{10,... | collective-permute-start | bytes 98312 | tf_op jit(solution)/shard_map/ppermute | solution.py:363
  8.4 7.9 %collective-permute-start.1 = (f32[16,512]{1,0:T(8,128)S(1)}, f32[16,512]{1,0:T(8,128)S(1)}, u32[]{:S(2)}, u32[]{:S(2)}) collective-permute-start(f32[16,512]{1,0:T(8,128)S(1)} %add.6.refs_0_), channel_id=1, source_target_pairs={{0,6},{1,7},{2,0},{3,1},{4,2},{5,3},{6,4},{7,5},{8,14},{9,15},{10,... | collective-permute-start | bytes 98312 | tf_op jit(solution)/shard_map/ppermute | solution.py:363
  23.8 30.7 %all-to-all-start = ((f32[4,256,512]{2,1,0:T(8,128)}), f32[4,256,512]{2,1,0:T(8,128)S(1)}, u32[]{:S(2)}, u32[]{:S(2)}) async-start(f32[4,256,512]{2,1,0:T(8,128)} %bitcast), calls=%async_computation | async-start | bytes 4194304 | tf_op jit(solution)/shard_map/all_to_all | solution.py:438
  36.6 7.8 %collective-permute-start.11 = (f32[64,512]{1,0:T(8,128)S(1)}, f32[64,512]{1,0:T(8,128)S(1)}, u32[]{:S(2)}, u32[]{:S(2)}) collective-permute-start(f32[64,512]{1,0:T(8,128)S(1)} %join.5.refs_0_), channel_id=1, source_target_pairs={{0,16},{8,24},{16,0},{24,8},{32,48},{40,56},{48,32},{56,40},{64,80... | collective-permute-start | bytes 393224 | tf_op jit(solution)/shard_map/ppermute | solution.py:363
  60.6 11.3 %collective-permute-start.15 = (f32[256,512]{1,0:T(8,128)S(1)}, f32[256,512]{1,0:T(8,128)S(1)}, u32[]{:S(2)}, u32[]{:S(2)}) collective-permute-start(f32[256,512]{1,0:T(8,128)S(1)} %sweep.2.w_ref.refs_2_), channel_id=1, source_target_pairs={{0,1},{1,0},{2,3},{3,2},{4,5},{5,4},{6,7},{7,6},{8,9},{9,8},{10,11... | collective-permute-start | bytes 1572872 | tf_op jit(solution)/shard_map/ppermute | solution.py:355
  61.1 18.0 %collective-permute-start.19 = (f32[256,512]{1,0:T(8,128)S(1)}, f32[256,512]{1,0:T(8,128)S(1)}, u32[]{:S(2)}, u32[]{:S(2)}) collective-permute-start(f32[256,512]{1,0:T(8,128)S(1)} %sweep.2.w_ref.refs_2_), channel_id=1, source_target_pairs={{0,2},{1,3},{2,4},{3,5},{4,6},{5,7},{6,0},{7,1},{8,10},{9,11},{10,... | collective-permute-start | bytes 1572872 | tf_op jit(solution)/shard_map/ppermute | solution.py:359
  61.7 17.5 %collective-permute-start.13 = (f32[256,512]{1,0:T(8,128)S(1)}, f32[256,512]{1,0:T(8,128)S(1)}, u32[]{:S(2)}, u32[]{:S(2)}) collective-permute-start(f32[256,512]{1,0:T(8,128)S(1)} %sweep.2.w_ref.refs_2_), channel_id=1, source_target_pairs={{0,6},{1,7},{2,0},{3,1},{4,2},{5,3},{6,4},{7,5},{8,14},{9,15},{10,... | collective-permute-start | bytes 1572872 | tf_op jit(solution)/shard_map/ppermute | solution.py:359
  67.8 8.1 %collective-permute-start.16 = (f32[64,512]{1,0:T(8,128)S(1)}, f32[64,512]{1,0:T(8,128)S(1)}, u32[]{:S(2)}, u32[]{:S(2)}) collective-permute-start(f32[64,512]{1,0:T(8,128)S(1)} %get-tuple-element.70), channel_id=1, source_target_pairs={{0,32},{8,40},{16,48},{24,56},{32,64},{40,72},{48,80},{56,88},{64,... | collective-permute-start | bytes 393224 | tf_op jit(solution)/shard_map/ppermute | solution.py:359
  69.8 7.5 %collective-permute-start.17 = (f32[64,512]{1,0:T(8,128)S(1)}, f32[64,512]{1,0:T(8,128)S(1)}, u32[]{:S(2)}, u32[]{:S(2)}) collective-permute-start(f32[64,512]{1,0:T(8,128)S(1)} %get-tuple-element.71), channel_id=1, source_target_pairs={{0,96},{8,104},{16,112},{24,120},{32,0},{40,8},{48,16},{56,24},{64... | collective-permute-start | bytes 393224 | tf_op jit(solution)/shard_map/ppermute | solution.py:359
  79.2 15.8 %collective-permute-start.24 = (f32[256,512]{1,0:T(8,128)S(1)}, f32[256,512]{1,0:T(8,128)S(1)}, u32[]{:S(2)}, u32[]{:S(2)}) collective-permute-start(f32[256,512]{1,0:T(8,128)S(1)} %collective-permute-done.13.refs_2_), channel_id=1, source_target_pairs={{0,1},{1,0},{2,3},{3,2},{4,5},{5,4},{6,7},{7,6},{8,9},{9,8},{10,11... | collective-permute-start | bytes 1572872 | tf_op jit(solution)/shard_map/ppermute | solution.py:355
  79.3 17.9 %collective-permute-start.25 = (f32[256,512]{1,0:T(8,128)S(1)}, f32[256,512]{1,0:T(8,128)S(1)}, u32[]{:S(2)}, u32[]{:S(2)}) collective-permute-start(f32[256,512]{1,0:T(8,128)S(1)} %collective-permute-done.19.refs_3_), channel_id=1, source_target_pairs={{0,1},{1,0},{2,3},{3,2},{4,5},{5,4},{6,7},{7,6},{8,9},{9,8},{10,11... | collective-permute-start | bytes 1572872 | tf_op jit(solution)/shard_map/ppermute | solution.py:355
  79.8 19.9 %collective-permute-start.20 = (f32[256,512]{1,0:T(8,128)S(1)}, f32[256,512]{1,0:T(8,128)S(1)}, u32[]{:S(2)}, u32[]{:S(2)}) collective-permute-start(f32[256,512]{1,0:T(8,128)S(1)} %sweep.2.w_ref.refs_2_), channel_id=1, source_target_pairs={{0,4},{1,5},{2,6},{3,7},{4,0},{5,1},{6,2},{7,3},{8,12},{9,13},{10,... | collective-permute-start | bytes 1572872 | tf_op jit(solution)/shard_map/ppermute | solution.py:359
  91.5 8.1 %collective-permute-start.28 = (f32[16,512]{1,0:T(8,128)S(1)}, f32[16,512]{1,0:T(8,128)S(1)}, u32[]{:S(2)}, u32[]{:S(2)}) collective-permute-start(f32[16,512]{1,0:T(8,128)S(1)} %add.10.refs_0_), channel_id=1, source_target_pairs={{0,64},{8,72},{16,80},{24,88},{32,96},{40,104},{48,112},{56,120},{... | collective-permute-start | bytes 98312 | tf_op jit(solution)/shard_map/ppermute | solution.py:363
  105.1 43.7 %all-to-all-start.1 = ((f32[16,64,512]{2,1,0:T(8,128)}), f32[16,64,512]{2,1,0:T(8,128)S(1)}, u32[]{:S(2)}, u32[]{:S(2)}) async-start(f32[16,64,512]{2,1,0:T(8,128)} %bitcast.7), calls=%async_computation.1 | async-start | bytes 4194304 | tf_op jit(solution)/shard_map/all_to_all | solution.py:465
  121.3 24.4 %collective-permute-start.35 = (f32[64,512]{1,0:T(8,128)S(1)}, f32[64,512]{1,0:T(8,128)S(1)}, u32[]{:S(2)}, u32[]{:S(2)}) collective-permute-start(f32[64,512]{1,0:T(8,128)S(1)} %add.11.refs_0_), channel_id=1, source_target_pairs={{0,16},{8,24},{16,0},{24,8},{32,48},{40,56},{48,32},{56,40},{64,80... | collective-permute-start | bytes 393224 | tf_op jit(solution)/shard_map/ppermute | solution.py:363
  122.8 24.0 %collective-permute-start.34 = (f32[64,512]{1,0:T(8,128)S(1)}, f32[64,512]{1,0:T(8,128)S(1)}, u32[]{:S(2)}, u32[]{:S(2)}) collective-permute-start(f32[64,512]{1,0:T(8,128)S(1)} %add.11.refs_0_), channel_id=1, source_target_pairs={{0,8},{8,16},{16,24},{24,0},{32,40},{40,48},{48,56},{56,32},{64,72... | collective-permute-start | bytes 393224 | tf_op jit(solution)/shard_map/ppermute | solution.py:363
  124.9 21.9 %collective-permute-start.33 = (f32[64,512]{1,0:T(8,128)S(1)}, f32[64,512]{1,0:T(8,128)S(1)}, u32[]{:S(2)}, u32[]{:S(2)}) collective-permute-start(f32[64,512]{1,0:T(8,128)S(1)} %add.11.refs_0_), channel_id=1, source_target_pairs={{0,24},{8,0},{16,8},{24,16},{32,56},{40,32},{48,40},{56,48},{64,88... | collective-permute-start | bytes 393224 | tf_op jit(solution)/shard_map/ppermute | solution.py:363
  151.9 8.6 %collective-permute-start.39 = (f32[32,512]{1,0:T(8,128)S(1)}, f32[32,512]{1,0:T(8,128)S(1)}, u32[]{:S(2)}, u32[]{:S(2)}) collective-permute-start(f32[32,512]{1,0:T(8,128)S(1)} %get-tuple-element.94.refs_0_), channel_id=1, source_target_pairs={{0,64},{8,72},{16,80},{24,88},{32,96},{40,104},{48,112},{56,120},{... | collective-permute-start | bytes 196616 | tf_op jit(solution)/shard_map/ppermute | solution.py:363
  165.9 10.8 %collective-permute-start.45 = (f32[128,512]{1,0:T(8,128)S(1)}, f32[128,512]{1,0:T(8,128)S(1)}, u32[]{:S(2)}, u32[]{:S(2)}) collective-permute-start(f32[128,512]{1,0:T(8,128)S(1)} %get-tuple-element.96.refs_0_), channel_id=1, source_target_pairs={{0,16},{8,24},{16,0},{24,8},{32,48},{40,56},{48,32},{56,40},{64,80... | collective-permute-start | bytes 786440 | tf_op jit(solution)/shard_map/ppermute | solution.py:363
  166.4 11.0 %collective-permute-start.44 = (f32[128,512]{1,0:T(8,128)S(1)}, f32[128,512]{1,0:T(8,128)S(1)}, u32[]{:S(2)}, u32[]{:S(2)}) collective-permute-start(f32[128,512]{1,0:T(8,128)S(1)} %get-tuple-element.96.refs_0_), channel_id=1, source_target_pairs={{0,8},{8,16},{16,24},{24,0},{32,40},{40,48},{48,56},{56,32},{64,72... | collective-permute-start | bytes 786440 | tf_op jit(solution)/shard_map/ppermute | solution.py:363
  167.5 12.2 %collective-permute-start.43 = (f32[128,512]{1,0:T(8,128)S(1)}, f32[128,512]{1,0:T(8,128)S(1)}, u32[]{:S(2)}, u32[]{:S(2)}) collective-permute-start(f32[128,512]{1,0:T(8,128)S(1)} %get-tuple-element.96.refs_0_), channel_id=1, source_target_pairs={{0,24},{8,0},{16,8},{24,16},{32,56},{40,32},{48,40},{56,48},{64,88... | collective-permute-start | bytes 786440 | tf_op jit(solution)/shard_map/ppermute | solution.py:363
  168.4 11.3 %collective-permute-start.48 = (f32[128,512]{1,0:T(8,128)S(1)}, f32[128,512]{1,0:T(8,128)S(1)}, u32[]{:S(2)}, u32[]{:S(2)}) collective-permute-start(f32[128,512]{1,0:T(8,128)S(1)} %get-tuple-element.97.refs_4_), channel_id=1, source_target_pairs={{0,64},{8,72},{16,80},{24,88},{32,96},{40,104},{48,112},{56,120},{... | collective-permute-start | bytes 786440 | tf_op jit(solution)/shard_map/ppermute | solution.py:363
  168.7 12.3 %collective-permute-start.47 = (f32[128,512]{1,0:T(8,128)S(1)}, f32[128,512]{1,0:T(8,128)S(1)}, u32[]{:S(2)}, u32[]{:S(2)}) collective-permute-start(f32[128,512]{1,0:T(8,128)S(1)} %get-tuple-element.97.refs_4_), channel_id=1, source_target_pairs={{0,32},{8,40},{16,48},{24,56},{32,64},{40,72},{48,80},{56,88},{64,... | collective-permute-start | bytes 786440 | tf_op jit(solution)/shard_map/ppermute | solution.py:363
  (34 other events, 172.5 us)

commit v4 on v3

--- a/solution.py
+++ b/solution.py
@@ -196,15 +196,13 @@
 
 
 def gram_w_kernel(w_ref, mine_ref, theirs_ref, tmp):
-    z, y, _, c = place()
+    _, _, _, c = place()
     w = w_ref[...]
     tmp[...] = dot3(*split(w.T), *split(w))
-    for k in range(4):
-        for m in range(4):
-            s = 4 * ((z + REL[k]) % 4) + (y + REL[m]) % 4
-            at = 64 * k + 16 * m
-            mine_ref[at : at + 16, :] = tmp[pl.ds(pl.multiple_of(32 * s + 16 * c, 16), 16), :]
-            theirs_ref[at : at + 16, :] = tmp[pl.ds(pl.multiple_of(32 * s + 16 * (1 - c), 16), 16), :]
+    for s in range(16):
+        rows = slice(16 * s, 16 * s + 16)
+        mine_ref[rows, :] = tmp[pl.ds(pl.multiple_of(32 * s + 16 * c, 16), 16), :]
+        theirs_ref[rows, :] = tmp[pl.ds(pl.multiple_of(32 * s + 16 * (1 - c), 16), 16), :]
 
 
 def gram_w(w):
@@ -394,28 +392,40 @@
     total = refs[0][...]
     for r in refs[1:n]:
         total = total + r[...]
-    outs = refs[n:]
-    rows = total.shape[0] // len(outs)
-    for k, out in enumerate(outs):
-        out[...] = total[rows * k : rows * (k + 1)]
-
-
-def add(parts, nout=1):
+    refs[-1][...] = total
+
+
+def add(parts, hold=None):
     rows = parts[0].shape[0]
-    out = pl.pallas_call(
+    held = [] if hold is None else [hold]
+    return pl.pallas_call(
         functools.partial(add_kernel, len(parts)),
-        out_shape=[sds(rows // nout, 512)] * nout,
-        in_specs=[VM] * len(parts),
-        out_specs=[VM] * nout,
-        compiler_params=params(4),
+        out_shape=sds(rows, 512),
+        in_specs=[VM] * (len(parts) + len(held)),
+        out_specs=VM,
+        compiler_params=params(14 if held else 4),
         cost_estimate=cost(rows * 512 * len(parts), rows * 4096 * len(parts)),
         name="add",
-    )(*parts)
-    return out if nout > 1 else out[0]
-
-
-def deal(pieces, axis, table):
-    return [pieces[0]] + [send(pieces[k], axis, table, REL[k]) for k in (1, 2, 3)]
+    )(*parts, *held)
+
+
+def fold_kernel(a_ref, out_ref):
+    total = a_ref[:16, :]
+    for k in range(16, 256, 16):
+        total = total + a_ref[k : k + 16, :]
+    out_ref[...] = total
+
+
+def fold(a):
+    return pl.pallas_call(
+        fold_kernel,
+        out_shape=sds(16, 512),
+        in_specs=[VM],
+        out_specs=VM,
+        compiler_params=params(4),
+        cost_estimate=cost(1 << 17, 1 << 20),
+        name="fold",
+    )(a)
 
 
 def spread(strip):
@@ -425,7 +435,7 @@
 
 def shards(spectra, w_start, h_start):
     g_mine, g_theirs = gram_h(h_start)
-    strip = add([g_mine, swap(g_theirs)])
+    strip = add([g_mine, swap(g_theirs)], spectra)
 
     a1, hh, hl = prod(spectra, after(h_start, strip), (0, 1), True)
     r1 = swap(a1)
@@ -445,19 +455,16 @@
     near_p, near_m = send(w, "col", X, 3), send(w, "col", X, 1)
 
     g_mine, g_theirs = gram_w(w)
-    flipped = flip(after(spectra, g_theirs))
-    strips = add([g_mine, after(swap(g_theirs), *flipped)], 4)
-    strips = deal(strips, "samp", Z)
-    carry = back(flipped, (w, ws), ((0, False), (0, True)))
-    strips = add([after(strips[0], carry[0])] + strips[1:], 4)
-    near_p, near_m = after(near_p, *strips), after(near_m, *strips)
+    strip = fold(lax.all_to_all(add([g_mine, swap(g_theirs)]), "samp", 0, 0, tiled=True))
+    near_p, near_m = after(near_p, strip), after(near_m, strip)
     far = send(after(w, near_p, near_m), "col", X, 2)
     sib_p, sib_m = swap(near_p), swap(near_m)
-    strips = deal(strips, "samp", Y)
-    carry = back(flipped, (near_p, near_m), ((1, False), (3, False)), (after(carry[0], *strips), carry[1]))
-    strip = add([after(strips[0], carry[0])] + strips[1:])
-    carry = back(flipped, (sib_p, sib_m), ((1, True), (3, True)), (after(carry[0], strip), carry[1]))
+    flipped = flip(after(spectra, strip))
+    carry = back(flipped, (w, ws), ((0, False), (0, True)))
     part = join([after(strip, carry[0])] + fetch(strip, "samp", Z))
+    carry = back(flipped, (near_p, near_m), ((1, False), (3, False)), (after(carry[0], part), carry[1]))
+    carry = back(flipped, (sib_p, sib_m), ((1, True), (3, True)), carry)
+    part = join([after(part, carry[0])] + fetch(part, "samp", Y))
     sib_f = swap(after(far, part))
     carry = (after(carry[0], part), carry[1])
     back_sum, w_out = back(flipped, (far, sib_f), ((2, False), (2, True)), carry, True)
@@ -465,7 +472,6 @@
     product = lax.all_to_all(back_sum, "samp", 0, 0, tiled=True)
     part = after(part, back_sum)
     part = add([part] + fetch(part, "col", X))
-    part = join([part] + fetch(part, "samp", Y))
     ha, hb = sweep(product, h_start, "samp", 64, (part, swap(part)), 2)
 
     row_a, row_b = join([ha] + fetch(ha, "samp", Z) + [hb] + fetch(hb, "samp", Y), 2)

time: 186 us -> 189 us (1.016)
  local copies, waits for them, and re-layouts: 7.48 us -> 12.5 us
  waiting for transfers between devices: 74 us -> 69.7 us
    ppermute x9 -> x3, waiting for transfers between devices: 9.29 us -> 0.01 us  [send(): return lax.ppermute(a, axis, table[r])]
    ppermute x9 -> x3, starting transfers between devices: 12.5 us -> 3.31 us  [send(): return lax.ppermute(a, axis, table[r])]
    all_to_all x0 -> x1, waiting for transfers between devices: none -> 8.95 us  [shards(): lax.all_to_all(add([g_mine, swap(g_theirs)]), 'samp', 0, 0, tiled=True)]
    all_to_all x0 -> x1, starting transfers between devices: none -> 8.18 us  [shards(): lax.all_to_all(add([g_mine, swap(g_theirs)]), 'samp', 0, 0, tiled=True)]
    unnamed x14 -> x16, local copies, waits for them, and re-layouts: 7.48 us -> 12.5 us
    ppermute x30, waiting for transfers between devices: 53.1 us -> 49 us  [fetch(): return [lax.ppermute(a, axis, table[(4 - r) % 4]) for r in REL[1:]]]
    ppermute x30, starting transfers between devices: 43.7 us -> 46.2 us  [fetch(): return [lax.ppermute(a, axis, table[(4 - r) % 4]) for r in REL[1:]]]
  transfers between devices with their start and end apart: 51 -> 46, of which waited for: 25 -> 20; matrix products, arithmetic and copies ran while one was open for 0% -> 0% of each run, Pallas kernels for 10% -> 10%
where the time goes in v4:
time: 189 us; the launch traced here: 188 us
  starting transfers between devices  70.8 us (37%)
  waiting for transfers between devices  69.7 us (37%)
  Pallas kernels  34.1 us (18%)
  local copies, waits for them, and re-layouts  12.5 us (7%)
    ppermute x30, waiting for transfers between devices, fetch(): return [lax.ppermute(a, axis, table[(4 - r) % 4]) for r in REL[1:]]  49 us
    ppermute x30, starting transfers between devices, fetch(): return [lax.ppermute(a, axis, table[(4 - r) % 4]) for r in REL[1:]]  46.2 us
    unnamed x16, local copies, waits for them, and re-layouts  12.5 us
    pallas_call x4, Pallas kernels, back(): pl.pallas_call(functools.partial(back_kernel, tuple(chunks), bool(carry))...  9.05 us
    all_to_all x1, waiting for transfers between devices, shards(): lax.all_to_all(add([g_mine, swap(g_theirs)]), 'samp', 0, 0, tiled=True)  8.95 us
    all_to_all x1, starting transfers between devices, shards(): lax.all_to_all(add([g_mine, swap(g_theirs)]), 'samp', 0, 0, tiled=True)  8.18 us
    pallas_call x4, Pallas kernels, prod(): pl.pallas_call(functools.partial(prod_kernel, chunks, sibling, first, rec...  8.14 us
    pallas_call x2, Pallas kernels, sweep(): pl.pallas_call(functools.partial(sweep_kernel, axis), out_shape=[sds(rows...  7.1 us
  transfers between devices with their start and end apart: 46, of which 20 were waited for; matrix products, arithmetic and copies ran while one was open for 0% of the time, Pallas kernels for 10%

profile of v4, /device:TPU:24, one launch (start us, length us, event | category | flops | bytes accessed | tf_op | source)
XLA Modules:
  0.0 188.1 jit_solution(4232043320744081749)
XLA Ops:
  4.8 3.4 %copy-done = f32[2048,1024]{1,0:T(8,128)S(1)} copy-done((f32[2048,1024]{1,0:T(8,128)S(1)}, f32[2048,1024]{1,0:T(8,128)}, u32[]{:S(2)}) %copy-start) | copy-done | bytes 8388632
  8.2 3.1 %collective-permute-start.3 = (f32[16,512]{1,0:T(8,128)S(1)}, f32[16,512]{1,0:T(8,128)S(1)}, u32[]{:S(2)}, u32[]{:S(2)}) collective-permute-start(f32[16,512]{1,0:T(8,128)S(1)} %add.4.refs_0_), channel_id=1, source_target_pairs={{0,4},{1,5},{2,6},{3,7},{4,0},{5,1},{6,2},{7,3},{8,12},{9,13},{10,... | collective-permute-start | bytes 98312 | tf_op jit(solution)/shard_map/ppermute | solution.py:361
  21.1 2.8 %prod.7 = f32[1024,512]{1,0:T(8,128)} custom-call(f32[2048,1024]{1,0:T(8,128)S(1)} %copy-done, bf16[1024,512]{1,0:T(8,128)(2,1)S(1)} %get-tuple-element.45.refs_1_, bf16[1024,512]{1,0:T(8,128)(2,1)S(1)} %get-tuple-element.46.refs_2_, f32[512,512]{1,0:T(8,128)S(1)} %collective-permute-done.4.refs_3_, f32[512,512]{1,0:T(8,128)S(1)} %prod.6.refs_4_), custom_call_target="tpu_custom_call" | custom-call | flops 1610612736 | bytes 6291456 | tf_op jit(solution)/shard_map/prod/pallas_call | solution.py:89
  23.9 4.4 %all-to-all-start = ((f32[4,256,512]{2,1,0:T(8,128)}), f32[4,256,512]{2,1,0:T(8,128)S(1)}, u32[]{:S(2)}, u32[]{:S(2)}) async-start(f32[4,256,512]{2,1,0:T(8,128)} %bitcast), calls=%async_computation | async-start | bytes 4194304 | tf_op jit(solution)/shard_map/all_to_all | solution.py:448
  28.3 3.9 %collective-permute-start.8 = (f32[16,512]{1,0:T(8,128)S(1)}, f32[16,512]{1,0:T(8,128)S(1)}, u32[]{:S(2)}, u32[]{:S(2)}) collective-permute-start(f32[16,512]{1,0:T(8,128)S(1)} %add.5.refs_0_), channel_id=1, source_target_pairs={{0,64},{8,72},{16,80},{24,88},{32,96},{40,104},{48,112},{56,120},{... | collective-permute-start | bytes 98312 | tf_op jit(solution)/shard_map/ppermute | solution.py:361
  40.8 3.8 %collective-permute-done.11.refs_3_ = f32[64,512]{1,0:T(8,128)S(1)} collective-permute-done((f32[64,512]{1,0:T(8,128)S(1)}, f32[64,512]{1,0:T(8,128)S(1)}, u32[]{:S(2)}, u32[]{:S(2)}) %collective-permute-start.11) | collective-permute-done | bytes 131104 | tf_op jit(solution)/shard_map/ppermute | solution.py:361
  50.0 4.9 %all-to-all-done = f32[4,256,512]{2,1,0:T(8,128)S(1)} async-done(((f32[4,256,512]{2,1,0:T(8,128)}), f32[4,256,512]{2,1,0:T(8,128)S(1)}, u32[]{:S(2)}, u32[]{:S(2)}) %all-to-all-start) | async-done | bytes 2097184 | tf_op jit(solution)/shard_map/all_to_all | solution.py:448
  57.0 4.1 %sweep.2.w_ref.refs_2_ = f32[256,512]{1,0:T(8,128)S(1)} custom-call(f32[1024,512]{1,0:T(8,128)S(1)} %bitcast.7, f32[256,512]{1,0:T(8,128)S(1)} %copy-done.5, f32[256,512]{1,0:T(8,128)S(1)} %join.6.mine, f32[256,512]{1,0:T(8,128)S(1)} %copy-done.7), custom_call_target="tpu_custom_call" | custom-call | flops 4831838208 | bytes 4194304 | tf_op jit(solution)/shard_map/sweep/pallas_call | solution.py:266
  66.0 8.2 %all-to-all-start.1 = ((f32[16,16,512]{2,1,0:T(8,128)}), f32[16,16,512]{2,1,0:T(8,128)S(1)}, u32[]{:S(2)}, u32[]{:S(2)}) async-start(f32[16,16,512]{2,1,0:T(8,128)} %bitcast.2), calls=%async_computation.1 | async-start | bytes 1048576 | tf_op jit(solution)/shard_map/all_to_all | solution.py:458
  74.2 9.0 %all-to-all-done.1 = f32[16,16,512]{2,1,0:T(8,128)S(1)} async-done(((f32[16,16,512]{2,1,0:T(8,128)}), f32[16,16,512]{2,1,0:T(8,128)S(1)}, u32[]{:S(2)}, u32[]{:S(2)}) %all-to-all-start.1) | async-done | bytes 524320 | tf_op jit(solution)/shard_map/all_to_all | solution.py:458
  85.3 3.4 %copy-done.1 = f32[2048,1024]{1,0:T(8,128)S(1)} copy-done((f32[2048,1024]{1,0:T(8,128)S(1)}, f32[2048,1024]{1,0:T(8,128)}, u32[]{:S(2)}) %copy-start.1) | copy-done | bytes 8388632
  88.7 3.3 %flip.1 = (bf16[16,1024,128]{2,1,0:T(8,128)(2,1)S(1)}, bf16[16,1024,128]{2,1,0:T(8,128)(2,1)S(1)}) custom-call(f32[2048,1024]{1,0:T(8,128)S(1)} %copy-done.1), custom_call_target="tpu_custom_call" | custom-call | flops 16777216 | bytes 16777216 | tf_op jit(solution)/shard_map/flip/pallas_call | solution.py:111
  92.7 2.7 %collective-permute-start.18 = (f32[16,512]{1,0:T(8,128)S(1)}, f32[16,512]{1,0:T(8,128)S(1)}, u32[]{:S(2)}, u32[]{:S(2)}) collective-permute-start(f32[16,512]{1,0:T(8,128)S(1)} %fold.1.refs_0_), channel_id=1, source_target_pairs={{0,96},{8,104},{16,112},{24,120},{32,0},{40,8},{48,16},{56,24},{64... | collective-permute-start | bytes 98312 | tf_op jit(solution)/shard_map/ppermute | solution.py:361
  106.8 3.2 %collective-permute-done.23.refs_1_ = f32[64,512]{1,0:T(8,128)S(1)} collective-permute-done((f32[64,512]{1,0:T(8,128)S(1)}, f32[64,512]{1,0:T(8,128)S(1)}, u32[]{:S(2)}, u32[]{:S(2)}) %collective-permute-start.23) | collective-permute-done | bytes 131104 | tf_op jit(solution)/shard_map/ppermute | solution.py:361
  115.5 6.9 %all-to-all-start.2 = ((f32[16,64,512]{2,1,0:T(8,128)}), f32[16,64,512]{2,1,0:T(8,128)S(1)}, u32[]{:S(2)}, u32[]{:S(2)}) async-start(f32[16,64,512]{2,1,0:T(8,128)} %bitcast.8), calls=%async_computation.2 | async-start | bytes 4194304 | tf_op jit(solution)/shard_map/all_to_all | solution.py:472
  122.5 3.5 %collective-permute-start.29 = (f32[256,512]{1,0:T(8,128)S(1)}, f32[256,512]{1,0:T(8,128)S(1)}, u32[]{:S(2)}, u32[]{:S(2)}) collective-permute-start(f32[256,512]{1,0:T(8,128)S(1)} %join.8.refs_0_), channel_id=1, source_target_pairs={{0,4},{1,5},{2,6},{3,7},{4,0},{5,1},{6,2},{7,3},{8,12},{9,13},{10,... | collective-permute-start | bytes 1572872 | tf_op jit(solution)/shard_map/ppermute | solution.py:361
  126.0 3.2 %collective-permute-start.27 = (f32[256,512]{1,0:T(8,128)S(1)}, f32[256,512]{1,0:T(8,128)S(1)}, u32[]{:S(2)}, u32[]{:S(2)}) collective-permute-start(f32[256,512]{1,0:T(8,128)S(1)} %join.8.refs_0_), channel_id=1, source_target_pairs={{0,6},{1,7},{2,0},{3,1},{4,2},{5,3},{6,4},{7,5},{8,14},{9,15},{10,... | collective-permute-start | bytes 1572872 | tf_op jit(solution)/shard_map/ppermute | solution.py:361
  129.2 9.6 %collective-permute-done.29.refs_3_ = f32[256,512]{1,0:T(8,128)S(1)} collective-permute-done((f32[256,512]{1,0:T(8,128)S(1)}, f32[256,512]{1,0:T(8,128)S(1)}, u32[]{:S(2)}, u32[]{:S(2)}) %collective-permute-start.29) | collective-permute-done | bytes 524320 | tf_op jit(solution)/shard_map/ppermute | solution.py:361
  138.8 10.1 %collective-permute-done.28.refs_2_ = f32[256,512]{1,0:T(8,128)S(1)} collective-permute-done((f32[256,512]{1,0:T(8,128)S(1)}, f32[256,512]{1,0:T(8,128)S(1)}, u32[]{:S(2)}, u32[]{:S(2)}) %collective-permute-start.28) | collective-permute-done | bytes 524320 | tf_op jit(solution)/shard_map/ppermute | solution.py:361
  152.3 3.0 %sweep.3 = (f32[32,512]{1,0:T(8,128)S(1)}, f32[32,512]{1,0:T(8,128)S(1)}) custom-call(f32[1024,512]{1,0:T(8,128)S(1)} %bitcast.6, f32[1024,512]{1,0:T(8,128)} %start.1, f32[256,512]{1,0:T(8,128)S(1)} %add.7.mine, f32[256,512]{1,0:T(8,128)S(1)} %collective-permute-done.30.theirs), custom_call_target="tpu_custom_call" | custom-call | flops 1207959552 | bytes 4194304 | tf_op jit(solution)/shard_map/sweep/pallas_call | solution.py:266
  155.4 2.8 %collective-permute-start.33 = (f32[32,512]{1,0:T(8,128)S(1)}, f32[32,512]{1,0:T(8,128)S(1)}, u32[]{:S(2)}, u32[]{:S(2)}) collective-permute-start(f32[32,512]{1,0:T(8,128)S(1)} %get-tuple-element.72.refs_0_), channel_id=1, source_target_pairs={{0,64},{8,72},{16,80},{24,88},{32,96},{40,104},{48,112},{56,120},{... | collective-permute-start | bytes 196616 | tf_op jit(solution)/shard_map/ppermute | solution.py:361
  158.2 3.2 %collective-permute-start.31 = (f32[32,512]{1,0:T(8,128)S(1)}, f32[32,512]{1,0:T(8,128)S(1)}, u32[]{:S(2)}, u32[]{:S(2)}) collective-permute-start(f32[32,512]{1,0:T(8,128)S(1)} %get-tuple-element.72.refs_0_), channel_id=1, source_target_pairs={{0,96},{8,104},{16,112},{24,120},{32,0},{40,8},{48,16},{56,24},{64... | collective-permute-start | bytes 196616 | tf_op jit(solution)/shard_map/ppermute | solution.py:361
  163.9 3.4 %collective-permute-done.36.refs_7_ = f32[32,512]{1,0:T(8,128)S(1)} collective-permute-done((f32[32,512]{1,0:T(8,128)S(1)}, f32[32,512]{1,0:T(8,128)S(1)}, u32[]{:S(2)}, u32[]{:S(2)}) %collective-permute-start.36) | collective-permute-done | bytes 65568 | tf_op jit(solution)/shard_map/ppermute | solution.py:361
  173.8 6.4 %collective-permute-done.39.refs_3_ = f32[128,512]{1,0:T(8,128)S(1)} collective-permute-done((f32[128,512]{1,0:T(8,128)S(1)}, f32[128,512]{1,0:T(8,128)S(1)}, u32[]{:S(2)}, u32[]{:S(2)}) %collective-permute-start.39) | collective-permute-done | bytes 262176 | tf_op jit(solution)/shard_map/ppermute | solution.py:361
  (109 shorter events, 74.9 us)
Async XLA Ops:
  8.2 8.2 %collective-permute-start.3 = (f32[16,512]{1,0:T(8,128)S(1)}, f32[16,512]{1,0:T(8,128)S(1)}, u32[]{:S(2)}, u32[]{:S(2)}) collective-permute-start(f32[16,512]{1,0:T(8,128)S(1)} %add.4.refs_0_), channel_id=1, source_target_pairs={{0,4},{1,5},{2,6},{3,7},{4,0},{5,1},{6,2},{7,3},{8,12},{9,13},{10,... | collective-permute-start | bytes 98312 | tf_op jit(solution)/shard_map/ppermute | solution.py:361
  23.9 31.0 %all-to-all-start = ((f32[4,256,512]{2,1,0:T(8,128)}), f32[4,256,512]{2,1,0:T(8,128)S(1)}, u32[]{:S(2)}, u32[]{:S(2)}) async-start(f32[4,256,512]{2,1,0:T(8,128)} %bitcast), calls=%async_computation | async-start | bytes 4194304 | tf_op jit(solution)/shard_map/all_to_all | solution.py:448
  28.3 7.1 %collective-permute-start.8 = (f32[16,512]{1,0:T(8,128)S(1)}, f32[16,512]{1,0:T(8,128)S(1)}, u32[]{:S(2)}, u32[]{:S(2)}) collective-permute-start(f32[16,512]{1,0:T(8,128)S(1)} %add.5.refs_0_), channel_id=1, source_target_pairs={{0,64},{8,72},{16,80},{24,88},{32,96},{40,104},{48,112},{56,120},{... | collective-permute-start | bytes 98312 | tf_op jit(solution)/shard_map/ppermute | solution.py:361
  37.3 7.3 %collective-permute-start.11 = (f32[64,512]{1,0:T(8,128)S(1)}, f32[64,512]{1,0:T(8,128)S(1)}, u32[]{:S(2)}, u32[]{:S(2)}) collective-permute-start(f32[64,512]{1,0:T(8,128)S(1)} %join.5.refs_0_), channel_id=1, source_target_pairs={{0,16},{8,24},{16,0},{24,8},{32,48},{40,56},{48,32},{56,40},{64,80... | collective-permute-start | bytes 393224 | tf_op jit(solution)/shard_map/ppermute | solution.py:361
  61.9 21.3 %collective-permute-start.15 = (f32[256,512]{1,0:T(8,128)S(1)}, f32[256,512]{1,0:T(8,128)S(1)}, u32[]{:S(2)}, u32[]{:S(2)}) collective-permute-start(f32[256,512]{1,0:T(8,128)S(1)} %sweep.2.w_ref.refs_2_), channel_id=1, source_target_pairs={{0,2},{1,3},{2,4},{3,5},{4,6},{5,7},{6,0},{7,1},{8,10},{9,11},{10,... | collective-permute-start | bytes 1572872 | tf_op jit(solution)/shard_map/ppermute | solution.py:357
  62.5 20.7 %collective-permute-start.14 = (f32[256,512]{1,0:T(8,128)S(1)}, f32[256,512]{1,0:T(8,128)S(1)}, u32[]{:S(2)}, u32[]{:S(2)}) collective-permute-start(f32[256,512]{1,0:T(8,128)S(1)} %sweep.2.w_ref.refs_2_), channel_id=1, source_target_pairs={{0,6},{1,7},{2,0},{3,1},{4,2},{5,3},{6,4},{7,5},{8,14},{9,15},{10,... | collective-permute-start | bytes 1572872 | tf_op jit(solution)/shard_map/ppermute | solution.py:357
  66.0 17.1 %all-to-all-start.1 = ((f32[16,16,512]{2,1,0:T(8,128)}), f32[16,16,512]{2,1,0:T(8,128)S(1)}, u32[]{:S(2)}, u32[]{:S(2)}) async-start(f32[16,16,512]{2,1,0:T(8,128)} %bitcast.2), calls=%async_computation.1 | async-start | bytes 1048576 | tf_op jit(solution)/shard_map/all_to_all | solution.py:458
  74.2 17.9 %collective-permute-start.17 = (f32[256,512]{1,0:T(8,128)S(1)}, f32[256,512]{1,0:T(8,128)S(1)}, u32[]{:S(2)}, u32[]{:S(2)}) collective-permute-start(f32[256,512]{1,0:T(8,128)S(1)} %sweep.2.w_ref.refs_2_), channel_id=1, source_target_pairs={{0,1},{1,0},{2,3},{3,2},{4,5},{5,4},{6,7},{7,6},{8,9},{9,8},{10,11... | collective-permute-start | bytes 1572872 | tf_op jit(solution)/shard_map/ppermute | solution.py:353
  83.2 20.3 %collective-permute-start.21 = (f32[256,512]{1,0:T(8,128)S(1)}, f32[256,512]{1,0:T(8,128)S(1)}, u32[]{:S(2)}, u32[]{:S(2)}) collective-permute-start(f32[256,512]{1,0:T(8,128)S(1)} %collective-permute-done.14.refs_2_), channel_id=1, source_target_pairs={{0,1},{1,0},{2,3},{3,2},{4,5},{5,4},{6,7},{7,6},{8,9},{9,8},{10,11... | collective-permute-start | bytes 1572872 | tf_op jit(solution)/shard_map/ppermute | solution.py:353
  83.3 21.1 %collective-permute-start.22 = (f32[256,512]{1,0:T(8,128)S(1)}, f32[256,512]{1,0:T(8,128)S(1)}, u32[]{:S(2)}, u32[]{:S(2)}) collective-permute-start(f32[256,512]{1,0:T(8,128)S(1)} %collective-permute-done.15.refs_3_), channel_id=1, source_target_pairs={{0,1},{1,0},{2,3},{3,2},{4,5},{5,4},{6,7},{7,6},{8,9},{9,8},{10,11... | collective-permute-start | bytes 1572872 | tf_op jit(solution)/shard_map/ppermute | solution.py:353
  83.8 26.3 %collective-permute-start.16 = (f32[256,512]{1,0:T(8,128)S(1)}, f32[256,512]{1,0:T(8,128)S(1)}, u32[]{:S(2)}, u32[]{:S(2)}) collective-permute-start(f32[256,512]{1,0:T(8,128)S(1)} %sweep.2.w_ref.refs_2_), channel_id=1, source_target_pairs={{0,4},{1,5},{2,6},{3,7},{4,0},{5,1},{6,2},{7,3},{8,12},{9,13},{10,... | collective-permute-start | bytes 1572872 | tf_op jit(solution)/shard_map/ppermute | solution.py:357
  83.8 8.9 %collective-permute-start.20 = (f32[16,512]{1,0:T(8,128)S(1)}, f32[16,512]{1,0:T(8,128)S(1)}, u32[]{:S(2)}, u32[]{:S(2)}) collective-permute-start(f32[16,512]{1,0:T(8,128)S(1)} %fold.1.refs_0_), channel_id=1, source_target_pairs={{0,64},{8,72},{16,80},{24,88},{32,96},{40,104},{48,112},{56,120},{... | collective-permute-start | bytes 98312 | tf_op jit(solution)/shard_map/ppermute | solution.py:361
  97.5 9.3 %collective-permute-start.25 = (f32[64,512]{1,0:T(8,128)S(1)}, f32[64,512]{1,0:T(8,128)S(1)}, u32[]{:S(2)}, u32[]{:S(2)}) collective-permute-start(f32[64,512]{1,0:T(8,128)S(1)} %join.7.refs_0_), channel_id=1, source_target_pairs={{0,16},{8,24},{16,0},{24,8},{32,48},{40,56},{48,32},{56,40},{64,80... | collective-permute-start | bytes 393224 | tf_op jit(solution)/shard_map/ppermute | solution.py:361
  99.7 7.1 %collective-permute-start.24 = (f32[64,512]{1,0:T(8,128)S(1)}, f32[64,512]{1,0:T(8,128)S(1)}, u32[]{:S(2)}, u32[]{:S(2)}) collective-permute-start(f32[64,512]{1,0:T(8,128)S(1)} %join.7.refs_0_), channel_id=1, source_target_pairs={{0,8},{8,16},{16,24},{24,0},{32,40},{40,48},{48,56},{56,32},{64,72... | collective-permute-start | bytes 393224 | tf_op jit(solution)/shard_map/ppermute | solution.py:361
  115.5 36.8 %all-to-all-start.2 = ((f32[16,64,512]{2,1,0:T(8,128)}), f32[16,64,512]{2,1,0:T(8,128)S(1)}, u32[]{:S(2)}, u32[]{:S(2)}) async-start(f32[16,64,512]{2,1,0:T(8,128)} %bitcast.8), calls=%async_computation.2 | async-start | bytes 4194304 | tf_op jit(solution)/shard_map/all_to_all | solution.py:472
  122.5 16.4 %collective-permute-start.29 = (f32[256,512]{1,0:T(8,128)S(1)}, f32[256,512]{1,0:T(8,128)S(1)}, u32[]{:S(2)}, u32[]{:S(2)}) collective-permute-start(f32[256,512]{1,0:T(8,128)S(1)} %join.8.refs_0_), channel_id=1, source_target_pairs={{0,4},{1,5},{2,6},{3,7},{4,0},{5,1},{6,2},{7,3},{8,12},{9,13},{10,... | collective-permute-start | bytes 1572872 | tf_op jit(solution)/shard_map/ppermute | solution.py:361
  126.0 22.9 %collective-permute-start.28 = (f32[256,512]{1,0:T(8,128)S(1)}, f32[256,512]{1,0:T(8,128)S(1)}, u32[]{:S(2)}, u32[]{:S(2)}) collective-permute-start(f32[256,512]{1,0:T(8,128)S(1)} %join.8.refs_0_), channel_id=1, source_target_pairs={{0,2},{1,3},{2,4},{3,5},{4,6},{5,7},{6,0},{7,1},{8,10},{9,11},{10,... | collective-permute-start | bytes 1572872 | tf_op jit(solution)/shard_map/ppermute | solution.py:361
  126.0 22.9 %collective-permute-start.27 = (f32[256,512]{1,0:T(8,128)S(1)}, f32[256,512]{1,0:T(8,128)S(1)}, u32[]{:S(2)}, u32[]{:S(2)}) collective-permute-start(f32[256,512]{1,0:T(8,128)S(1)} %join.8.refs_0_), channel_id=1, source_target_pairs={{0,6},{1,7},{2,0},{3,1},{4,2},{5,3},{6,4},{7,5},{8,14},{9,15},{10,... | collective-permute-start | bytes 1572872 | tf_op jit(solution)/shard_map/ppermute | solution.py:361
  155.4 8.5 %collective-permute-start.33 = (f32[32,512]{1,0:T(8,128)S(1)}, f32[32,512]{1,0:T(8,128)S(1)}, u32[]{:S(2)}, u32[]{:S(2)}) collective-permute-start(f32[32,512]{1,0:T(8,128)S(1)} %get-tuple-element.72.refs_0_), channel_id=1, source_target_pairs={{0,64},{8,72},{16,80},{24,88},{32,96},{40,104},{48,112},{56,120},{... | collective-permute-start | bytes 196616 | tf_op jit(solution)/shard_map/ppermute | solution.py:361
  169.4 10.9 %collective-permute-start.39 = (f32[128,512]{1,0:T(8,128)S(1)}, f32[128,512]{1,0:T(8,128)S(1)}, u32[]{:S(2)}, u32[]{:S(2)}) collective-permute-start(f32[128,512]{1,0:T(8,128)S(1)} %get-tuple-element.74.refs_0_), channel_id=1, source_target_pairs={{0,16},{8,24},{16,0},{24,8},{32,48},{40,56},{48,32},{56,40},{64,80... | collective-permute-start | bytes 786440 | tf_op jit(solution)/shard_map/ppermute | solution.py:361
  169.7 10.8 %collective-permute-start.38 = (f32[128,512]{1,0:T(8,128)S(1)}, f32[128,512]{1,0:T(8,128)S(1)}, u32[]{:S(2)}, u32[]{:S(2)}) collective-permute-start(f32[128,512]{1,0:T(8,128)S(1)} %get-tuple-element.74.refs_0_), channel_id=1, source_target_pairs={{0,8},{8,16},{16,24},{24,0},{32,40},{40,48},{48,56},{56,32},{64,72... | collective-permute-start | bytes 786440 | tf_op jit(solution)/shard_map/ppermute | solution.py:361
  170.9 12.2 %collective-permute-start.37 = (f32[128,512]{1,0:T(8,128)S(1)}, f32[128,512]{1,0:T(8,128)S(1)}, u32[]{:S(2)}, u32[]{:S(2)}) collective-permute-start(f32[128,512]{1,0:T(8,128)S(1)} %get-tuple-element.74.refs_0_), channel_id=1, source_target_pairs={{0,24},{8,0},{16,8},{24,16},{32,56},{40,32},{48,40},{56,48},{64,88... | collective-permute-start | bytes 786440 | tf_op jit(solution)/shard_map/ppermute | solution.py:361
  171.7 11.4 %collective-permute-start.42 = (f32[128,512]{1,0:T(8,128)S(1)}, f32[128,512]{1,0:T(8,128)S(1)}, u32[]{:S(2)}, u32[]{:S(2)}) collective-permute-start(f32[128,512]{1,0:T(8,128)S(1)} %get-tuple-element.75.refs_4_), channel_id=1, source_target_pairs={{0,64},{8,72},{16,80},{24,88},{32,96},{40,104},{48,112},{56,120},{... | collective-permute-start | bytes 786440 | tf_op jit(solution)/shard_map/ppermute | solution.py:361
  173.5 10.9 %collective-permute-start.41 = (f32[128,512]{1,0:T(8,128)S(1)}, f32[128,512]{1,0:T(8,128)S(1)}, u32[]{:S(2)}, u32[]{:S(2)}) collective-permute-start(f32[128,512]{1,0:T(8,128)S(1)} %get-tuple-element.75.refs_4_), channel_id=1, source_target_pairs={{0,32},{8,40},{16,48},{24,56},{32,64},{40,72},{48,80},{56,88},{64,... | collective-permute-start | bytes 786440 | tf_op jit(solution)/shard_map/ppermute | solution.py:361
  (30 other events, 117.7 us)

commit v5 on v3

--- a/solution.py
+++ b/solution.py
@@ -171,7 +171,7 @@
     )(*ins)
 
 
-def gram_h_kernel(h_ref, mine_ref, theirs_ref, tmp):
+def gram_h_kernel(h_ref, _, mine_ref, theirs_ref, tmp):
     z, y, _, c = place()
     h = h_ref[...]
     tmp[...] = h.T
@@ -182,42 +182,41 @@
     theirs_ref[...] = both[16:] * first + both[:16] * (1.0 - first)
 
 
-def gram_h(h):
+def gram_h(h, hold):
     return pl.pallas_call(
         gram_h_kernel,
         out_shape=[sds(16, 512)] * 2,
-        in_specs=[VM],
+        in_specs=[VM] * 2,
         out_specs=[VM] * 2,
         scratch_shapes=[pltpu.VMEM((512, 1024), f32)],
-        compiler_params=params(12),
+        compiler_params=params(14),
         cost_estimate=cost(6 * 512 * 32 * 1024, 4 << 20),
         name="gram_h",
-    )(h)
-
-
-def gram_w_kernel(w_ref, mine_ref, theirs_ref, tmp):
-    z, y, _, c = place()
-    w = w_ref[...]
-    tmp[...] = dot3(*split(w.T), *split(w))
+    )(h, hold)
+
+
+def gram_w_kernel(w_ref, ws_ref, *refs):
+    outs, tmp = refs[:4], refs[4]
+    _, _, x, c = place()
+    right = jnp.concatenate([w_ref[...], ws_ref[...]], axis=0)
+    tmp[...] = right.T
+    rows = [tmp[pl.ds(pl.multiple_of(128 * ((x + r) % 4) + 64 * c, 64), 64), :] for r in REL]
+    out = dot3(*split(jnp.concatenate(rows, axis=0)), *split(right))
     for k in range(4):
-        for m in range(4):
-            s = 4 * ((z + REL[k]) % 4) + (y + REL[m]) % 4
-            at = 64 * k + 16 * m
-            mine_ref[at : at + 16, :] = tmp[pl.ds(pl.multiple_of(32 * s + 16 * c, 16), 16), :]
-            theirs_ref[at : at + 16, :] = tmp[pl.ds(pl.multiple_of(32 * s + 16 * (1 - c), 16), 16), :]
-
-
-def gram_w(w):
+        outs[k][...] = out[64 * k : 64 * (k + 1)]
+
+
+def gram_w(w, ws):
     return pl.pallas_call(
         gram_w_kernel,
-        out_shape=[sds(256, 512)] * 2,
-        in_specs=[VM],
-        out_specs=[VM] * 2,
+        out_shape=[sds(64, 512)] * 4,
+        in_specs=[VM] * 2,
+        out_specs=[VM] * 4,
         scratch_shapes=[pltpu.VMEM((512, 512), f32)],
         compiler_params=params(10),
-        cost_estimate=cost(6 * 512 * 512 * 256, 4 << 20),
+        cost_estimate=cost(6 * 256 * 512 * 512, 4 << 20),
         name="gram_w",
-    )(w)
+    )(w, ws)
 
 
 def sweep_kernel(axis, product, start, mine, theirs, *refs):
@@ -233,6 +232,10 @@
     for t, piece in enumerate((mine, theirs)):
         cc = c if t == 0 else 1 - c
         for j in range(4):
+            if axis == "samp":
+                row = 128 * ((x + REL[j]) % 4) + 64 * cc
+                g[pl.ds(pl.multiple_of(row, 64), 64), :] = piece[64 * j : 64 * j + 64, :]
+                continue
             for i in range(4):
                 row = 32 * (4 * ((z + REL[i]) % 4) + (y + REL[j]) % 4) + 16 * cc
                 g[pl.ds(pl.multiple_of(row, 16), 16), :] = piece[64 * j + 16 * i : 64 * j + 16 * i + 16, :]
@@ -394,24 +397,20 @@
     total = refs[0][...]
     for r in refs[1:n]:
         total = total + r[...]
-    outs = refs[n:]
-    rows = total.shape[0] // len(outs)
-    for k, out in enumerate(outs):
-        out[...] = total[rows * k : rows * (k + 1)]
-
-
-def add(parts, nout=1):
+    refs[-1][...] = total
+
+
+def add(parts):
     rows = parts[0].shape[0]
-    out = pl.pallas_call(
+    return pl.pallas_call(
         functools.partial(add_kernel, len(parts)),
-        out_shape=[sds(rows // nout, 512)] * nout,
+        out_shape=sds(rows, 512),
         in_specs=[VM] * len(parts),
-        out_specs=[VM] * nout,
+        out_specs=VM,
         compiler_params=params(4),
         cost_estimate=cost(rows * 512 * len(parts), rows * 4096 * len(parts)),
         name="add",
     )(*parts)
-    return out if nout > 1 else out[0]
 
 
 def deal(pieces, axis, table):
@@ -424,7 +423,7 @@
 
 
 def shards(spectra, w_start, h_start):
-    g_mine, g_theirs = gram_h(h_start)
+    g_mine, g_theirs = gram_h(h_start, spectra)
     strip = add([g_mine, swap(g_theirs)])
 
     a1, hh, hl = prod(spectra, after(h_start, strip), (0, 1), True)
@@ -442,30 +441,26 @@
     (w,) = sweep(product, w0, "col", 256, (part, swap(part)), 1)
 
     ws = swap(w)
-    near_p, near_m = send(w, "col", X, 3), send(w, "col", X, 1)
-
-    g_mine, g_theirs = gram_w(w)
-    flipped = flip(after(spectra, g_theirs))
-    strips = add([g_mine, after(swap(g_theirs), *flipped)], 4)
-    strips = deal(strips, "samp", Z)
-    carry = back(flipped, (w, ws), ((0, False), (0, True)))
-    strips = add([after(strips[0], carry[0])] + strips[1:], 4)
-    near_p, near_m = after(near_p, *strips), after(near_m, *strips)
-    far = send(after(w, near_p, near_m), "col", X, 2)
+    slices = gram_w(w, ws)
+    flipped = flip(after(spectra, slices[0]))
+    slices = deal(slices, "col", X)
+    part = add([after(slices[0], *flipped)] + slices[1:])
+    late = after(w, part)
+    near_p, near_m, far = send(late, "col", X, 3), send(late, "col", X, 1), send(late, "col", X, 2)
+    carry = back(flipped, (w, after(ws, part)), ((0, False), (0, True)))
+    part = add([after(part, carry[0])] + fetch(part, "samp", Y))
+    near_p, near_m = after(near_p, part), after(near_m, part)
     sib_p, sib_m = swap(near_p), swap(near_m)
-    strips = deal(strips, "samp", Y)
-    carry = back(flipped, (near_p, near_m), ((1, False), (3, False)), (after(carry[0], *strips), carry[1]))
-    strip = add([after(strips[0], carry[0])] + strips[1:])
-    carry = back(flipped, (sib_p, sib_m), ((1, True), (3, True)), (after(carry[0], strip), carry[1]))
-    part = join([after(strip, carry[0])] + fetch(strip, "samp", Z))
+    carry = back(flipped, (near_p, near_m), ((1, False), (3, False)), carry)
+    part = add([after(part, carry[0])] + fetch(part, "samp", Z))
+    carry = back(flipped, (sib_p, sib_m), ((1, True), (3, True)), carry)
     sib_f = swap(after(far, part))
     carry = (after(carry[0], part), carry[1])
     back_sum, w_out = back(flipped, (far, sib_f), ((2, False), (2, True)), carry, True)
 
     product = lax.all_to_all(back_sum, "samp", 0, 0, tiled=True)
     part = after(part, back_sum)
-    part = add([part] + fetch(part, "col", X))
-    part = join([part] + fetch(part, "samp", Y))
+    part = join([part] + fetch(part, "col", X))
     ha, hb = sweep(product, h_start, "samp", 64, (part, swap(part)), 2)
 
     row_a, row_b = join([ha] + fetch(ha, "samp", Z) + [hb] + fetch(hb, "samp", Y), 2)

time: 186 us -> 186 us (level)
  waiting for transfers between devices: 74 us -> 80 us
  starting transfers between devices: 69 us -> 63.2 us
    all_to_all x1, waiting for transfers between devices: 0.01 us -> 16.4 us  [shards(): product = lax.all_to_all(back_sum, 'samp', 0, 0, tiled=True)]
    ppermute x30, waiting for transfers between devices: 53.1 us -> 45.9 us  [fetch(): return [lax.ppermute(a, axis, table[(4 - r) % 4]) for r in REL[1:]]]
    ppermute x9 -> x6, starting transfers between devices: 12.5 us -> 7.64 us  [send(): return lax.ppermute(a, axis, table[r])]
    ppermute x9 -> x6, waiting for transfers between devices: 9.29 us -> 6.01 us  [send(): return lax.ppermute(a, axis, table[r])]
    ppermute x30, starting transfers between devices: 43.7 us -> 41.6 us  [fetch(): return [lax.ppermute(a, axis, table[(4 - r) % 4]) for r in REL[1:]]]
    ppermute x10 -> x9, waiting for transfers between devices: 5.52 us -> 5.87 us  [swap(): return lax.ppermute(a, 'col', CORE[0])]
    unnamed x14 -> x12, local copies, waits for them, and re-layouts: 7.48 us -> 7.48 us
  transfers between devices with their start and end apart: 51 -> 47, of which waited for: 25 -> 26; matrix products, arithmetic and copies ran while one was open for 0% -> 0% of each run, Pallas kernels for 10% -> 10%
where the time goes in v5:
time: 186 us; the launch traced here: 185 us
  waiting for transfers between devices  80 us (43%)
  starting transfers between devices  63.2 us (34%)
  Pallas kernels  33.4 us (18%)
  local copies, waits for them, and re-layouts  7.48 us (4%)
    ppermute x30, waiting for transfers between devices, fetch(): return [lax.ppermute(a, axis, table[(4 - r) % 4]) for r in REL[1:]]  45.9 us
    ppermute x30, starting transfers between devices, fetch(): return [lax.ppermute(a, axis, table[(4 - r) % 4]) for r in REL[1:]]  41.6 us
    all_to_all x1, waiting for transfers between devices, shards(): product = lax.all_to_all(back_sum, 'samp', 0, 0, tiled=True)  16.4 us
    pallas_call x4, Pallas kernels, back(): pl.pallas_call(functools.partial(back_kernel, tuple(chunks), bool(carry))...  9.05 us
    all_to_all x1, starting transfers between devices, shards(): product = lax.all_to_all(back_sum, 'samp', 0, 0, tiled=True)  8.17 us
    pallas_call x4, Pallas kernels, prod(): pl.pallas_call(functools.partial(prod_kernel, chunks, sibling, first, rec...  8.14 us
    ppermute x6, starting transfers between devices, send(): return lax.ppermute(a, axis, table[r])  7.64 us
    unnamed x12, local copies, waits for them, and re-layouts  7.48 us
  transfers between devices with their start and end apart: 47, of which 26 were waited for; matrix products, arithmetic and copies ran while one was open for 0% of the time, Pallas kernels for 10%

profile of v5, /device:TPU:24, one launch (start us, length us, event | category | flops | bytes accessed | tf_op | source)
XLA Modules:
  0.0 185.0 jit_solution(6037988617311063746)
XLA Ops:
  0.6 3.4 %copy-done = f32[2048,1024]{1,0:T(8,128)S(1)} copy-done((f32[2048,1024]{1,0:T(8,128)S(1)}, f32[2048,1024]{1,0:T(8,128)}, u32[]{:S(2)}) %copy-start) | copy-done | bytes 8388632
  8.2 2.8 %collective-permute-start.1 = (f32[16,512]{1,0:T(8,128)S(1)}, f32[16,512]{1,0:T(8,128)S(1)}, u32[]{:S(2)}, u32[]{:S(2)}) collective-permute-start(f32[16,512]{1,0:T(8,128)S(1)} %add.5.refs_0_), channel_id=1, source_target_pairs={{0,6},{1,7},{2,0},{3,1},{4,2},{5,3},{6,4},{7,5},{8,14},{9,15},{10,... | collective-permute-start | bytes 98312 | tf_op jit(solution)/shard_map/ppermute | solution.py:366
  21.0 2.8 %prod.7 = f32[1024,512]{1,0:T(8,128)} custom-call(f32[2048,1024]{1,0:T(8,128)S(1)} %copy-done, bf16[1024,512]{1,0:T(8,128)(2,1)S(1)} %get-tuple-element.48.refs_1_, bf16[1024,512]{1,0:T(8,128)(2,1)S(1)} %get-tuple-element.49.refs_2_, f32[512,512]{1,0:T(8,128)S(1)} %collective-permute-done.4.refs_3_, f32[512,512]{1,0:T(8,128)S(1)} %prod.6.refs_4_), custom_call_target="tpu_custom_call" | custom-call | flops 1610612736 | bytes 6291456 | tf_op jit(solution)/shard_map/prod/pallas_call | solution.py:89
  23.7 4.5 %all-to-all-start = ((f32[4,256,512]{2,1,0:T(8,128)}), f32[4,256,512]{2,1,0:T(8,128)S(1)}, u32[]{:S(2)}, u32[]{:S(2)}) async-start(f32[4,256,512]{2,1,0:T(8,128)} %bitcast), calls=%async_computation | async-start | bytes 4194304 | tf_op jit(solution)/shard_map/all_to_all | solution.py:437
  28.2 4.0 %collective-permute-start.6 = (f32[16,512]{1,0:T(8,128)S(1)}, f32[16,512]{1,0:T(8,128)S(1)}, u32[]{:S(2)}, u32[]{:S(2)}) collective-permute-start(f32[16,512]{1,0:T(8,128)S(1)} %add.6.refs_0_), channel_id=1, source_target_pairs={{0,96},{8,104},{16,112},{24,120},{32,0},{40,8},{48,16},{56,24},{64... | collective-permute-start | bytes 98312 | tf_op jit(solution)/shard_map/ppermute | solution.py:366
  34.1 3.3 %collective-permute-done.7.refs_2_ = f32[16,512]{1,0:T(8,128)S(1)} collective-permute-done((f32[16,512]{1,0:T(8,128)S(1)}, f32[16,512]{1,0:T(8,128)S(1)}, u32[]{:S(2)}, u32[]{:S(2)}) %collective-permute-start.7) | collective-permute-done | bytes 32800 | tf_op jit(solution)/shard_map/ppermute | solution.py:366
  49.0 5.8 %all-to-all-done = f32[4,256,512]{2,1,0:T(8,128)S(1)} async-done(((f32[4,256,512]{2,1,0:T(8,128)}), f32[4,256,512]{2,1,0:T(8,128)S(1)}, u32[]{:S(2)}, u32[]{:S(2)}) %all-to-all-start) | async-done | bytes 2097184 | tf_op jit(solution)/shard_map/all_to_all | solution.py:437
  56.0 4.1 %sweep.2.w_ref.refs_2_ = f32[256,512]{1,0:T(8,128)S(1)} custom-call(f32[1024,512]{1,0:T(8,128)S(1)} %bitcast.7, f32[256,512]{1,0:T(8,128)S(1)} %copy-done.3, f32[256,512]{1,0:T(8,128)S(1)} %join.5.mine, f32[256,512]{1,0:T(8,128)S(1)} %collective-permute-done.12.theirs), custom_call_target="tpu_custom_call" | custom-call | flops 4831838208 | bytes 4194304 | tf_op jit(solution)/shard_map/sweep/pallas_call | solution.py:271
  66.3 3.4 %flip.1 = (bf16[16,1024,128]{2,1,0:T(8,128)(2,1)S(1)}, bf16[16,1024,128]{2,1,0:T(8,128)(2,1)S(1)}) custom-call(f32[2048,1024]{1,0:T(8,128)S(1)} %bitcast.5), custom_call_target="tpu_custom_call" | custom-call | flops 16777216 | bytes 16777216 | tf_op jit(solution)/shard_map/flip/pallas_call | solution.py:111
  84.5 4.3 %collective-permute-done.20.refs_3_ = f32[64,512]{1,0:T(8,128)S(1)} collective-permute-done((f32[64,512]{1,0:T(8,128)S(1)}, f32[64,512]{1,0:T(8,128)S(1)}, u32[]{:S(2)}, u32[]{:S(2)}) %collective-permute-start.20) | collective-permute-done | bytes 131104 | tf_op jit(solution)/shard_map/ppermute | solution.py:366
  88.8 4.1 %collective-permute-start.23 = (f32[64,512]{1,0:T(8,128)S(1)}, f32[64,512]{1,0:T(8,128)S(1)}, u32[]{:S(2)}, u32[]{:S(2)}) collective-permute-start(f32[64,512]{1,0:T(8,128)S(1)} %add.8.refs_0_), channel_id=1, source_target_pairs={{0,96},{8,104},{16,112},{24,120},{32,0},{40,8},{48,16},{56,24},{64... | collective-permute-start | bytes 393224 | tf_op jit(solution)/shard_map/ppermute | solution.py:366
  94.8 2.9 %collective-permute-done.21.refs_2_ = f32[256,512]{1,0:T(8,128)S(1)} collective-permute-done((f32[256,512]{1,0:T(8,128)S(1)}, f32[256,512]{1,0:T(8,128)S(1)}, u32[]{:S(2)}, u32[]{:S(2)}) %collective-permute-start.21) | collective-permute-done | bytes 524320 | tf_op jit(solution)/shard_map/ppermute | solution.py:362
  106.7 8.2 %all-to-all-start.1 = ((f32[16,64,512]{2,1,0:T(8,128)}), f32[16,64,512]{2,1,0:T(8,128)S(1)}, u32[]{:S(2)}, u32[]{:S(2)}) async-start(f32[16,64,512]{2,1,0:T(8,128)} %bitcast.8), calls=%async_computation.1 | async-start | bytes 4194304 | tf_op jit(solution)/shard_map/all_to_all | solution.py:461
  114.9 3.7 %collective-permute-start.29 = (f32[64,512]{1,0:T(8,128)S(1)}, f32[64,512]{1,0:T(8,128)S(1)}, u32[]{:S(2)}, u32[]{:S(2)}) collective-permute-start(f32[64,512]{1,0:T(8,128)S(1)} %add.9.refs_0_), channel_id=1, source_target_pairs={{0,6},{1,7},{2,0},{3,1},{4,2},{5,3},{6,4},{7,5},{8,14},{9,15},{10,... | collective-permute-start | bytes 393224 | tf_op jit(solution)/shard_map/ppermute | solution.py:366
  121.4 6.2 %collective-permute-done.30.refs_2_ = f32[64,512]{1,0:T(8,128)S(1)} collective-permute-done((f32[64,512]{1,0:T(8,128)S(1)}, f32[64,512]{1,0:T(8,128)S(1)}, u32[]{:S(2)}, u32[]{:S(2)}) %collective-permute-start.30) | collective-permute-done | bytes 131104 | tf_op jit(solution)/shard_map/ppermute | solution.py:366
  129.6 16.4 %all-to-all-done.1 = f32[16,64,512]{2,1,0:T(8,128)S(1)} async-done(((f32[16,64,512]{2,1,0:T(8,128)}), f32[16,64,512]{2,1,0:T(8,128)S(1)}, u32[]{:S(2)}, u32[]{:S(2)}) %all-to-all-start.1) | async-done | bytes 2097184 | tf_op jit(solution)/shard_map/all_to_all | solution.py:461
  146.0 3.0 %sweep.3 = (f32[32,512]{1,0:T(8,128)S(1)}, f32[32,512]{1,0:T(8,128)S(1)}) custom-call(f32[1024,512]{1,0:T(8,128)S(1)} %bitcast.6, f32[1024,512]{1,0:T(8,128)} %start.1, f32[256,512]{1,0:T(8,128)S(1)} %join.6.mine, f32[256,512]{1,0:T(8,128)S(1)} %collective-permute-done.32.theirs), custom_call_target="tpu_custom_call" | custom-call | flops 1207959552 | bytes 4194304 | tf_op jit(solution)/shard_map/sweep/pallas_call | solution.py:271
  151.1 2.7 %collective-permute-start.35 = (f32[32,512]{1,0:T(8,128)S(1)}, f32[32,512]{1,0:T(8,128)S(1)}, u32[]{:S(2)}, u32[]{:S(2)}) collective-permute-start(f32[32,512]{1,0:T(8,128)S(1)} %get-tuple-element.78.refs_0_), channel_id=1, source_target_pairs={{0,64},{8,72},{16,80},{24,88},{32,96},{40,104},{48,112},{56,120},{... | collective-permute-start | bytes 196616 | tf_op jit(solution)/shard_map/ppermute | solution.py:366
  153.8 3.2 %collective-permute-start.37 = (f32[32,512]{1,0:T(8,128)S(1)}, f32[32,512]{1,0:T(8,128)S(1)}, u32[]{:S(2)}, u32[]{:S(2)}) collective-permute-start(f32[32,512]{1,0:T(8,128)S(1)} %get-tuple-element.79.refs_4_), channel_id=1, source_target_pairs={{0,8},{8,16},{16,24},{24,0},{32,40},{40,48},{48,56},{56,32},{64,72... | collective-permute-start | bytes 196616 | tf_op jit(solution)/shard_map/ppermute | solution.py:366
  157.1 2.9 %collective-permute-done.36.refs_5_ = f32[32,512]{1,0:T(8,128)S(1)} collective-permute-done((f32[32,512]{1,0:T(8,128)S(1)}, f32[32,512]{1,0:T(8,128)S(1)}, u32[]{:S(2)}, u32[]{:S(2)}) %collective-permute-start.36) | collective-permute-done | bytes 65568 | tf_op jit(solution)/shard_map/ppermute | solution.py:366
  160.0 2.9 %collective-permute-done.38.refs_7_ = f32[32,512]{1,0:T(8,128)S(1)} collective-permute-done((f32[32,512]{1,0:T(8,128)S(1)}, f32[32,512]{1,0:T(8,128)S(1)}, u32[]{:S(2)}, u32[]{:S(2)}) %collective-permute-start.38) | collective-permute-done | bytes 65568 | tf_op jit(solution)/shard_map/ppermute | solution.py:366
  163.0 3.2 %collective-permute-start.40 = (f32[128,512]{1,0:T(8,128)S(1)}, f32[128,512]{1,0:T(8,128)S(1)}, u32[]{:S(2)}, u32[]{:S(2)}) collective-permute-start(f32[128,512]{1,0:T(8,128)S(1)} %get-tuple-element.80.refs_0_), channel_id=1, source_target_pairs={{0,8},{8,16},{16,24},{24,0},{32,40},{40,48},{48,56},{56,32},{64,72... | collective-permute-start | bytes 786440 | tf_op jit(solution)/shard_map/ppermute | solution.py:366
  168.2 7.4 %collective-permute-done.39.refs_1_ = f32[128,512]{1,0:T(8,128)S(1)} collective-permute-done((f32[128,512]{1,0:T(8,128)S(1)}, f32[128,512]{1,0:T(8,128)S(1)}, u32[]{:S(2)}, u32[]{:S(2)}) %collective-permute-start.39) | collective-permute-done | bytes 262176 | tf_op jit(solution)/shard_map/ppermute | solution.py:366
  176.4 7.1 %collective-permute-done.44.refs_7_ = f32[128,512]{1,0:T(8,128)S(1)} collective-permute-done((f32[128,512]{1,0:T(8,128)S(1)}, f32[128,512]{1,0:T(8,128)S(1)}, u32[]{:S(2)}, u32[]{:S(2)}) %collective-permute-start.44) | collective-permute-done | bytes 262176 | tf_op jit(solution)/shard_map/ppermute | solution.py:366
  (107 shorter events, 71.9 us)
Async XLA Ops:
  8.2 6.9 %collective-permute-start.1 = (f32[16,512]{1,0:T(8,128)S(1)}, f32[16,512]{1,0:T(8,128)S(1)}, u32[]{:S(2)}, u32[]{:S(2)}) collective-permute-start(f32[16,512]{1,0:T(8,128)S(1)} %add.5.refs_0_), channel_id=1, source_target_pairs={{0,6},{1,7},{2,0},{3,1},{4,2},{5,3},{6,4},{7,5},{8,14},{9,15},{10,... | collective-permute-start | bytes 98312 | tf_op jit(solution)/shard_map/ppermute | solution.py:366
  23.7 31.1 %all-to-all-start = ((f32[4,256,512]{2,1,0:T(8,128)}), f32[4,256,512]{2,1,0:T(8,128)S(1)}, u32[]{:S(2)}, u32[]{:S(2)}) async-start(f32[4,256,512]{2,1,0:T(8,128)} %bitcast), calls=%async_computation | async-start | bytes 4194304 | tf_op jit(solution)/shard_map/all_to_all | solution.py:437
  38.0 7.2 %collective-permute-start.11 = (f32[64,512]{1,0:T(8,128)S(1)}, f32[64,512]{1,0:T(8,128)S(1)}, u32[]{:S(2)}, u32[]{:S(2)}) collective-permute-start(f32[64,512]{1,0:T(8,128)S(1)} %join.4.refs_0_), channel_id=1, source_target_pairs={{0,16},{8,24},{16,0},{24,8},{32,48},{40,56},{48,32},{56,40},{64,80... | collective-permute-start | bytes 393224 | tf_op jit(solution)/shard_map/ppermute | solution.py:366
  63.0 6.8 %collective-permute-start.14 = (f32[64,512]{1,0:T(8,128)S(1)}, f32[64,512]{1,0:T(8,128)S(1)}, u32[]{:S(2)}, u32[]{:S(2)}) collective-permute-start(f32[64,512]{1,0:T(8,128)S(1)} %get-tuple-element.58), channel_id=1, source_target_pairs={{0,2},{1,3},{2,4},{3,5},{4,6},{5,7},{6,0},{7,1},{8,10},{9,11},{10,... | collective-permute-start | bytes 393224 | tf_op jit(solution)/shard_map/ppermute | solution.py:362
  63.6 8.3 %collective-permute-start.15 = (f32[64,512]{1,0:T(8,128)S(1)}, f32[64,512]{1,0:T(8,128)S(1)}, u32[]{:S(2)}, u32[]{:S(2)}) collective-permute-start(f32[64,512]{1,0:T(8,128)S(1)} %get-tuple-element.59), channel_id=1, source_target_pairs={{0,6},{1,7},{2,0},{3,1},{4,2},{5,3},{6,4},{7,5},{8,14},{9,15},{10,... | collective-permute-start | bytes 393224 | tf_op jit(solution)/shard_map/ppermute | solution.py:362
  72.8 20.1 %collective-permute-start.22 = (f32[256,512]{1,0:T(8,128)S(1)}, f32[256,512]{1,0:T(8,128)S(1)}, u32[]{:S(2)}, u32[]{:S(2)}) collective-permute-start(f32[256,512]{1,0:T(8,128)S(1)} %sweep.2.w_ref.refs_2_), channel_id=1, source_target_pairs={{0,2},{1,3},{2,4},{3,5},{4,6},{5,7},{6,0},{7,1},{8,10},{9,11},{10,... | collective-permute-start | bytes 1572872 | tf_op jit(solution)/shard_map/ppermute | solution.py:362
  73.6 24.1 %collective-permute-start.21 = (f32[256,512]{1,0:T(8,128)S(1)}, f32[256,512]{1,0:T(8,128)S(1)}, u32[]{:S(2)}, u32[]{:S(2)}) collective-permute-start(f32[256,512]{1,0:T(8,128)S(1)} %sweep.2.w_ref.refs_2_), channel_id=1, source_target_pairs={{0,6},{1,7},{2,0},{3,1},{4,2},{5,3},{6,4},{7,5},{8,14},{9,15},{10,... | collective-permute-start | bytes 1572872 | tf_op jit(solution)/shard_map/ppermute | solution.py:362
  76.9 23.8 %collective-permute-start.17 = (f32[256,512]{1,0:T(8,128)S(1)}, f32[256,512]{1,0:T(8,128)S(1)}, u32[]{:S(2)}, u32[]{:S(2)}) collective-permute-start(f32[256,512]{1,0:T(8,128)S(1)} %sweep.2.w_ref.refs_2_), channel_id=1, source_target_pairs={{0,4},{1,5},{2,6},{3,7},{4,0},{5,1},{6,2},{7,3},{8,12},{9,13},{10,... | collective-permute-start | bytes 1572872 | tf_op jit(solution)/shard_map/ppermute | solution.py:362
  77.9 6.5 %collective-permute-start.19 = (f32[64,512]{1,0:T(8,128)S(1)}, f32[64,512]{1,0:T(8,128)S(1)}, u32[]{:S(2)}, u32[]{:S(2)}) collective-permute-start(f32[64,512]{1,0:T(8,128)S(1)} %add.7.refs_0_), channel_id=1, source_target_pairs={{0,8},{8,16},{16,24},{24,0},{32,40},{40,48},{48,56},{56,32},{64,72... | collective-permute-start | bytes 393224 | tf_op jit(solution)/shard_map/ppermute | solution.py:366
  88.8 8.9 %collective-permute-start.23 = (f32[64,512]{1,0:T(8,128)S(1)}, f32[64,512]{1,0:T(8,128)S(1)}, u32[]{:S(2)}, u32[]{:S(2)}) collective-permute-start(f32[64,512]{1,0:T(8,128)S(1)} %add.8.refs_0_), channel_id=1, source_target_pairs={{0,96},{8,104},{16,112},{24,120},{32,0},{40,8},{48,16},{56,24},{64... | collective-permute-start | bytes 393224 | tf_op jit(solution)/shard_map/ppermute | solution.py:366
  92.9 7.7 %collective-permute-start.24 = (f32[64,512]{1,0:T(8,128)S(1)}, f32[64,512]{1,0:T(8,128)S(1)}, u32[]{:S(2)}, u32[]{:S(2)}) collective-permute-start(f32[64,512]{1,0:T(8,128)S(1)} %add.8.refs_0_), channel_id=1, source_target_pairs={{0,32},{8,40},{16,48},{24,56},{32,64},{40,72},{48,80},{56,88},{64,... | collective-permute-start | bytes 393224 | tf_op jit(solution)/shard_map/ppermute | solution.py:366
  92.9 7.7 %collective-permute-start.25 = (f32[64,512]{1,0:T(8,128)S(1)}, f32[64,512]{1,0:T(8,128)S(1)}, u32[]{:S(2)}, u32[]{:S(2)}) collective-permute-start(f32[64,512]{1,0:T(8,128)S(1)} %add.8.refs_0_), channel_id=1, source_target_pairs={{0,64},{8,72},{16,80},{24,88},{32,96},{40,104},{48,112},{56,120},{... | collective-permute-start | bytes 393224 | tf_op jit(solution)/shard_map/ppermute | solution.py:366
  106.7 39.3 %all-to-all-start.1 = ((f32[16,64,512]{2,1,0:T(8,128)}), f32[16,64,512]{2,1,0:T(8,128)S(1)}, u32[]{:S(2)}, u32[]{:S(2)}) async-start(f32[16,64,512]{2,1,0:T(8,128)} %bitcast.8), calls=%async_computation.1 | async-start | bytes 4194304 | tf_op jit(solution)/shard_map/all_to_all | solution.py:461
  114.9 6.5 %collective-permute-start.29 = (f32[64,512]{1,0:T(8,128)S(1)}, f32[64,512]{1,0:T(8,128)S(1)}, u32[]{:S(2)}, u32[]{:S(2)}) collective-permute-start(f32[64,512]{1,0:T(8,128)S(1)} %add.9.refs_0_), channel_id=1, source_target_pairs={{0,6},{1,7},{2,0},{3,1},{4,2},{5,3},{6,4},{7,5},{8,14},{9,15},{10,... | collective-permute-start | bytes 393224 | tf_op jit(solution)/shard_map/ppermute | solution.py:366
  118.5 9.1 %collective-permute-start.30 = (f32[64,512]{1,0:T(8,128)S(1)}, f32[64,512]{1,0:T(8,128)S(1)}, u32[]{:S(2)}, u32[]{:S(2)}) collective-permute-start(f32[64,512]{1,0:T(8,128)S(1)} %add.9.refs_0_), channel_id=1, source_target_pairs={{0,2},{1,3},{2,4},{3,5},{4,6},{5,7},{6,0},{7,1},{8,10},{9,11},{10,... | collective-permute-start | bytes 393224 | tf_op jit(solution)/shard_map/ppermute | solution.py:366
  118.5 9.1 %collective-permute-start.31 = (f32[64,512]{1,0:T(8,128)S(1)}, f32[64,512]{1,0:T(8,128)S(1)}, u32[]{:S(2)}, u32[]{:S(2)}) collective-permute-start(f32[64,512]{1,0:T(8,128)S(1)} %add.9.refs_0_), channel_id=1, source_target_pairs={{0,4},{1,5},{2,6},{3,7},{4,0},{5,1},{6,2},{7,3},{8,12},{9,13},{10,... | collective-permute-start | bytes 393224 | tf_op jit(solution)/shard_map/ppermute | solution.py:366
  149.0 8.0 %collective-permute-start.33 = (f32[32,512]{1,0:T(8,128)S(1)}, f32[32,512]{1,0:T(8,128)S(1)}, u32[]{:S(2)}, u32[]{:S(2)}) collective-permute-start(f32[32,512]{1,0:T(8,128)S(1)} %get-tuple-element.78.refs_0_), channel_id=1, source_target_pairs={{0,96},{8,104},{16,112},{24,120},{32,0},{40,8},{48,16},{56,24},{64... | collective-permute-start | bytes 196616 | tf_op jit(solution)/shard_map/ppermute | solution.py:366
  150.1 7.0 %collective-permute-start.34 = (f32[32,512]{1,0:T(8,128)S(1)}, f32[32,512]{1,0:T(8,128)S(1)}, u32[]{:S(2)}, u32[]{:S(2)}) collective-permute-start(f32[32,512]{1,0:T(8,128)S(1)} %get-tuple-element.78.refs_0_), channel_id=1, source_target_pairs={{0,32},{8,40},{16,48},{24,56},{32,64},{40,72},{48,80},{56,88},{64,... | collective-permute-start | bytes 196616 | tf_op jit(solution)/shard_map/ppermute | solution.py:366
  162.9 12.7 %collective-permute-start.39 = (f32[128,512]{1,0:T(8,128)S(1)}, f32[128,512]{1,0:T(8,128)S(1)}, u32[]{:S(2)}, u32[]{:S(2)}) collective-permute-start(f32[128,512]{1,0:T(8,128)S(1)} %get-tuple-element.80.refs_0_), channel_id=1, source_target_pairs={{0,24},{8,0},{16,8},{24,16},{32,56},{40,32},{48,40},{56,48},{64,88... | collective-permute-start | bytes 786440 | tf_op jit(solution)/shard_map/ppermute | solution.py:366
  163.0 12.6 %collective-permute-start.40 = (f32[128,512]{1,0:T(8,128)S(1)}, f32[128,512]{1,0:T(8,128)S(1)}, u32[]{:S(2)}, u32[]{:S(2)}) collective-permute-start(f32[128,512]{1,0:T(8,128)S(1)} %get-tuple-element.80.refs_0_), channel_id=1, source_target_pairs={{0,8},{8,16},{16,24},{24,0},{32,40},{40,48},{48,56},{56,32},{64,72... | collective-permute-start | bytes 786440 | tf_op jit(solution)/shard_map/ppermute | solution.py:366
  166.2 9.4 %collective-permute-start.41 = (f32[128,512]{1,0:T(8,128)S(1)}, f32[128,512]{1,0:T(8,128)S(1)}, u32[]{:S(2)}, u32[]{:S(2)}) collective-permute-start(f32[128,512]{1,0:T(8,128)S(1)} %get-tuple-element.80.refs_0_), channel_id=1, source_target_pairs={{0,16},{8,24},{16,0},{24,8},{32,48},{40,56},{48,32},{56,40},{64,80... | collective-permute-start | bytes 786440 | tf_op jit(solution)/shard_map/ppermute | solution.py:366
  166.2 9.4 %collective-permute-start.42 = (f32[128,512]{1,0:T(8,128)S(1)}, f32[128,512]{1,0:T(8,128)S(1)}, u32[]{:S(2)}, u32[]{:S(2)}) collective-permute-start(f32[128,512]{1,0:T(8,128)S(1)} %get-tuple-element.81.refs_4_), channel_id=1, source_target_pairs={{0,96},{8,104},{16,112},{24,120},{32,0},{40,8},{48,16},{56,24},{64... | collective-permute-start | bytes 786440 | tf_op jit(solution)/shard_map/ppermute | solution.py:366
  166.8 9.6 %collective-permute-start.43 = (f32[128,512]{1,0:T(8,128)S(1)}, f32[128,512]{1,0:T(8,128)S(1)}, u32[]{:S(2)}, u32[]{:S(2)}) collective-permute-start(f32[128,512]{1,0:T(8,128)S(1)} %get-tuple-element.81.refs_4_), channel_id=1, source_target_pairs={{0,32},{8,40},{16,48},{24,56},{32,64},{40,72},{48,80},{56,88},{64,... | collective-permute-start | bytes 786440 | tf_op jit(solution)/shard_map/ppermute | solution.py:366
  175.6 7.9 %collective-permute-start.44 = (f32[128,512]{1,0:T(8,128)S(1)}, f32[128,512]{1,0:T(8,128)S(1)}, u32[]{:S(2)}, u32[]{:S(2)}) collective-permute-start(f32[128,512]{1,0:T(8,128)S(1)} %get-tuple-element.81.refs_4_), channel_id=1, source_target_pairs={{0,64},{8,72},{16,80},{24,88},{32,96},{40,104},{48,112},{56,120},{... | collective-permute-start | bytes 786440 | tf_op jit(solution)/shard_map/ppermute | solution.py:366
  (29 other events, 133.3 us)

commit v6 on v5

--- a/solution.py
+++ b/solution.py
@@ -445,7 +445,7 @@
     flipped = flip(after(spectra, slices[0]))
     slices = deal(slices, "col", X)
     part = add([after(slices[0], *flipped)] + slices[1:])
-    late = after(w, part)
+    late = after(w, *flipped)
     near_p, near_m, far = send(late, "col", X, 3), send(late, "col", X, 1), send(late, "col", X, 2)
     carry = back(flipped, (w, after(ws, part)), ((0, False), (0, True)))
     part = add([after(part, carry[0])] + fetch(part, "samp", Y))

time: 186 us -> 186 us (level); the launches traced: 185 us -> 182 us
  waiting for transfers between devices: 80 us -> 72.9 us
  starting transfers between devices: 63.2 us -> 67.6 us
    ppermute x30, starting transfers between devices: 41.6 us -> 44.7 us  [fetch(): return [lax.ppermute(a, axis, table[(4 - r) % 4]) for r in REL[1:]]]
    ppermute x30, waiting for transfers between devices: 45.9 us -> 43 us  [fetch(): return [lax.ppermute(a, axis, table[(4 - r) % 4]) for r in REL[1:]]]
    ppermute x6, waiting for transfers between devices: 6.01 us -> 3.14 us  [send(): return lax.ppermute(a, axis, table[r])]
  transfers between devices with their start and end apart: 47 -> 47, of which waited for: 26 -> 24; matrix products, arithmetic and copies ran while one was open for 0% -> 0% of each run, Pallas kernels for 10% -> 10%
where the time goes in v6:
time: 186 us; the launch traced here: 182 us
  waiting for transfers between devices  72.9 us (39%)
  starting transfers between devices  67.6 us (36%)
  Pallas kernels  33.4 us (18%)
  local copies, waits for them, and re-layouts  7.48 us (4%)
    ppermute x30, starting transfers between devices, fetch(): return [lax.ppermute(a, axis, table[(4 - r) % 4]) for r in REL[1:]]  44.7 us
    ppermute x30, waiting for transfers between devices, fetch(): return [lax.ppermute(a, axis, table[(4 - r) % 4]) for r in REL[1:]]  43 us
    all_to_all x1, waiting for transfers between devices, shards(): product = lax.all_to_all(back_sum, 'samp', 0, 0, tiled=True)  15 us
    pallas_call x4, Pallas kernels, back(): pl.pallas_call(functools.partial(back_kernel, tuple(chunks), bool(carry))...  9.06 us
    ppermute x6, starting transfers between devices, send(): return lax.ppermute(a, axis, table[r])  8.9 us
    all_to_all x1, starting transfers between devices, shards(): product = lax.all_to_all(back_sum, 'samp', 0, 0, tiled=True)  8.17 us
    pallas_call x4, Pallas kernels, prod(): pl.pallas_call(functools.partial(prod_kernel, chunks, sibling, first, rec...  8.14 us
    unnamed x12, local copies, waits for them, and re-layouts  7.48 us
  transfers between devices with their start and end apart: 47, of which 24 were waited for; matrix products, arithmetic and copies ran while one was open for 0% of the time, Pallas kernels for 10%

profile of v6, /device:TPU:24, one launch (start us, length us, event | category | flops | bytes accessed | tf_op | source)
XLA Modules:
  0.0 182.3 jit_solution(427426913346380238)
XLA Ops:
  0.6 3.4 %copy-done = f32[2048,1024]{1,0:T(8,128)S(1)} copy-done((f32[2048,1024]{1,0:T(8,128)S(1)}, f32[2048,1024]{1,0:T(8,128)}, u32[]{:S(2)}) %copy-start) | copy-done | bytes 8388632
  8.2 2.8 %collective-permute-start.1 = (f32[16,512]{1,0:T(8,128)S(1)}, f32[16,512]{1,0:T(8,128)S(1)}, u32[]{:S(2)}, u32[]{:S(2)}) collective-permute-start(f32[16,512]{1,0:T(8,128)S(1)} %add.5.refs_0_), channel_id=1, source_target_pairs={{0,6},{1,7},{2,0},{3,1},{4,2},{5,3},{6,4},{7,5},{8,14},{9,15},{10,... | collective-permute-start | bytes 98312 | tf_op jit(solution)/shard_map/ppermute | solution.py:366
  21.0 2.8 %prod.7 = f32[1024,512]{1,0:T(8,128)} custom-call(f32[2048,1024]{1,0:T(8,128)S(1)} %copy-done, bf16[1024,512]{1,0:T(8,128)(2,1)S(1)} %get-tuple-element.48.refs_1_, bf16[1024,512]{1,0:T(8,128)(2,1)S(1)} %get-tuple-element.49.refs_2_, f32[512,512]{1,0:T(8,128)S(1)} %collective-permute-done.4.refs_3_, f32[512,512]{1,0:T(8,128)S(1)} %prod.6.refs_4_), custom_call_target="tpu_custom_call" | custom-call | flops 1610612736 | bytes 6291456 | tf_op jit(solution)/shard_map/prod/pallas_call | solution.py:89
  23.7 4.5 %all-to-all-start = ((f32[4,256,512]{2,1,0:T(8,128)}), f32[4,256,512]{2,1,0:T(8,128)S(1)}, u32[]{:S(2)}, u32[]{:S(2)}) async-start(f32[4,256,512]{2,1,0:T(8,128)} %bitcast), calls=%async_computation | async-start | bytes 4194304 | tf_op jit(solution)/shard_map/all_to_all | solution.py:437
  28.2 4.0 %collective-permute-start.6 = (f32[16,512]{1,0:T(8,128)S(1)}, f32[16,512]{1,0:T(8,128)S(1)}, u32[]{:S(2)}, u32[]{:S(2)}) collective-permute-start(f32[16,512]{1,0:T(8,128)S(1)} %add.6.refs_0_), channel_id=1, source_target_pairs={{0,96},{8,104},{16,112},{24,120},{32,0},{40,8},{48,16},{56,24},{64... | collective-permute-start | bytes 98312 | tf_op jit(solution)/shard_map/ppermute | solution.py:366
  34.1 3.3 %collective-permute-done.7.refs_2_ = f32[16,512]{1,0:T(8,128)S(1)} collective-permute-done((f32[16,512]{1,0:T(8,128)S(1)}, f32[16,512]{1,0:T(8,128)S(1)}, u32[]{:S(2)}, u32[]{:S(2)}) %collective-permute-start.7) | collective-permute-done | bytes 32800 | tf_op jit(solution)/shard_map/ppermute | solution.py:366
  49.0 5.8 %all-to-all-done = f32[4,256,512]{2,1,0:T(8,128)S(1)} async-done(((f32[4,256,512]{2,1,0:T(8,128)}), f32[4,256,512]{2,1,0:T(8,128)S(1)}, u32[]{:S(2)}, u32[]{:S(2)}) %all-to-all-start) | async-done | bytes 2097184 | tf_op jit(solution)/shard_map/all_to_all | solution.py:437
  56.0 4.1 %sweep.2.w_ref.refs_2_ = f32[256,512]{1,0:T(8,128)S(1)} custom-call(f32[1024,512]{1,0:T(8,128)S(1)} %bitcast.7, f32[256,512]{1,0:T(8,128)S(1)} %copy-done.3, f32[256,512]{1,0:T(8,128)S(1)} %join.5.mine, f32[256,512]{1,0:T(8,128)S(1)} %collective-permute-done.12.theirs), custom_call_target="tpu_custom_call" | custom-call | flops 4831838208 | bytes 4194304 | tf_op jit(solution)/shard_map/sweep/pallas_call | solution.py:271
  66.3 3.4 %flip.1 = (bf16[16,1024,128]{2,1,0:T(8,128)(2,1)S(1)}, bf16[16,1024,128]{2,1,0:T(8,128)(2,1)S(1)}) custom-call(f32[2048,1024]{1,0:T(8,128)S(1)} %bitcast.5), custom_call_target="tpu_custom_call" | custom-call | flops 16777216 | bytes 16777216 | tf_op jit(solution)/shard_map/flip/pallas_call | solution.py:111
  82.6 3.2 %collective-permute-done.20.refs_3_ = f32[64,512]{1,0:T(8,128)S(1)} collective-permute-done((f32[64,512]{1,0:T(8,128)S(1)}, f32[64,512]{1,0:T(8,128)S(1)}, u32[]{:S(2)}, u32[]{:S(2)}) %collective-permute-start.20) | collective-permute-done | bytes 131104 | tf_op jit(solution)/shard_map/ppermute | solution.py:366
  85.8 4.1 %collective-permute-start.23 = (f32[64,512]{1,0:T(8,128)S(1)}, f32[64,512]{1,0:T(8,128)S(1)}, u32[]{:S(2)}, u32[]{:S(2)}) collective-permute-start(f32[64,512]{1,0:T(8,128)S(1)} %add.8.refs_0_), channel_id=1, source_target_pairs={{0,96},{8,104},{16,112},{24,120},{32,0},{40,8},{48,16},{56,24},{64... | collective-permute-start | bytes 393224 | tf_op jit(solution)/shard_map/ppermute | solution.py:366
  91.8 3.1 %collective-permute-done.21.refs_2_ = f32[256,512]{1,0:T(8,128)S(1)} collective-permute-done((f32[256,512]{1,0:T(8,128)S(1)}, f32[256,512]{1,0:T(8,128)S(1)}, u32[]{:S(2)}, u32[]{:S(2)}) %collective-permute-start.21) | collective-permute-done | bytes 524320 | tf_op jit(solution)/shard_map/ppermute | solution.py:362
  103.9 8.2 %all-to-all-start.1 = ((f32[16,64,512]{2,1,0:T(8,128)}), f32[16,64,512]{2,1,0:T(8,128)S(1)}, u32[]{:S(2)}, u32[]{:S(2)}) async-start(f32[16,64,512]{2,1,0:T(8,128)} %bitcast.8), calls=%async_computation.1 | async-start | bytes 4194304 | tf_op jit(solution)/shard_map/all_to_all | solution.py:461
  112.1 3.7 %collective-permute-start.29 = (f32[64,512]{1,0:T(8,128)S(1)}, f32[64,512]{1,0:T(8,128)S(1)}, u32[]{:S(2)}, u32[]{:S(2)}) collective-permute-start(f32[64,512]{1,0:T(8,128)S(1)} %add.9.refs_0_), channel_id=1, source_target_pairs={{0,6},{1,7},{2,0},{3,1},{4,2},{5,3},{6,4},{7,5},{8,14},{9,15},{10,... | collective-permute-start | bytes 393224 | tf_op jit(solution)/shard_map/ppermute | solution.py:366
  115.9 4.5 %collective-permute-start.31 = (f32[64,512]{1,0:T(8,128)S(1)}, f32[64,512]{1,0:T(8,128)S(1)}, u32[]{:S(2)}, u32[]{:S(2)}) collective-permute-start(f32[64,512]{1,0:T(8,128)S(1)} %add.9.refs_0_), channel_id=1, source_target_pairs={{0,4},{1,5},{2,6},{3,7},{4,0},{5,1},{6,2},{7,3},{8,12},{9,13},{10,... | collective-permute-start | bytes 393224 | tf_op jit(solution)/shard_map/ppermute | solution.py:366
  122.4 3.8 %collective-permute-done.31.refs_3_ = f32[64,512]{1,0:T(8,128)S(1)} collective-permute-done((f32[64,512]{1,0:T(8,128)S(1)}, f32[64,512]{1,0:T(8,128)S(1)}, u32[]{:S(2)}, u32[]{:S(2)}) %collective-permute-start.31) | collective-permute-done | bytes 131104 | tf_op jit(solution)/shard_map/ppermute | solution.py:366
  128.2 15.0 %all-to-all-done.1 = f32[16,64,512]{2,1,0:T(8,128)S(1)} async-done(((f32[16,64,512]{2,1,0:T(8,128)}), f32[16,64,512]{2,1,0:T(8,128)S(1)}, u32[]{:S(2)}, u32[]{:S(2)}) %all-to-all-start.1) | async-done | bytes 2097184 | tf_op jit(solution)/shard_map/all_to_all | solution.py:461
  143.2 3.0 %sweep.3 = (f32[32,512]{1,0:T(8,128)S(1)}, f32[32,512]{1,0:T(8,128)S(1)}) custom-call(f32[1024,512]{1,0:T(8,128)S(1)} %bitcast.6, f32[1024,512]{1,0:T(8,128)} %start.1, f32[256,512]{1,0:T(8,128)S(1)} %join.6.mine, f32[256,512]{1,0:T(8,128)S(1)} %collective-permute-done.32.theirs), custom_call_target="tpu_custom_call" | custom-call | flops 1207959552 | bytes 4194304 | tf_op jit(solution)/shard_map/sweep/pallas_call | solution.py:271
  151.0 3.2 %collective-permute-start.37 = (f32[32,512]{1,0:T(8,128)S(1)}, f32[32,512]{1,0:T(8,128)S(1)}, u32[]{:S(2)}, u32[]{:S(2)}) collective-permute-start(f32[32,512]{1,0:T(8,128)S(1)} %get-tuple-element.79.refs_4_), channel_id=1, source_target_pairs={{0,8},{8,16},{16,24},{24,0},{32,40},{40,48},{48,56},{56,32},{64,72... | collective-permute-start | bytes 196616 | tf_op jit(solution)/shard_map/ppermute | solution.py:366
  154.3 2.9 %collective-permute-done.36.refs_5_ = f32[32,512]{1,0:T(8,128)S(1)} collective-permute-done((f32[32,512]{1,0:T(8,128)S(1)}, f32[32,512]{1,0:T(8,128)S(1)}, u32[]{:S(2)}, u32[]{:S(2)}) %collective-permute-start.36) | collective-permute-done | bytes 65568 | tf_op jit(solution)/shard_map/ppermute | solution.py:366
  157.2 3.0 %collective-permute-done.38.refs_7_ = f32[32,512]{1,0:T(8,128)S(1)} collective-permute-done((f32[32,512]{1,0:T(8,128)S(1)}, f32[32,512]{1,0:T(8,128)S(1)}, u32[]{:S(2)}, u32[]{:S(2)}) %collective-permute-start.38) | collective-permute-done | bytes 65568 | tf_op jit(solution)/shard_map/ppermute | solution.py:366
  160.3 3.2 %collective-permute-start.40 = (f32[128,512]{1,0:T(8,128)S(1)}, f32[128,512]{1,0:T(8,128)S(1)}, u32[]{:S(2)}, u32[]{:S(2)}) collective-permute-start(f32[128,512]{1,0:T(8,128)S(1)} %get-tuple-element.80.refs_0_), channel_id=1, source_target_pairs={{0,8},{8,16},{16,24},{24,0},{32,40},{40,48},{48,56},{56,32},{64,72... | collective-permute-start | bytes 786440 | tf_op jit(solution)/shard_map/ppermute | solution.py:366
  165.6 7.3 %collective-permute-done.39.refs_1_ = f32[128,512]{1,0:T(8,128)S(1)} collective-permute-done((f32[128,512]{1,0:T(8,128)S(1)}, f32[128,512]{1,0:T(8,128)S(1)}, u32[]{:S(2)}, u32[]{:S(2)}) %collective-permute-start.39) | collective-permute-done | bytes 262176 | tf_op jit(solution)/shard_map/ppermute | solution.py:366
  173.7 7.1 %collective-permute-done.44.refs_7_ = f32[128,512]{1,0:T(8,128)S(1)} collective-permute-done((f32[128,512]{1,0:T(8,128)S(1)}, f32[128,512]{1,0:T(8,128)S(1)}, u32[]{:S(2)}, u32[]{:S(2)}) %collective-permute-start.44) | collective-permute-done | bytes 262176 | tf_op jit(solution)/shard_map/ppermute | solution.py:366
  (107 shorter events, 72.0 us)
Async XLA Ops:
  8.2 6.9 %collective-permute-start.1 = (f32[16,512]{1,0:T(8,128)S(1)}, f32[16,512]{1,0:T(8,128)S(1)}, u32[]{:S(2)}, u32[]{:S(2)}) collective-permute-start(f32[16,512]{1,0:T(8,128)S(1)} %add.5.refs_0_), channel_id=1, source_target_pairs={{0,6},{1,7},{2,0},{3,1},{4,2},{5,3},{6,4},{7,5},{8,14},{9,15},{10,... | collective-permute-start | bytes 98312 | tf_op jit(solution)/shard_map/ppermute | solution.py:366
  23.7 31.1 %all-to-all-start = ((f32[4,256,512]{2,1,0:T(8,128)}), f32[4,256,512]{2,1,0:T(8,128)S(1)}, u32[]{:S(2)}, u32[]{:S(2)}) async-start(f32[4,256,512]{2,1,0:T(8,128)} %bitcast), calls=%async_computation | async-start | bytes 4194304 | tf_op jit(solution)/shard_map/all_to_all | solution.py:437
  38.0 7.2 %collective-permute-start.11 = (f32[64,512]{1,0:T(8,128)S(1)}, f32[64,512]{1,0:T(8,128)S(1)}, u32[]{:S(2)}, u32[]{:S(2)}) collective-permute-start(f32[64,512]{1,0:T(8,128)S(1)} %join.4.refs_0_), channel_id=1, source_target_pairs={{0,16},{8,24},{16,0},{24,8},{32,48},{40,56},{48,32},{56,40},{64,80... | collective-permute-start | bytes 393224 | tf_op jit(solution)/shard_map/ppermute | solution.py:366
  63.0 10.0 %collective-permute-start.15 = (f32[64,512]{1,0:T(8,128)S(1)}, f32[64,512]{1,0:T(8,128)S(1)}, u32[]{:S(2)}, u32[]{:S(2)}) collective-permute-start(f32[64,512]{1,0:T(8,128)S(1)} %get-tuple-element.59), channel_id=1, source_target_pairs={{0,2},{1,3},{2,4},{3,5},{4,6},{5,7},{6,0},{7,1},{8,10},{9,11},{10,... | collective-permute-start | bytes 393224 | tf_op jit(solution)/shard_map/ppermute | solution.py:362
  63.6 9.4 %collective-permute-start.16 = (f32[64,512]{1,0:T(8,128)S(1)}, f32[64,512]{1,0:T(8,128)S(1)}, u32[]{:S(2)}, u32[]{:S(2)}) collective-permute-start(f32[64,512]{1,0:T(8,128)S(1)} %get-tuple-element.60), channel_id=1, source_target_pairs={{0,6},{1,7},{2,0},{3,1},{4,2},{5,3},{6,4},{7,5},{8,14},{9,15},{10,... | collective-permute-start | bytes 393224 | tf_op jit(solution)/shard_map/ppermute | solution.py:362
  66.3 6.7 %collective-permute-start.17 = (f32[64,512]{1,0:T(8,128)S(1)}, f32[64,512]{1,0:T(8,128)S(1)}, u32[]{:S(2)}, u32[]{:S(2)}) collective-permute-start(f32[64,512]{1,0:T(8,128)S(1)} %get-tuple-element.61), channel_id=1, source_target_pairs={{0,4},{1,5},{2,6},{3,7},{4,0},{5,1},{6,2},{7,3},{8,12},{9,13},{10,... | collective-permute-start | bytes 393224 | tf_op jit(solution)/shard_map/ppermute | solution.py:362
  69.7 20.2 %collective-permute-start.22 = (f32[256,512]{1,0:T(8,128)S(1)}, f32[256,512]{1,0:T(8,128)S(1)}, u32[]{:S(2)}, u32[]{:S(2)}) collective-permute-start(f32[256,512]{1,0:T(8,128)S(1)} %sweep.2.w_ref.refs_2_), channel_id=1, source_target_pairs={{0,2},{1,3},{2,4},{3,5},{4,6},{5,7},{6,0},{7,1},{8,10},{9,11},{10,... | collective-permute-start | bytes 1572872 | tf_op jit(solution)/shard_map/ppermute | solution.py:362
  70.6 24.3 %collective-permute-start.21 = (f32[256,512]{1,0:T(8,128)S(1)}, f32[256,512]{1,0:T(8,128)S(1)}, u32[]{:S(2)}, u32[]{:S(2)}) collective-permute-start(f32[256,512]{1,0:T(8,128)S(1)} %sweep.2.w_ref.refs_2_), channel_id=1, source_target_pairs={{0,6},{1,7},{2,0},{3,1},{4,2},{5,3},{6,4},{7,5},{8,14},{9,15},{10,... | collective-permute-start | bytes 1572872 | tf_op jit(solution)/shard_map/ppermute | solution.py:362
  73.9 24.0 %collective-permute-start.14 = (f32[256,512]{1,0:T(8,128)S(1)}, f32[256,512]{1,0:T(8,128)S(1)}, u32[]{:S(2)}, u32[]{:S(2)}) collective-permute-start(f32[256,512]{1,0:T(8,128)S(1)} %sweep.2.w_ref.refs_2_), channel_id=1, source_target_pairs={{0,4},{1,5},{2,6},{3,7},{4,0},{5,1},{6,2},{7,3},{8,12},{9,13},{10,... | collective-permute-start | bytes 1572872 | tf_op jit(solution)/shard_map/ppermute | solution.py:362
  85.8 9.1 %collective-permute-start.23 = (f32[64,512]{1,0:T(8,128)S(1)}, f32[64,512]{1,0:T(8,128)S(1)}, u32[]{:S(2)}, u32[]{:S(2)}) collective-permute-start(f32[64,512]{1,0:T(8,128)S(1)} %add.8.refs_0_), channel_id=1, source_target_pairs={{0,96},{8,104},{16,112},{24,120},{32,0},{40,8},{48,16},{56,24},{64... | collective-permute-start | bytes 393224 | tf_op jit(solution)/shard_map/ppermute | solution.py:366
  89.9 7.9 %collective-permute-start.24 = (f32[64,512]{1,0:T(8,128)S(1)}, f32[64,512]{1,0:T(8,128)S(1)}, u32[]{:S(2)}, u32[]{:S(2)}) collective-permute-start(f32[64,512]{1,0:T(8,128)S(1)} %add.8.refs_0_), channel_id=1, source_target_pairs={{0,32},{8,40},{16,48},{24,56},{32,64},{40,72},{48,80},{56,88},{64,... | collective-permute-start | bytes 393224 | tf_op jit(solution)/shard_map/ppermute | solution.py:366
  89.9 7.9 %collective-permute-start.25 = (f32[64,512]{1,0:T(8,128)S(1)}, f32[64,512]{1,0:T(8,128)S(1)}, u32[]{:S(2)}, u32[]{:S(2)}) collective-permute-start(f32[64,512]{1,0:T(8,128)S(1)} %add.8.refs_0_), channel_id=1, source_target_pairs={{0,64},{8,72},{16,80},{24,88},{32,96},{40,104},{48,112},{56,120},{... | collective-permute-start | bytes 393224 | tf_op jit(solution)/shard_map/ppermute | solution.py:366
  103.9 39.3 %all-to-all-start.1 = ((f32[16,64,512]{2,1,0:T(8,128)}), f32[16,64,512]{2,1,0:T(8,128)S(1)}, u32[]{:S(2)}, u32[]{:S(2)}) async-start(f32[16,64,512]{2,1,0:T(8,128)} %bitcast.8), calls=%async_computation.1 | async-start | bytes 4194304 | tf_op jit(solution)/shard_map/all_to_all | solution.py:461
  112.1 8.3 %collective-permute-start.29 = (f32[64,512]{1,0:T(8,128)S(1)}, f32[64,512]{1,0:T(8,128)S(1)}, u32[]{:S(2)}, u32[]{:S(2)}) collective-permute-start(f32[64,512]{1,0:T(8,128)S(1)} %add.9.refs_0_), channel_id=1, source_target_pairs={{0,6},{1,7},{2,0},{3,1},{4,2},{5,3},{6,4},{7,5},{8,14},{9,15},{10,... | collective-permute-start | bytes 393224 | tf_op jit(solution)/shard_map/ppermute | solution.py:366
  115.7 6.6 %collective-permute-start.30 = (f32[64,512]{1,0:T(8,128)S(1)}, f32[64,512]{1,0:T(8,128)S(1)}, u32[]{:S(2)}, u32[]{:S(2)}) collective-permute-start(f32[64,512]{1,0:T(8,128)S(1)} %add.9.refs_0_), channel_id=1, source_target_pairs={{0,2},{1,3},{2,4},{3,5},{4,6},{5,7},{6,0},{7,1},{8,10},{9,11},{10,... | collective-permute-start | bytes 393224 | tf_op jit(solution)/shard_map/ppermute | solution.py:366
  115.9 10.3 %collective-permute-start.31 = (f32[64,512]{1,0:T(8,128)S(1)}, f32[64,512]{1,0:T(8,128)S(1)}, u32[]{:S(2)}, u32[]{:S(2)}) collective-permute-start(f32[64,512]{1,0:T(8,128)S(1)} %add.9.refs_0_), channel_id=1, source_target_pairs={{0,4},{1,5},{2,6},{3,7},{4,0},{5,1},{6,2},{7,3},{8,12},{9,13},{10,... | collective-permute-start | bytes 393224 | tf_op jit(solution)/shard_map/ppermute | solution.py:366
  146.3 8.0 %collective-permute-start.33 = (f32[32,512]{1,0:T(8,128)S(1)}, f32[32,512]{1,0:T(8,128)S(1)}, u32[]{:S(2)}, u32[]{:S(2)}) collective-permute-start(f32[32,512]{1,0:T(8,128)S(1)} %get-tuple-element.78.refs_0_), channel_id=1, source_target_pairs={{0,96},{8,104},{16,112},{24,120},{32,0},{40,8},{48,16},{56,24},{64... | collective-permute-start | bytes 196616 | tf_op jit(solution)/shard_map/ppermute | solution.py:366
  147.3 7.0 %collective-permute-start.34 = (f32[32,512]{1,0:T(8,128)S(1)}, f32[32,512]{1,0:T(8,128)S(1)}, u32[]{:S(2)}, u32[]{:S(2)}) collective-permute-start(f32[32,512]{1,0:T(8,128)S(1)} %get-tuple-element.78.refs_0_), channel_id=1, source_target_pairs={{0,32},{8,40},{16,48},{24,56},{32,64},{40,72},{48,80},{56,88},{64,... | collective-permute-start | bytes 196616 | tf_op jit(solution)/shard_map/ppermute | solution.py:366
  160.2 12.7 %collective-permute-start.39 = (f32[128,512]{1,0:T(8,128)S(1)}, f32[128,512]{1,0:T(8,128)S(1)}, u32[]{:S(2)}, u32[]{:S(2)}) collective-permute-start(f32[128,512]{1,0:T(8,128)S(1)} %get-tuple-element.80.refs_0_), channel_id=1, source_target_pairs={{0,24},{8,0},{16,8},{24,16},{32,56},{40,32},{48,40},{56,48},{64,88... | collective-permute-start | bytes 786440 | tf_op jit(solution)/shard_map/ppermute | solution.py:366
  160.3 12.6 %collective-permute-start.40 = (f32[128,512]{1,0:T(8,128)S(1)}, f32[128,512]{1,0:T(8,128)S(1)}, u32[]{:S(2)}, u32[]{:S(2)}) collective-permute-start(f32[128,512]{1,0:T(8,128)S(1)} %get-tuple-element.80.refs_0_), channel_id=1, source_target_pairs={{0,8},{8,16},{16,24},{24,0},{32,40},{40,48},{48,56},{56,32},{64,72... | collective-permute-start | bytes 786440 | tf_op jit(solution)/shard_map/ppermute | solution.py:366
  163.6 9.4 %collective-permute-start.41 = (f32[128,512]{1,0:T(8,128)S(1)}, f32[128,512]{1,0:T(8,128)S(1)}, u32[]{:S(2)}, u32[]{:S(2)}) collective-permute-start(f32[128,512]{1,0:T(8,128)S(1)} %get-tuple-element.80.refs_0_), channel_id=1, source_target_pairs={{0,16},{8,24},{16,0},{24,8},{32,48},{40,56},{48,32},{56,40},{64,80... | collective-permute-start | bytes 786440 | tf_op jit(solution)/shard_map/ppermute | solution.py:366
  163.6 9.4 %collective-permute-start.42 = (f32[128,512]{1,0:T(8,128)S(1)}, f32[128,512]{1,0:T(8,128)S(1)}, u32[]{:S(2)}, u32[]{:S(2)}) collective-permute-start(f32[128,512]{1,0:T(8,128)S(1)} %get-tuple-element.81.refs_4_), channel_id=1, source_target_pairs={{0,96},{8,104},{16,112},{24,120},{32,0},{40,8},{48,16},{56,24},{64... | collective-permute-start | bytes 786440 | tf_op jit(solution)/shard_map/ppermute | solution.py:366
  164.1 9.6 %collective-permute-start.43 = (f32[128,512]{1,0:T(8,128)S(1)}, f32[128,512]{1,0:T(8,128)S(1)}, u32[]{:S(2)}, u32[]{:S(2)}) collective-permute-start(f32[128,512]{1,0:T(8,128)S(1)} %get-tuple-element.81.refs_4_), channel_id=1, source_target_pairs={{0,32},{8,40},{16,48},{24,56},{32,64},{40,72},{48,80},{56,88},{64,... | collective-permute-start | bytes 786440 | tf_op jit(solution)/shard_map/ppermute | solution.py:366
  172.9 7.9 %collective-permute-start.44 = (f32[128,512]{1,0:T(8,128)S(1)}, f32[128,512]{1,0:T(8,128)S(1)}, u32[]{:S(2)}, u32[]{:S(2)}) collective-permute-start(f32[128,512]{1,0:T(8,128)S(1)} %get-tuple-element.81.refs_4_), channel_id=1, source_target_pairs={{0,64},{8,72},{16,80},{24,88},{32,96},{40,104},{48,112},{56,120},{... | collective-permute-start | bytes 786440 | tf_op jit(solution)/shard_map/ppermute | solution.py:366
  (29 other events, 133.4 us)

commit v7 on v6

--- a/solution.py
+++ b/solution.py
@@ -223,10 +223,8 @@
     outs, (g, gh, gl, fh, fl, ff, pp, sem) = refs[:-8], refs[-8:]
     z, y, x, c = place()
     n = ff.shape[0]
-    if axis == "col":
-        rows = start
-    else:
-        rows = start.at[pl.ds(pl.multiple_of(n * (4 * z + y), n), n), :]
+    first = n * (2 * x + c if axis == "col" else 4 * z + y)
+    rows = start.at[pl.ds(pl.multiple_of(first, n), n), :]
     begin = pltpu.make_async_copy(rows, ff, sem)
     begin.start()
     for t, piece in enumerate((mine, theirs)):
@@ -271,7 +269,7 @@
     return pl.pallas_call(
         functools.partial(sweep_kernel, axis),
         out_shape=[sds(rows // nout, 512)] * nout,
-        in_specs=[VM, VM if axis == "col" else HBM, VM, VM],
+        in_specs=[VM, HBM, VM, VM],
         out_specs=[VM] * nout,
         scratch_shapes=[
             pltpu.VMEM((512, 512), f32),
@@ -283,31 +281,10 @@
             pltpu.VMEM((rows, 512), f32),
             pltpu.SemaphoreType.DMA,
         ],
-        compiler_params=params(12 if axis == "col" else 50),
+        compiler_params=params(50),
         cost_estimate=cost(72 * rows * 512 * 512, 4 << 20),
         name="sweep",
     )(product, start, *pieces)
-
-
-def take_kernel(w_ref, out_ref, sem):
-    _, _, x, c = place()
-    rows = w_ref.at[pl.ds(pl.multiple_of(256 * (2 * x + c), 256), 256), :]
-    cp = pltpu.make_async_copy(rows, out_ref, sem)
-    cp.start()
-    cp.wait()
-
-
-def take(w_start):
-    return pl.pallas_call(
-        take_kernel,
-        out_shape=sds(256, 512),
-        in_specs=[HBM],
-        out_specs=VM,
-        scratch_shapes=[pltpu.SemaphoreType.DMA],
-        compiler_params=params(57),
-        cost_estimate=cost(0, 1 << 20),
-        name="take",
-    )(w_start)
 
 
 def lay_h_kernel(*refs):
@@ -437,8 +414,7 @@
     product = lax.all_to_all(both, "col", 0, 0, axis_index_groups=XGROUPS, tiled=True)
 
     part = spread(after(strip, both))
-    w0 = take(after(w_start, part))
-    (w,) = sweep(product, w0, "col", 256, (part, swap(part)), 1)
+    (w,) = sweep(product, w_start, "col", 256, (part, swap(part)), 1)
 
     ws = swap(w)
     slices = gram_w(w, ws)

time: 186 us -> 186 us (level)
    ppermute x9, waiting for transfers between devices: 5.87 us -> 7.74 us  [swap(): return lax.ppermute(a, 'col', CORE[0])]
    unnamed x12 -> x10, local copies, waits for them, and re-layouts: 7.48 us -> 6.29 us
  transfers between devices with their start and end apart: 47 -> 47, of which waited for: 24 -> 25; matrix products, arithmetic and copies ran while one was open for 0% -> 0% of each run, Pallas kernels for 10% -> 9%
where the time goes in v7:
time: 186 us; the launch traced here: 182 us
  waiting for transfers between devices  74.7 us (40%)
  starting transfers between devices  67.8 us (36%)
  Pallas kernels  32.3 us (17%)
  local copies, waits for them, and re-layouts  6.29 us (3%)
    ppermute x30, starting transfers between devices, fetch(): return [lax.ppermute(a, axis, table[(4 - r) % 4]) for r in REL[1:]]  44.7 us
    ppermute x30, waiting for transfers between devices, fetch(): return [lax.ppermute(a, axis, table[(4 - r) % 4]) for r in REL[1:]]  42.9 us
    all_to_all x1, waiting for transfers between devices, shards(): product = lax.all_to_all(back_sum, 'samp', 0, 0, tiled=True)  15 us
    pallas_call x4, Pallas kernels, back(): pl.pallas_call(functools.partial(back_kernel, tuple(chunks), bool(carry))...  9.06 us
    ppermute x6, starting transfers between devices, send(): return lax.ppermute(a, axis, table[r])  8.9 us
    all_to_all x1, starting transfers between devices, shards(): product = lax.all_to_all(back_sum, 'samp', 0, 0, tiled=True)  8.18 us
    pallas_call x4, Pallas kernels, prod(): pl.pallas_call(functools.partial(prod_kernel, chunks, sibling, first, rec...  8.14 us
    pallas_call x2, Pallas kernels, sweep(): pl.pallas_call(functools.partial(sweep_kernel, axis), out_shape=[sds(rows...  7.8 us
  transfers between devices with their start and end apart: 47, of which 25 were waited for; matrix products, arithmetic and copies ran while one was open for 0% of the time, Pallas kernels for 9%

profile of v7, /device:TPU:24, one launch (start us, length us, event | category | flops | bytes accessed | tf_op | source)
XLA Modules:
  0.0 182.0 jit_solution(12613139060883643684)
XLA Ops:
  0.6 3.4 %copy-done = f32[2048,1024]{1,0:T(8,128)S(1)} copy-done((f32[2048,1024]{1,0:T(8,128)S(1)}, f32[2048,1024]{1,0:T(8,128)}, u32[]{:S(2)}) %copy-start) | copy-done | bytes 8388632
  8.2 2.8 %collective-permute-start.1 = (f32[16,512]{1,0:T(8,128)S(1)}, f32[16,512]{1,0:T(8,128)S(1)}, u32[]{:S(2)}, u32[]{:S(2)}) collective-permute-start(f32[16,512]{1,0:T(8,128)S(1)} %add.5.refs_0_), channel_id=1, source_target_pairs={{0,6},{1,7},{2,0},{3,1},{4,2},{5,3},{6,4},{7,5},{8,14},{9,15},{10,... | collective-permute-start | bytes 98312 | tf_op jit(solution)/shard_map/ppermute | solution.py:343
  21.0 2.8 %prod.7 = f32[1024,512]{1,0:T(8,128)} custom-call(f32[2048,1024]{1,0:T(8,128)S(1)} %copy-done, bf16[1024,512]{1,0:T(8,128)(2,1)S(1)} %get-tuple-element.47.refs_1_, bf16[1024,512]{1,0:T(8,128)(2,1)S(1)} %get-tuple-element.48.refs_2_, f32[512,512]{1,0:T(8,128)S(1)} %collective-permute-done.4.refs_3_, f32[512,512]{1,0:T(8,128)S(1)} %prod.6.refs_4_), custom_call_target="tpu_custom_call" | custom-call | flops 1610612736 | bytes 6291456 | tf_op jit(solution)/shard_map/prod/pallas_call | solution.py:89
  23.7 4.5 %all-to-all-start = ((f32[4,256,512]{2,1,0:T(8,128)}), f32[4,256,512]{2,1,0:T(8,128)S(1)}, u32[]{:S(2)}, u32[]{:S(2)}) async-start(f32[4,256,512]{2,1,0:T(8,128)} %bitcast), calls=%async_computation | async-start | bytes 4194304 | tf_op jit(solution)/shard_map/all_to_all | solution.py:414
  28.2 4.0 %collective-permute-start.6 = (f32[16,512]{1,0:T(8,128)S(1)}, f32[16,512]{1,0:T(8,128)S(1)}, u32[]{:S(2)}, u32[]{:S(2)}) collective-permute-start(f32[16,512]{1,0:T(8,128)S(1)} %add.6.refs_0_), channel_id=1, source_target_pairs={{0,96},{8,104},{16,112},{24,120},{32,0},{40,8},{48,16},{56,24},{64... | collective-permute-start | bytes 98312 | tf_op jit(solution)/shard_map/ppermute | solution.py:343
  34.1 3.3 %collective-permute-done.7.refs_2_ = f32[16,512]{1,0:T(8,128)S(1)} collective-permute-done((f32[16,512]{1,0:T(8,128)S(1)}, f32[16,512]{1,0:T(8,128)S(1)}, u32[]{:S(2)}, u32[]{:S(2)}) %collective-permute-start.7) | collective-permute-done | bytes 32800 | tf_op jit(solution)/shard_map/ppermute | solution.py:343
  49.0 5.8 %all-to-all-done = f32[4,256,512]{2,1,0:T(8,128)S(1)} async-done(((f32[4,256,512]{2,1,0:T(8,128)}), f32[4,256,512]{2,1,0:T(8,128)S(1)}, u32[]{:S(2)}, u32[]{:S(2)}) %all-to-all-start) | async-done | bytes 2097184 | tf_op jit(solution)/shard_map/all_to_all | solution.py:414
  54.8 4.8 %sweep.2.w_ref.refs_2_ = f32[256,512]{1,0:T(8,128)S(1)} custom-call(f32[1024,512]{1,0:T(8,128)S(1)} %bitcast.7, f32[2048,512]{1,0:T(8,128)} %start.2, f32[256,512]{1,0:T(8,128)S(1)} %join.5.mine, f32[256,512]{1,0:T(8,128)S(1)} %collective-permute-done.12.theirs), custom_call_target="tpu_custom_call" | custom-call | flops 4831838208 | bytes 4194304 | tf_op jit(solution)/shard_map/sweep/pallas_call | solution.py:269
  65.8 3.4 %flip.1 = (bf16[16,1024,128]{2,1,0:T(8,128)(2,1)S(1)}, bf16[16,1024,128]{2,1,0:T(8,128)(2,1)S(1)}) custom-call(f32[2048,1024]{1,0:T(8,128)S(1)} %bitcast.5), custom_call_target="tpu_custom_call" | custom-call | flops 16777216 | bytes 16777216 | tf_op jit(solution)/shard_map/flip/pallas_call | solution.py:111
  82.1 3.2 %collective-permute-done.20.refs_3_ = f32[64,512]{1,0:T(8,128)S(1)} collective-permute-done((f32[64,512]{1,0:T(8,128)S(1)}, f32[64,512]{1,0:T(8,128)S(1)}, u32[]{:S(2)}, u32[]{:S(2)}) %collective-permute-start.20) | collective-permute-done | bytes 131104 | tf_op jit(solution)/shard_map/ppermute | solution.py:343
  85.3 4.1 %collective-permute-start.23 = (f32[64,512]{1,0:T(8,128)S(1)}, f32[64,512]{1,0:T(8,128)S(1)}, u32[]{:S(2)}, u32[]{:S(2)}) collective-permute-start(f32[64,512]{1,0:T(8,128)S(1)} %add.8.refs_0_), channel_id=1, source_target_pairs={{0,96},{8,104},{16,112},{24,120},{32,0},{40,8},{48,16},{56,24},{64... | collective-permute-start | bytes 393224 | tf_op jit(solution)/shard_map/ppermute | solution.py:343
  91.3 3.1 %collective-permute-done.21.refs_2_ = f32[256,512]{1,0:T(8,128)S(1)} collective-permute-done((f32[256,512]{1,0:T(8,128)S(1)}, f32[256,512]{1,0:T(8,128)S(1)}, u32[]{:S(2)}, u32[]{:S(2)}) %collective-permute-start.21) | collective-permute-done | bytes 524320 | tf_op jit(solution)/shard_map/ppermute | solution.py:339
  103.6 8.2 %all-to-all-start.1 = ((f32[16,64,512]{2,1,0:T(8,128)}), f32[16,64,512]{2,1,0:T(8,128)S(1)}, u32[]{:S(2)}, u32[]{:S(2)}) async-start(f32[16,64,512]{2,1,0:T(8,128)} %bitcast.8), calls=%async_computation.1 | async-start | bytes 4194304 | tf_op jit(solution)/shard_map/all_to_all | solution.py:437
  111.8 3.7 %collective-permute-start.29 = (f32[64,512]{1,0:T(8,128)S(1)}, f32[64,512]{1,0:T(8,128)S(1)}, u32[]{:S(2)}, u32[]{:S(2)}) collective-permute-start(f32[64,512]{1,0:T(8,128)S(1)} %add.9.refs_0_), channel_id=1, source_target_pairs={{0,6},{1,7},{2,0},{3,1},{4,2},{5,3},{6,4},{7,5},{8,14},{9,15},{10,... | collective-permute-start | bytes 393224 | tf_op jit(solution)/shard_map/ppermute | solution.py:343
  115.6 4.5 %collective-permute-start.31 = (f32[64,512]{1,0:T(8,128)S(1)}, f32[64,512]{1,0:T(8,128)S(1)}, u32[]{:S(2)}, u32[]{:S(2)}) collective-permute-start(f32[64,512]{1,0:T(8,128)S(1)} %add.9.refs_0_), channel_id=1, source_target_pairs={{0,4},{1,5},{2,6},{3,7},{4,0},{5,1},{6,2},{7,3},{8,12},{9,13},{10,... | collective-permute-start | bytes 393224 | tf_op jit(solution)/shard_map/ppermute | solution.py:343
  122.1 3.8 %collective-permute-done.31.refs_3_ = f32[64,512]{1,0:T(8,128)S(1)} collective-permute-done((f32[64,512]{1,0:T(8,128)S(1)}, f32[64,512]{1,0:T(8,128)S(1)}, u32[]{:S(2)}, u32[]{:S(2)}) %collective-permute-start.31) | collective-permute-done | bytes 131104 | tf_op jit(solution)/shard_map/ppermute | solution.py:343
  127.9 15.0 %all-to-all-done.1 = f32[16,64,512]{2,1,0:T(8,128)S(1)} async-done(((f32[16,64,512]{2,1,0:T(8,128)}), f32[16,64,512]{2,1,0:T(8,128)S(1)}, u32[]{:S(2)}, u32[]{:S(2)}) %all-to-all-start.1) | async-done | bytes 2097184 | tf_op jit(solution)/shard_map/all_to_all | solution.py:437
  143.0 3.0 %sweep.3 = (f32[32,512]{1,0:T(8,128)S(1)}, f32[32,512]{1,0:T(8,128)S(1)}) custom-call(f32[1024,512]{1,0:T(8,128)S(1)} %bitcast.6, f32[1024,512]{1,0:T(8,128)} %start.3, f32[256,512]{1,0:T(8,128)S(1)} %join.6.mine, f32[256,512]{1,0:T(8,128)S(1)} %collective-permute-done.32.theirs), custom_call_target="tpu_custom_call" | custom-call | flops 1207959552 | bytes 4194304 | tf_op jit(solution)/shard_map/sweep/pallas_call | solution.py:269
  150.8 3.2 %collective-permute-start.37 = (f32[32,512]{1,0:T(8,128)S(1)}, f32[32,512]{1,0:T(8,128)S(1)}, u32[]{:S(2)}, u32[]{:S(2)}) collective-permute-start(f32[32,512]{1,0:T(8,128)S(1)} %get-tuple-element.77.refs_4_), channel_id=1, source_target_pairs={{0,8},{8,16},{16,24},{24,0},{32,40},{40,48},{48,56},{56,32},{64,72... | collective-permute-start | bytes 196616 | tf_op jit(solution)/shard_map/ppermute | solution.py:343
  154.0 2.9 %collective-permute-done.36.refs_5_ = f32[32,512]{1,0:T(8,128)S(1)} collective-permute-done((f32[32,512]{1,0:T(8,128)S(1)}, f32[32,512]{1,0:T(8,128)S(1)}, u32[]{:S(2)}, u32[]{:S(2)}) %collective-permute-start.36) | collective-permute-done | bytes 65568 | tf_op jit(solution)/shard_map/ppermute | solution.py:343
  156.9 2.9 %collective-permute-done.38.refs_7_ = f32[32,512]{1,0:T(8,128)S(1)} collective-permute-done((f32[32,512]{1,0:T(8,128)S(1)}, f32[32,512]{1,0:T(8,128)S(1)}, u32[]{:S(2)}, u32[]{:S(2)}) %collective-permute-start.38) | collective-permute-done | bytes 65568 | tf_op jit(solution)/shard_map/ppermute | solution.py:343
  160.0 3.2 %collective-permute-start.40 = (f32[128,512]{1,0:T(8,128)S(1)}, f32[128,512]{1,0:T(8,128)S(1)}, u32[]{:S(2)}, u32[]{:S(2)}) collective-permute-start(f32[128,512]{1,0:T(8,128)S(1)} %get-tuple-element.78.refs_0_), channel_id=1, source_target_pairs={{0,8},{8,16},{16,24},{24,0},{32,40},{40,48},{48,56},{56,32},{64,72... | collective-permute-start | bytes 786440 | tf_op jit(solution)/shard_map/ppermute | solution.py:343
  165.3 7.3 %collective-permute-done.39.refs_1_ = f32[128,512]{1,0:T(8,128)S(1)} collective-permute-done((f32[128,512]{1,0:T(8,128)S(1)}, f32[128,512]{1,0:T(8,128)S(1)}, u32[]{:S(2)}, u32[]{:S(2)}) %collective-permute-start.39) | collective-permute-done | bytes 262176 | tf_op jit(solution)/shard_map/ppermute | solution.py:343
  173.4 7.1 %collective-permute-done.44.refs_7_ = f32[128,512]{1,0:T(8,128)S(1)} collective-permute-done((f32[128,512]{1,0:T(8,128)S(1)}, f32[128,512]{1,0:T(8,128)S(1)}, u32[]{:S(2)}, u32[]{:S(2)}) %collective-permute-start.44) | collective-permute-done | bytes 262176 | tf_op jit(solution)/shard_map/ppermute | solution.py:343
  (104 shorter events, 71.1 us)
Async XLA Ops:
  8.2 6.9 %collective-permute-start.1 = (f32[16,512]{1,0:T(8,128)S(1)}, f32[16,512]{1,0:T(8,128)S(1)}, u32[]{:S(2)}, u32[]{:S(2)}) collective-permute-start(f32[16,512]{1,0:T(8,128)S(1)} %add.5.refs_0_), channel_id=1, source_target_pairs={{0,6},{1,7},{2,0},{3,1},{4,2},{5,3},{6,4},{7,5},{8,14},{9,15},{10,... | collective-permute-start | bytes 98312 | tf_op jit(solution)/shard_map/ppermute | solution.py:343
  23.7 31.1 %all-to-all-start = ((f32[4,256,512]{2,1,0:T(8,128)}), f32[4,256,512]{2,1,0:T(8,128)S(1)}, u32[]{:S(2)}, u32[]{:S(2)}) async-start(f32[4,256,512]{2,1,0:T(8,128)} %bitcast), calls=%async_computation | async-start | bytes 4194304 | tf_op jit(solution)/shard_map/all_to_all | solution.py:414
  38.0 7.2 %collective-permute-start.11 = (f32[64,512]{1,0:T(8,128)S(1)}, f32[64,512]{1,0:T(8,128)S(1)}, u32[]{:S(2)}, u32[]{:S(2)}) collective-permute-start(f32[64,512]{1,0:T(8,128)S(1)} %join.4.refs_0_), channel_id=1, source_target_pairs={{0,16},{8,24},{16,0},{24,8},{32,48},{40,56},{48,32},{56,40},{64,80... | collective-permute-start | bytes 393224 | tf_op jit(solution)/shard_map/ppermute | solution.py:343
  62.5 10.0 %collective-permute-start.15 = (f32[64,512]{1,0:T(8,128)S(1)}, f32[64,512]{1,0:T(8,128)S(1)}, u32[]{:S(2)}, u32[]{:S(2)}) collective-permute-start(f32[64,512]{1,0:T(8,128)S(1)} %get-tuple-element.57), channel_id=1, source_target_pairs={{0,2},{1,3},{2,4},{3,5},{4,6},{5,7},{6,0},{7,1},{8,10},{9,11},{10,... | collective-permute-start | bytes 393224 | tf_op jit(solution)/shard_map/ppermute | solution.py:339
  63.2 9.3 %collective-permute-start.16 = (f32[64,512]{1,0:T(8,128)S(1)}, f32[64,512]{1,0:T(8,128)S(1)}, u32[]{:S(2)}, u32[]{:S(2)}) collective-permute-start(f32[64,512]{1,0:T(8,128)S(1)} %get-tuple-element.58), channel_id=1, source_target_pairs={{0,6},{1,7},{2,0},{3,1},{4,2},{5,3},{6,4},{7,5},{8,14},{9,15},{10,... | collective-permute-start | bytes 393224 | tf_op jit(solution)/shard_map/ppermute | solution.py:339
  65.8 6.7 %collective-permute-start.17 = (f32[64,512]{1,0:T(8,128)S(1)}, f32[64,512]{1,0:T(8,128)S(1)}, u32[]{:S(2)}, u32[]{:S(2)}) collective-permute-start(f32[64,512]{1,0:T(8,128)S(1)} %get-tuple-element.59), channel_id=1, source_target_pairs={{0,4},{1,5},{2,6},{3,7},{4,0},{5,1},{6,2},{7,3},{8,12},{9,13},{10,... | collective-permute-start | bytes 393224 | tf_op jit(solution)/shard_map/ppermute | solution.py:339
  69.2 20.2 %collective-permute-start.22 = (f32[256,512]{1,0:T(8,128)S(1)}, f32[256,512]{1,0:T(8,128)S(1)}, u32[]{:S(2)}, u32[]{:S(2)}) collective-permute-start(f32[256,512]{1,0:T(8,128)S(1)} %sweep.2.w_ref.refs_2_), channel_id=1, source_target_pairs={{0,2},{1,3},{2,4},{3,5},{4,6},{5,7},{6,0},{7,1},{8,10},{9,11},{10,... | collective-permute-start | bytes 1572872 | tf_op jit(solution)/shard_map/ppermute | solution.py:339
  70.1 24.3 %collective-permute-start.21 = (f32[256,512]{1,0:T(8,128)S(1)}, f32[256,512]{1,0:T(8,128)S(1)}, u32[]{:S(2)}, u32[]{:S(2)}) collective-permute-start(f32[256,512]{1,0:T(8,128)S(1)} %sweep.2.w_ref.refs_2_), channel_id=1, source_target_pairs={{0,6},{1,7},{2,0},{3,1},{4,2},{5,3},{6,4},{7,5},{8,14},{9,15},{10,... | collective-permute-start | bytes 1572872 | tf_op jit(solution)/shard_map/ppermute | solution.py:339
  73.4 24.0 %collective-permute-start.14 = (f32[256,512]{1,0:T(8,128)S(1)}, f32[256,512]{1,0:T(8,128)S(1)}, u32[]{:S(2)}, u32[]{:S(2)}) collective-permute-start(f32[256,512]{1,0:T(8,128)S(1)} %sweep.2.w_ref.refs_2_), channel_id=1, source_target_pairs={{0,4},{1,5},{2,6},{3,7},{4,0},{5,1},{6,2},{7,3},{8,12},{9,13},{10,... | collective-permute-start | bytes 1572872 | tf_op jit(solution)/shard_map/ppermute | solution.py:339
  85.3 9.1 %collective-permute-start.23 = (f32[64,512]{1,0:T(8,128)S(1)}, f32[64,512]{1,0:T(8,128)S(1)}, u32[]{:S(2)}, u32[]{:S(2)}) collective-permute-start(f32[64,512]{1,0:T(8,128)S(1)} %add.8.refs_0_), channel_id=1, source_target_pairs={{0,96},{8,104},{16,112},{24,120},{32,0},{40,8},{48,16},{56,24},{64... | collective-permute-start | bytes 393224 | tf_op jit(solution)/shard_map/ppermute | solution.py:343
  89.4 7.9 %collective-permute-start.24 = (f32[64,512]{1,0:T(8,128)S(1)}, f32[64,512]{1,0:T(8,128)S(1)}, u32[]{:S(2)}, u32[]{:S(2)}) collective-permute-start(f32[64,512]{1,0:T(8,128)S(1)} %add.8.refs_0_), channel_id=1, source_target_pairs={{0,32},{8,40},{16,48},{24,56},{32,64},{40,72},{48,80},{56,88},{64,... | collective-permute-start | bytes 393224 | tf_op jit(solution)/shard_map/ppermute | solution.py:343
  89.4 7.9 %collective-permute-start.25 = (f32[64,512]{1,0:T(8,128)S(1)}, f32[64,512]{1,0:T(8,128)S(1)}, u32[]{:S(2)}, u32[]{:S(2)}) collective-permute-start(f32[64,512]{1,0:T(8,128)S(1)} %add.8.refs_0_), channel_id=1, source_target_pairs={{0,64},{8,72},{16,80},{24,88},{32,96},{40,104},{48,112},{56,120},{... | collective-permute-start | bytes 393224 | tf_op jit(solution)/shard_map/ppermute | solution.py:343
  103.6 39.3 %all-to-all-start.1 = ((f32[16,64,512]{2,1,0:T(8,128)}), f32[16,64,512]{2,1,0:T(8,128)S(1)}, u32[]{:S(2)}, u32[]{:S(2)}) async-start(f32[16,64,512]{2,1,0:T(8,128)} %bitcast.8), calls=%async_computation.1 | async-start | bytes 4194304 | tf_op jit(solution)/shard_map/all_to_all | solution.py:437
  111.8 8.3 %collective-permute-start.29 = (f32[64,512]{1,0:T(8,128)S(1)}, f32[64,512]{1,0:T(8,128)S(1)}, u32[]{:S(2)}, u32[]{:S(2)}) collective-permute-start(f32[64,512]{1,0:T(8,128)S(1)} %add.9.refs_0_), channel_id=1, source_target_pairs={{0,6},{1,7},{2,0},{3,1},{4,2},{5,3},{6,4},{7,5},{8,14},{9,15},{10,... | collective-permute-start | bytes 393224 | tf_op jit(solution)/shard_map/ppermute | solution.py:343
  115.5 6.6 %collective-permute-start.30 = (f32[64,512]{1,0:T(8,128)S(1)}, f32[64,512]{1,0:T(8,128)S(1)}, u32[]{:S(2)}, u32[]{:S(2)}) collective-permute-start(f32[64,512]{1,0:T(8,128)S(1)} %add.9.refs_0_), channel_id=1, source_target_pairs={{0,2},{1,3},{2,4},{3,5},{4,6},{5,7},{6,0},{7,1},{8,10},{9,11},{10,... | collective-permute-start | bytes 393224 | tf_op jit(solution)/shard_map/ppermute | solution.py:343
  115.6 10.3 %collective-permute-start.31 = (f32[64,512]{1,0:T(8,128)S(1)}, f32[64,512]{1,0:T(8,128)S(1)}, u32[]{:S(2)}, u32[]{:S(2)}) collective-permute-start(f32[64,512]{1,0:T(8,128)S(1)} %add.9.refs_0_), channel_id=1, source_target_pairs={{0,4},{1,5},{2,6},{3,7},{4,0},{5,1},{6,2},{7,3},{8,12},{9,13},{10,... | collective-permute-start | bytes 393224 | tf_op jit(solution)/shard_map/ppermute | solution.py:343
  146.0 8.0 %collective-permute-start.33 = (f32[32,512]{1,0:T(8,128)S(1)}, f32[32,512]{1,0:T(8,128)S(1)}, u32[]{:S(2)}, u32[]{:S(2)}) collective-permute-start(f32[32,512]{1,0:T(8,128)S(1)} %get-tuple-element.76.refs_0_), channel_id=1, source_target_pairs={{0,96},{8,104},{16,112},{24,120},{32,0},{40,8},{48,16},{56,24},{64... | collective-permute-start | bytes 196616 | tf_op jit(solution)/shard_map/ppermute | solution.py:343
  147.0 7.0 %collective-permute-start.34 = (f32[32,512]{1,0:T(8,128)S(1)}, f32[32,512]{1,0:T(8,128)S(1)}, u32[]{:S(2)}, u32[]{:S(2)}) collective-permute-start(f32[32,512]{1,0:T(8,128)S(1)} %get-tuple-element.76.refs_0_), channel_id=1, source_target_pairs={{0,32},{8,40},{16,48},{24,56},{32,64},{40,72},{48,80},{56,88},{64,... | collective-permute-start | bytes 196616 | tf_op jit(solution)/shard_map/ppermute | solution.py:343
  159.9 12.7 %collective-permute-start.39 = (f32[128,512]{1,0:T(8,128)S(1)}, f32[128,512]{1,0:T(8,128)S(1)}, u32[]{:S(2)}, u32[]{:S(2)}) collective-permute-start(f32[128,512]{1,0:T(8,128)S(1)} %get-tuple-element.78.refs_0_), channel_id=1, source_target_pairs={{0,24},{8,0},{16,8},{24,16},{32,56},{40,32},{48,40},{56,48},{64,88... | collective-permute-start | bytes 786440 | tf_op jit(solution)/shard_map/ppermute | solution.py:343
  160.0 12.6 %collective-permute-start.40 = (f32[128,512]{1,0:T(8,128)S(1)}, f32[128,512]{1,0:T(8,128)S(1)}, u32[]{:S(2)}, u32[]{:S(2)}) collective-permute-start(f32[128,512]{1,0:T(8,128)S(1)} %get-tuple-element.78.refs_0_), channel_id=1, source_target_pairs={{0,8},{8,16},{16,24},{24,0},{32,40},{40,48},{48,56},{56,32},{64,72... | collective-permute-start | bytes 786440 | tf_op jit(solution)/shard_map/ppermute | solution.py:343
  163.2 9.4 %collective-permute-start.41 = (f32[128,512]{1,0:T(8,128)S(1)}, f32[128,512]{1,0:T(8,128)S(1)}, u32[]{:S(2)}, u32[]{:S(2)}) collective-permute-start(f32[128,512]{1,0:T(8,128)S(1)} %get-tuple-element.78.refs_0_), channel_id=1, source_target_pairs={{0,16},{8,24},{16,0},{24,8},{32,48},{40,56},{48,32},{56,40},{64,80... | collective-permute-start | bytes 786440 | tf_op jit(solution)/shard_map/ppermute | solution.py:343
  163.2 9.4 %collective-permute-start.42 = (f32[128,512]{1,0:T(8,128)S(1)}, f32[128,512]{1,0:T(8,128)S(1)}, u32[]{:S(2)}, u32[]{:S(2)}) collective-permute-start(f32[128,512]{1,0:T(8,128)S(1)} %get-tuple-element.79.refs_4_), channel_id=1, source_target_pairs={{0,96},{8,104},{16,112},{24,120},{32,0},{40,8},{48,16},{56,24},{64... | collective-permute-start | bytes 786440 | tf_op jit(solution)/shard_map/ppermute | solution.py:343
  163.8 9.6 %collective-permute-start.43 = (f32[128,512]{1,0:T(8,128)S(1)}, f32[128,512]{1,0:T(8,128)S(1)}, u32[]{:S(2)}, u32[]{:S(2)}) collective-permute-start(f32[128,512]{1,0:T(8,128)S(1)} %get-tuple-element.79.refs_4_), channel_id=1, source_target_pairs={{0,32},{8,40},{16,48},{24,56},{32,64},{40,72},{48,80},{56,88},{64,... | collective-permute-start | bytes 786440 | tf_op jit(solution)/shard_map/ppermute | solution.py:343
  172.6 7.9 %collective-permute-start.44 = (f32[128,512]{1,0:T(8,128)S(1)}, f32[128,512]{1,0:T(8,128)S(1)}, u32[]{:S(2)}, u32[]{:S(2)}) collective-permute-start(f32[128,512]{1,0:T(8,128)S(1)} %get-tuple-element.79.refs_4_), channel_id=1, source_target_pairs={{0,64},{8,72},{16,80},{24,88},{32,96},{40,104},{48,112},{56,120},{... | collective-permute-start | bytes 786440 | tf_op jit(solution)/shard_map/ppermute | solution.py:343
  (28 other events, 133.1 us)
